TPU v7x, 32 devices: a whole 2x2x4 slice. The times are simulated.
32 devices in a mesh: dp: 8 (over z, x), seq: 4 (over y, core).
Axes of the slice: x: 2, y: 2, z: 4, core: 2. Of those that a mesh axis runs over, the one named last changes fastest.
Arguments:
- tokens: bfloat16 [12288, 1024], P(('dp', 'seq')), may hold values from -6 to 6
- lengths: int32 [8], P('dp'), may hold values from 193 to 1536, as said below
- cotangent: bfloat16 [12288, 1024], P(('dp', 'seq')), may hold values from -12 to 12
- ln1_gain: bfloat16 [1024], P(('dp', 'seq')), may hold values from 0.25 to 1.75
- ln1_shift: bfloat16 [1024], P(('dp', 'seq')), may hold values from -1.75 to 1.75
- w_qkv: bfloat16 [1024, 3, 1024], P('dp', None, 'seq'), may hold values from -0.1875 to 0.1875
- b_qv: bfloat16 [2048], P(('dp', 'seq')), may hold values from -1.75 to 1.75
- w_out: bfloat16 [1024, 1024], P('seq', 'dp'), may hold values from -0.5 to 0.5
- b_out: bfloat16 [1024], P(('dp', 'seq')), may hold values from -1.75 to 1.75
- ln2_gain: bfloat16 [1024], P(('dp', 'seq')), may hold values from 0.25 to 1.75
- ln2_shift: bfloat16 [1024], P(('dp', 'seq')), may hold values from -1.75 to 1.75
- w_fc1: bfloat16 [1024, 4096], P('dp', 'seq'), may hold values from -0.1875 to 0.1875
- b_fc1: bfloat16 [4096], P(('dp', 'seq')), may hold values from -3 to 3
- w_fc2: bfloat16 [4096, 1024], P('seq', 'dp'), may hold values from -0.125 to 0.125
- b_fc2: bfloat16 [1024], P(('dp', 'seq')), may hold values from -1.75 to 1.75
Outputs:
- output: bfloat16 [12288, 1024], P(('dp', 'seq'))
- grad_tokens: bfloat16 [12288, 1024], P(('dp', 'seq'))
- grad_ln1_gain: float32 [1024], P(('dp', 'seq'))
- grad_ln1_shift: float32 [1024], P(('dp', 'seq'))
- grad_w_qkv: float32 [1024, 3, 1024], P('dp', None, 'seq')
- grad_b_qv: float32 [2048], P(('dp', 'seq'))
- grad_w_out: float32 [1024, 1024], P('seq', 'dp')
- grad_b_out: float32 [1024], P(('dp', 'seq'))
- grad_ln2_gain: float32 [1024], P(('dp', 'seq'))
- grad_ln2_shift: float32 [1024], P(('dp', 'seq'))
- grad_w_fc1: float32 [1024, 4096], P('dp', 'seq')
- grad_b_fc1: float32 [4096], P(('dp', 'seq'))
- grad_w_fc2: float32 [4096, 1024], P('seq', 'dp')
- grad_b_fc2: float32 [1024], P(('dp', 'seq'))
Inputs may be any that keep to these rules, and one draw needn't show every extreme that they name: `lengths`: some sequence has length 1536 and some has length 193.
All inputs are finite; a program needn't handle non-finite values.
Results may differ from a plain program's by a relative error of at most 0.014.
Values may be sent and summed in bfloat16 or wider, within the bound.
A program may use at most 192 MiB of HBM per device.

v0:
```python
import math

import jax
import jax.numpy as jnp
from jax import lax
from jax.sharding import PartitionSpec as P

HEAD_DIM = 64


eps = 1e-05
gelu_coef = 0.044715


def layer_norm(stream, gain, shift):
    row_mean = jnp.mean(stream, axis=-1, keepdims=True)
    centred = stream - row_mean
    inv_std = lax.rsqrt(jnp.mean(centred * centred, axis=-1, keepdims=True) + eps)
    unit = centred * inv_std
    return (unit * gain + shift, unit, inv_std)


def norm_back(grad_out, gain, unit, inv_std):
    scaled = grad_out * gain
    mean_one = jnp.mean(scaled, axis=-1, keepdims=True)
    mean_two = jnp.mean(scaled * unit, axis=-1, keepdims=True)
    grad_in = inv_std * (scaled - mean_one - unit * mean_two)
    return (grad_in, jnp.sum(grad_out * unit, axis=0), jnp.sum(grad_out, axis=0))


def gelu_parts(pre_act):
    root = math.sqrt(2.0 / math.pi)
    tangent = jnp.tanh(root * (pre_act + gelu_coef * pre_act * pre_act * pre_act))
    value = 0.5 * pre_act * (1.0 + tangent)
    slope = 0.5 * (1.0 + tangent) + 0.5 * pre_act * (1.0 - tangent * tangent) * root * (
        1.0 + 3.0 * gelu_coef * pre_act * pre_act
    )
    return (value, slope)


def split_heads(matrix):
    row_count, width = matrix.shape
    return matrix.reshape(row_count, width // (2 * HEAD_DIM), 2, HEAD_DIM).transpose(1, 2, 0, 3)


def join_heads(blocks):
    groups, pair, row_count, depth = blocks.shape
    return blocks.transpose(2, 0, 1, 3).reshape(row_count, groups * pair * depth)


def on_device(
    tokens,
    lengths,
    cotangent,
    ln1_gain,
    ln1_shift,
    w_qkv,
    b_qv,
    w_out,
    b_out,
    ln2_gain,
    ln2_shift,
    w_fc1,
    b_fc1,
    w_fc2,
    b_fc2,
):
    f32 = jnp.float32
    bf16 = jnp.bfloat16
    row_count, width = tokens.shape
    heads = width // HEAD_DIM
    gain_one, shift_one, bias_qv, bias_out, gain_two, shift_two, bias_up, bias_down = (
        lax.all_gather(ln1_gain, ("dp", "seq"), axis=0, tiled=True),
        lax.all_gather(ln1_shift, ("dp", "seq"), axis=0, tiled=True),
        lax.all_gather(b_qv, ("dp", "seq"), axis=0, tiled=True),
        lax.all_gather(b_out, ("dp", "seq"), axis=0, tiled=True),
        lax.all_gather(ln2_gain, ("dp", "seq"), axis=0, tiled=True),
        lax.all_gather(ln2_shift, ("dp", "seq"), axis=0, tiled=True),
        lax.all_gather(b_fc1, ("dp", "seq"), axis=0, tiled=True),
        lax.all_gather(b_fc2, ("dp", "seq"), axis=0, tiled=True),
    )
    gain_one = gain_one.astype(f32)
    shift_one = shift_one.astype(f32)
    bias_qv = bias_qv.astype(f32)
    bias_out = bias_out.astype(f32)
    gain_two = gain_two.astype(f32)
    shift_two = shift_two.astype(f32)
    bias_up = bias_up.astype(f32)
    bias_down = bias_down.astype(f32)
    query_start = lax.axis_index("seq") * row_count
    local_width = heads * HEAD_DIM

    def collect():
        qkv_w, out_w, up_w, down_w = (
            lax.all_gather(w_qkv, "dp", axis=0, tiled=True),
            lax.all_gather(w_out, "dp", axis=1, tiled=True),
            lax.all_gather(w_fc1, "dp", axis=0, tiled=True),
            lax.all_gather(w_fc2, "dp", axis=1, tiled=True),
        )
        qkv_w, out_w, up_w, down_w = (
            lax.all_gather(qkv_w, "seq", axis=2, tiled=True),
            lax.all_gather(out_w, "seq", axis=0, tiled=True),
            lax.all_gather(up_w, "seq", axis=1, tiled=True),
            lax.all_gather(down_w, "seq", axis=0, tiled=True),
        )
        return (qkv_w, out_w, up_w, down_w)

    stream = tokens.astype(f32)
    length = lengths[0]
    own_pos = lax.axis_index("seq") * row_count + jnp.arange(row_count, dtype=jnp.int32)
    is_valid = own_pos < length
    qkv_w, out_w, up_w, down_w = collect()
    normed, unit_one, inv_one = layer_norm(stream, gain_one, shift_one)
    normed_wide = normed.astype(bf16)
    merged = jnp.einsum("td,dce->tce", normed_wide, qkv_w, preferred_element_type=f32)
    bias_local = bias_qv.reshape(2, width)
    queries = (merged[:, 0] + bias_local[0]).astype(bf16)
    key_own = merged[:, 1].astype(bf16)
    value_own = (merged[:, 2] + bias_local[1]).astype(bf16)
    key_all, value_all = (
        lax.all_gather(key_own, "seq", axis=0, tiled=True),
        lax.all_gather(value_own, "seq", axis=0, tiled=True),
    )
    key_count = key_all.shape[0]
    key_pos = jnp.arange(key_count, dtype=jnp.int32)
    query_pos = query_start + jnp.arange(row_count, dtype=jnp.int32)
    slopes = (2.0 ** (-8.0 * (jnp.arange(heads, dtype=jnp.int32) + 1).astype(f32) / heads)).reshape(
        heads // 2, 2
    )
    score_scale = HEAD_DIM ** (-0.5)
    q_block = min(512, row_count)
    block_count = row_count // q_block
    groups = heads // 2

    def to_blocks(matrix):
        return matrix.reshape(block_count, q_block, groups, 2, HEAD_DIM).transpose(0, 2, 3, 1, 4)

    def from_blocks(blocks):
        return blocks.transpose(0, 3, 1, 2, 4).reshape(row_count, local_width)

    def scores_of(query_pair, key_pair, slope_pair, pos_block):
        raw = (
            jnp.einsum("hqd,hkd->hqk", query_pair, key_pair, preferred_element_type=f32)
            * score_scale
        )
        offset = (key_pos[None, :] - pos_block[:, None]).astype(f32)
        allowed = (key_pos[None, :] <= pos_block[:, None]) & (key_pos[None, :] < length)
        raw = raw + slope_pair[:, None, None] * offset[None]
        return jnp.where(allowed[None], raw, -1e30)

    query_blocks = to_blocks(queries)
    pos_blocks = query_pos.reshape(block_count, q_block)
    key_groups = split_heads(key_all)
    value_groups = split_heads(value_all)

    def attend_block(items):
        query_blk, pos_blk = items

        def attend_group(parts):
            query_pair, key_pair, value_pair, slope_pair = parts
            scores = scores_of(query_pair, key_pair, slope_pair, pos_blk)
            top = jnp.max(scores, axis=-1, keepdims=True)
            expo = jnp.exp(scores - top)
            denom = jnp.sum(expo, axis=-1, keepdims=True)
            probs = (expo / denom).astype(bf16)
            mixed = jnp.einsum("hqk,hkd->hqd", probs, value_pair, preferred_element_type=f32)
            return (mixed, top[..., 0] + jnp.log(denom[..., 0]))

        return lax.map(attend_group, (query_blk, key_groups, value_groups, slopes))

    mixed_blocks, log_blocks = lax.map(attend_block, (query_blocks, pos_blocks))
    mixed_low = from_blocks(mixed_blocks).astype(bf16)
    middle = stream + jnp.dot(mixed_low, out_w, preferred_element_type=f32) + bias_out
    normed_two, unit_two, inv_two = layer_norm(middle, gain_two, shift_two)
    normed_two_wide = normed_two.astype(bf16)
    hidden_pre = jnp.dot(normed_two_wide, up_w, preferred_element_type=f32) + bias_up
    hidden, hidden_slope = gelu_parts(hidden_pre)
    hidden_low = hidden.astype(bf16)
    output = (middle + jnp.dot(hidden_low, down_w, preferred_element_type=f32) + bias_down).astype(
        bf16
    )
    qkv_w, out_w, up_w, down_w = collect()
    grad_low = jnp.where(is_valid[:, None], cotangent, jnp.zeros_like(cotangent))
    grad_bias_down = jnp.sum(grad_low.astype(f32), axis=0)
    grad_down = jnp.einsum("tf,td->fd", hidden_low, grad_low, preferred_element_type=f32)
    grad_hidden = jnp.einsum("td,fd->tf", grad_low, down_w, preferred_element_type=f32)
    grad_pre_low = (grad_hidden * hidden_slope).astype(bf16)
    grad_up = jnp.einsum("td,tf->df", normed_two_wide, grad_pre_low, preferred_element_type=f32)
    grad_bias_up = jnp.sum(grad_pre_low.astype(f32), axis=0)
    grad_normed_two = jnp.einsum("tf,df->td", grad_pre_low, up_w, preferred_element_type=f32)
    grad_mid_part, grad_gain_two, grad_shift_two = norm_back(
        grad_normed_two, gain_two, unit_two, inv_two
    )
    grad_middle = grad_low.astype(f32) + grad_mid_part
    grad_branch_low = grad_middle.astype(bf16)
    grad_bias_out = jnp.sum(grad_branch_low.astype(f32), axis=0)
    grad_out_proj = jnp.einsum("te,td->ed", mixed_low, grad_branch_low, preferred_element_type=f32)
    grad_mixed_low = jnp.einsum(
        "td,ed->te", grad_branch_low, out_w, preferred_element_type=f32
    ).astype(bf16)

    def back_block(totals, items):
        query_blk, grad_blk, log_blk, pos_blk = items

        def back_group(parts):
            query_pair, key_pair, value_pair, grad_pair, log_pair, slope_pair = parts
            scores = scores_of(query_pair, key_pair, slope_pair, pos_blk)
            probs = jnp.exp(scores - log_pair[..., None])
            grad_probs = jnp.einsum(
                "hqd,hkd->hqk", grad_pair, value_pair, preferred_element_type=f32
            )
            row_dot = jnp.sum(grad_probs * probs, axis=-1, keepdims=True)
            grad_scores = (probs * (grad_probs - row_dot)).astype(bf16)
            grad_query = (
                jnp.einsum("hqk,hkd->hqd", grad_scores, key_pair, preferred_element_type=f32)
                * score_scale
            )
            grad_key = (
                jnp.einsum("hqk,hqd->hkd", grad_scores, query_pair, preferred_element_type=f32)
                * score_scale
            )
            grad_value = jnp.einsum(
                "hqk,hqd->hkd", probs.astype(bf16), grad_pair, preferred_element_type=f32
            )
            return (grad_query, grad_key, grad_value)

        grad_q, grad_k, grad_v = lax.map(
            back_group, (query_blk, key_groups, value_groups, grad_blk, log_blk, slopes)
        )
        return ((totals[0] + grad_k, totals[1] + grad_v), grad_q)

    empty = jnp.zeros(key_groups.shape, f32)
    (grad_k_groups, grad_v_groups), grad_q_blocks = lax.scan(
        back_block,
        (empty, empty),
        (query_blocks, to_blocks(grad_mixed_low), log_blocks, pos_blocks),
    )
    key_sum = join_heads(grad_k_groups)
    value_sum = join_heads(grad_v_groups)
    key_sum, value_sum = (
        lax.psum_scatter(
            key_sum.astype(jnp.bfloat16), "seq", scatter_dimension=0, tiled=True
        ).astype(jnp.float32),
        lax.psum_scatter(
            value_sum.astype(jnp.bfloat16), "seq", scatter_dimension=0, tiled=True
        ).astype(jnp.float32),
    )
    grad_query_low = from_blocks(grad_q_blocks).astype(bf16)
    grad_merged_low = jnp.stack(
        [grad_query_low, key_sum.astype(bf16), value_sum.astype(bf16)], axis=1
    )
    grad_qkv = jnp.einsum("td,tce->dce", normed_wide, grad_merged_low, preferred_element_type=f32)
    qv_sums = jnp.stack(
        [
            jnp.sum(grad_merged_low[:, 0].astype(f32), axis=0),
            jnp.sum(grad_merged_low[:, 2].astype(f32), axis=0),
        ]
    )
    grad_bias_qv = qv_sums.reshape(2 * width)
    grad_normed = jnp.einsum("tce,dce->td", grad_merged_low, qkv_w, preferred_element_type=f32)
    grad_in_part, grad_gain_one, grad_shift_one = norm_back(
        grad_normed, gain_one, unit_one, inv_one
    )
    grad_tokens = (grad_middle + grad_in_part).astype(bf16)
    grad_qkv, grad_out_proj, grad_up, grad_down = (
        lax.psum_scatter(
            grad_qkv.astype(jnp.bfloat16), "seq", scatter_dimension=2, tiled=True
        ).astype(jnp.float32),
        lax.psum_scatter(
            grad_out_proj.astype(jnp.bfloat16), "seq", scatter_dimension=0, tiled=True
        ).astype(jnp.float32),
        lax.psum_scatter(
            grad_up.astype(jnp.bfloat16), "seq", scatter_dimension=1, tiled=True
        ).astype(jnp.float32),
        lax.psum_scatter(
            grad_down.astype(jnp.bfloat16), "seq", scatter_dimension=0, tiled=True
        ).astype(jnp.float32),
    )
    grad_qkv, grad_out_proj, grad_up, grad_down = (
        lax.psum_scatter(grad_qkv, "dp", scatter_dimension=0, tiled=True),
        lax.psum_scatter(grad_out_proj, "dp", scatter_dimension=1, tiled=True),
        lax.psum_scatter(grad_up, "dp", scatter_dimension=0, tiled=True),
        lax.psum_scatter(grad_down, "dp", scatter_dimension=1, tiled=True),
    )
    (
        grad_gain_one,
        grad_shift_one,
        grad_bias_qv,
        grad_bias_out,
        grad_gain_two,
        grad_shift_two,
        grad_bias_up,
        grad_bias_down,
    ) = (
        lax.psum_scatter(grad_gain_one, ("dp", "seq"), scatter_dimension=0, tiled=True),
        lax.psum_scatter(grad_shift_one, ("dp", "seq"), scatter_dimension=0, tiled=True),
        lax.psum_scatter(grad_bias_qv, ("dp", "seq"), scatter_dimension=0, tiled=True),
        lax.psum_scatter(grad_bias_out, ("dp", "seq"), scatter_dimension=0, tiled=True),
        lax.psum_scatter(grad_gain_two, ("dp", "seq"), scatter_dimension=0, tiled=True),
        lax.psum_scatter(grad_shift_two, ("dp", "seq"), scatter_dimension=0, tiled=True),
        lax.psum_scatter(grad_bias_up, ("dp", "seq"), scatter_dimension=0, tiled=True),
        lax.psum_scatter(grad_bias_down, ("dp", "seq"), scatter_dimension=0, tiled=True),
    )
    return (
        output,
        grad_tokens,
        grad_gain_one,
        grad_shift_one,
        grad_qkv,
        grad_bias_qv,
        grad_out_proj,
        grad_bias_out,
        grad_gain_two,
        grad_shift_two,
        grad_up,
        grad_bias_up,
        grad_down,
        grad_bias_down,
    )


def solution(mesh):
    return jax.shard_map(
        on_device,
        mesh=mesh,
        in_specs=(
            P(("dp", "seq"), None),
            P("dp"),
            P(("dp", "seq"), None),
            P(("dp", "seq")),
            P(("dp", "seq")),
            P("dp", None, "seq"),
            P(("dp", "seq")),
            P("seq", "dp"),
            P(("dp", "seq")),
            P(("dp", "seq")),
            P(("dp", "seq")),
            P("dp", "seq"),
            P(("dp", "seq")),
            P("seq", "dp"),
            P(("dp", "seq")),
        ),
        out_specs=(
            P(("dp", "seq"), None),
            P(("dp", "seq"), None),
            P(("dp", "seq")),
            P(("dp", "seq")),
            P("dp", None, "seq"),
            P(("dp", "seq")),
            P("seq", "dp"),
            P(("dp", "seq")),
            P(("dp", "seq")),
            P(("dp", "seq")),
            P("dp", "seq"),
            P(("dp", "seq")),
            P("seq", "dp"),
            P(("dp", "seq")),
        ),
        check_vma=False,
    )
```

profile of v0, /device:TPU:0, one launch (start us, length us, event | category | flops | bytes accessed | tf_op | source)
XLA Modules:
  0.0 1198.3 jit_solution(9885463966526346443)
XLA Ops:
  8.0 49.2 %all-gather.12.cloned.1.call-done = bf16[1024,3,256]{2,0,1:T(8,128)(2,1)} async-done(((bf16[128,3,256]{2,0,1:T(8,128)(2,1)}), bf16[1024,3,256]{2,0,1:T(8,128)(2,1)}) %all-gather.12.cloned.1.call-update) | async-done | bytes 1572880 | tf_op jit(solution)/shard_map/all_gather | solution.py:95
  64.4 40.3 %all-reduce.16 = (bf16[1024]{0:T(1024)(128)(2,1)S(1)}, bf16[1024]{0:T(1024)(128)(2,1)S(1)}, bf16[2048]{0:T(1024)(128)(2,1)S(1)}, bf16[1024]{0:T(1024)(128)(2,1)S...) all-reduce(bf16[1024]{0:T(1024)(128)(2,1)S(1)} %dynamic-update-slic, ...), channel_id=1, replica_groups=mesh['dp'=8,'seq'=4] {'dp','seq'}, use_global_device_ids=true, to_apply=%add.1 | all-reduce | flops 8192 | bytes 32768
  106.4 4.9 fusion.82
  114.6 2.6 fusion.76
  117.3 31.3 %all_gather.69 = bf16[256,1024]{1,0:T(8,128)(2,1)} all-gather(bf16[256,128]{1,0:T(8,128)(2,1)S(1)} %copy-done.16), channel_id=1, replica_groups=mesh['dp'=8,'seq'=4] {'dp'}, dimensions={1}, use_global_device_ids=true | all-gather | bytes 589824 | tf_op jit(solution)/shard_map/all_gather | solution.py:96
  148.6 13.3 %all-gather.20.cloned.1.call-done = bf16[1024,1024]{1,0:T(8,128)(2,1)} async-done(((bf16[128,1024]{1,0:T(8,128)(2,1)}), bf16[1024,1024]{1,0:T(8,128)(2,1)}) %all-gather.20.cloned.1.call-update) | async-done | bytes 2097168 | tf_op jit(solution)/shard_map/all_gather | solution.py:97
  162.1 39.8 %all-gather.1 = bf16[32,1,128]{2,1,0:T(2,128)(2,1)S(1)} all-gather(bf16[1,1,128]{2,1,0:T(2,128)(2,1)S(1)} %bitcast.192), channel_id=1, replica_groups=mesh['dp'=8,'seq'=4] {'dp','seq'}, dimensions={0}, use_global_device_ids=true | all-gather | bytes 8448 | tf_op jit(solution)/shard_map/all_gather | solution.py:79
  202.7 10.5 all-gather.24.cloned.1.call-done
  214.8 27.1 %all-gather.28.cloned.1.call-done = bf16[1536,1,1024]{2,0,1:T(8,128)(2,1)} async-done(((bf16[384,1,1024]{2,0,1:T(8,128)(2,1)}), bf16[1536,1,1024]{2,0,1:T(8,128)(2,1)}) %all-gather.28.cloned.1.call-update) | async-done | bytes 3145744 | tf_op jit(solution)/shard_map/all_gather | solution.py:121
  241.9 3.6 copy.46
  245.6 26.3 %all-gather.16.cloned.1.call-done = bf16[1536,1024]{1,0:T(8,128)(2,1)} async-done(((bf16[384,1024]{1,0:T(8,128)(2,1)}), bf16[1536,1024]{1,0:T(8,128)(2,1)}) %all-gather.16.cloned.1.call-update) | async-done | bytes 3145744 | tf_op jit(solution)/shard_map/all_gather | solution.py:122
  271.9 4.6 copy.47
  277.5 59.0 %while.50 = (s32[]{:T(128)}, bf16[8,2,384,64]{2,3,1,0:T(8,128)(2,1)}, f32[8,2,384]{2,1,0:T(2,128)S(1)}, s32[]{:T(128)}, bf16[8,2,384,64]{2,3,1,0:T(8,128)(2,1)},...) while((s32[]{:T(128)}, ...), condition=%wide.region_5.6_spmd.clone.clone, body=%wide.region_2.5_spmd.clone.clone.sunk | while | flops 316146816 | bytes 21170316 | solution.py:169
  278.9 2.5 fusion.130
  282.2 2.7 fusion.132
  286.3 2.5 fusion.130
  289.5 2.7 fusion.132
  293.6 2.5 fusion.130
  296.9 2.7 fusion.132
  304.3 2.7 fusion.132
  308.4 2.5 fusion.130
  311.7 2.7 fusion.132
  315.8 2.5 fusion.130
  319.1 2.7 fusion.132
  326.5 2.7 fusion.132
  330.5 2.5 fusion.130
  333.8 2.7 fusion.132
  336.5 3.1 fusion.90
  341.1 14.8 %all-gather.22.cloned.1.call-done = bf16[1024,4096]{1,0:T(8,128)(2,1)} async-done(((bf16[1024,1024]{1,0:T(8,128)(2,1)}), bf16[1024,4096]{1,0:T(8,128)(2,1)}) %all-gather.22.cloned.1.call-update) | async-done | bytes 8388624 | tf_op jit(solution)/shard_map/all_gather | solution.py:103
  355.9 10.5 convolution_add_fusion
  366.4 49.4 %all-gather.26.cloned.1.call-done = bf16[4096,1024]{1,0:T(8,128)(2,1)} async-done(((bf16[1024,1024]{1,0:T(8,128)(2,1)}), bf16[4096,1024]{1,0:T(8,128)(2,1)}) %all-gather.26.cloned.1.call-update) | async-done | bytes 8388624 | tf_op jit(solution)/shard_map/all_gather | solution.py:104
  415.8 10.3 convert_reduce_fusion
  427.8 3.9 multiply_reduce_fusion.1
  438.8 97.4 %while.51 = (s32[]{:T(128)}, bf16[8,2,384,64]{2,3,1,0:T(8,128)(2,1)}, bf16[8,2,1536,64]{2,3,1,0:T(8,128)(2,1)}, bf16[8,2,1536,64]{2,3,1,0:T(8,128)(2,1)}, s32[]{...) while((s32[]{:T(128)}, ...), condition=%wide.region_12.13_spmd.clone.clone, body=%wide.region_10.12_spmd.clone.clone.sunk | while | flops 770557056 | bytes 44658852 | solution.py:227
  440.2 2.5 subtract_exponential_fusion.3
  452.3 2.5 subtract_exponential_fusion.3
  464.5 2.5 subtract_exponential_fusion.3
  476.7 2.5 subtract_exponential_fusion.3
  488.9 2.5 subtract_exponential_fusion.3
  501.0 2.5 subtract_exponential_fusion.3
  513.2 2.5 subtract_exponential_fusion.3
  525.4 2.5 subtract_exponential_fusion.3
  536.2 4.6 copy.50
  542.8 2.9 copy.49
  547.4 3.8 convolution_convert_fusion.3
  552.7 26.3 %reduce-scatter.13.cloned.1.call-done = bf16[384,1024]{1,0:T(8,128)(2,1)} async-done(((bf16[1536,1024]{1,0:T(8,128)(2,1)}), bf16[384,1024]{1,0:T(8,128)(2,1)}) %reduce-scatter.13.cloned.1.call-update) | async-done | bytes 786448 | tf_op jit(solution)/shard_map/reduce_scatter | solution.py:244
  578.9 40.5 %reduce-scatter.11.cloned.1.call-done = bf16[384,1024]{1,0:T(8,128)(2,1)} async-done(((bf16[1536,1024]{1,0:T(8,128)(2,1)}), bf16[384,1024]{1,0:T(8,128)(2,1)}) %reduce-scatter.11.cloned.1.call-update) | async-done | bytes 786448 | tf_op jit(solution)/shard_map/reduce_scatter | solution.py:241
  619.4 7.3 convolution_convert_fusion.2
  628.2 9.3 convolution_convert_fusion.1
  637.5 11.6 convolution_convert_fusion
  649.2 3.8 reduce-scatter.19.cloned.1.call-done
  655.2 58.2 %reduce-scatter.15.cloned.1.call-done = bf16[1024,3,256]{2,0,1:T(8,128)(2,1)} async-done(((bf16[1024,3,1024]{2,0,1:T(8,128)(2,1)}), bf16[1024,3,256]{2,0,1:T(8,128)(2,1)}) %reduce-scatter.15.cloned.1.call-update) | async-done | bytes 1572880 | tf_op jit(solution)/shard_map/reduce_scatter | solution.py:266
  713.4 3.3 convert_element_type.233
  716.8 70.3 %reduce-scatter.23.cloned.1.call-done = bf16[1024,1024]{1,0:T(8,128)(2,1)} async-done(((bf16[1024,4096]{1,0:T(8,128)(2,1)}), bf16[1024,1024]{1,0:T(8,128)(2,1)}) %reduce-scatter.23.cloned.1.call-update) | async-done | bytes 2097168 | tf_op jit(solution)/shard_map/reduce_scatter | solution.py:272
  787.1 4.0 convert_element_type.240
  791.5 69.5 %reduce-scatter.27.cloned.1.call-done = bf16[1024,1024]{1,0:T(8,128)(2,1)} async-done(((bf16[4096,1024]{1,0:T(8,128)(2,1)}), bf16[1024,1024]{1,0:T(8,128)(2,1)}) %reduce-scatter.27.cloned.1.call-update) | async-done | bytes 2097168 | tf_op jit(solution)/shard_map/reduce_scatter | solution.py:275
  861.0 4.0 convert_element_type.243
  867.1 10.2 add_convert_fusion
  877.6 7.0 fusion.72
  884.6 40.0 %all-reduce.15 = (f32[1024]{0:T(1024)S(1)}, f32[1024]{0:T(1024)S(1)}, f32[2048]{0:T(1024)S(1)}, f32[1024]{0:T(1024)S(1)}, f32[1024]{0:T(1024)S(1)}, /*index=5*/f...) all-reduce(f32[1024]{0:T(1024)S(1)} %get-tuple-element.330, ...), channel_id=5, replica_groups=mesh['dp'=8,'seq'=4] {'dp','seq'}, use_global_device_ids=true, to_apply=%region_18.19.clone | all-reduce | flops 12288 | bytes 98304
  929.3 2.9 fusion.71
  932.1 75.2 %reduce-scatter.17.cloned.1.call-done = f32[128,3,256]{2,0,1:T(8,128)} async-done(((f32[1024,3,256]{2,0,1:T(8,128)}), f32[128,3,256]{2,0,1:T(8,128)}) %reduce-scatter.17.cloned.1.call-update) | async-done | bytes 393232 | tf_op jit(solution)/shard_map/reduce_scatter | solution.py:280
  1007.3 91.5 %reduce-scatter.25.cloned.1.call-done = f32[128,1024]{1,0:T(8,128)} async-done(((f32[1024,1024]{1,0:T(8,128)}), f32[128,1024]{1,0:T(8,128)}) %reduce-scatter.25.cloned.1.call-update) | async-done | bytes 524304 | tf_op jit(solution)/shard_map/reduce_scatter | solution.py:282
  1098.8 92.5 %reduce-scatter.29.cloned.1.call-done = f32[1024,128]{1,0:T(8,128)} async-done(((f32[1024,1024]{1,0:T(8,128)}), f32[1024,128]{1,0:T(8,128)}) %reduce-scatter.29.cloned.1.call-update) | async-done | bytes 524304 | tf_op jit(solution)/shard_map/reduce_scatter | solution.py:283
  (310 shorter events, 141.2 us)
Async XLA Ops:
  7.2 98.8 %copy-start.5 = (bf16[384,1024]{1,0:T(8,128)(2,1)S(1)}, bf16[384,1024]{1,0:T(8,128)(2,1)}, u32[]{:S(2)}) copy-start(bf16[384,1024]{1,0:T(8,128)(2,1)} %param.19) | copy-start | bytes 2359300
  7.2 49.9 %all-gather.12.cloned.1.call-start = ((), (), s32[]{:S(2)}) async-start(), calls=%async_computation.10 | async-start | bytes 1769472 | tf_op jit(solution)/shard_map/all_gather | solution.py:95
  7.9 98.5 %all-gather.14.cloned.1.call-start = ((), (), s32[]{:S(2)}) async-start(), calls=%async_computation.11 | async-start | bytes 7864320 | tf_op jit(solution)/shard_map/all_gather | solution.py:101
  57.1 104.7 %all-gather.20.cloned.1.call-start = ((), (), s32[]{:S(2)}) async-start(), calls=%async_computation.14 | async-start | bytes 2359296 | tf_op jit(solution)/shard_map/all_gather | solution.py:97
  57.9 155.3 %all-gather.24.cloned.1.call-start = ((), (), s32[]{:S(2)}) async-start(), calls=%async_computation.16 | async-start | bytes 2359296 | tf_op jit(solution)/shard_map/all_gather | solution.py:98
  58.5 183.5 %all-gather.28.cloned.1.call-start = ((), (), s32[]{:S(2)}) async-start(), calls=%async_computation.28 | async-start | bytes 3932160 | tf_op jit(solution)/shard_map/all_gather | solution.py:121
  104.7 6.7 copy-start.23
  104.7 6.7 copy-start.19
  106.0 5.4 copy-start.17
  106.4 5.0 copy-start.21
  111.4 2.1 copy-start.10
  113.5 3.7 copy-start.16
  114.5 157.3 %all-gather.16.cloned.1.call-start = ((), (), s32[]{:S(2)}) async-start(), calls=%async_computation.12 | async-start | bytes 3932160 | tf_op jit(solution)/shard_map/all_gather | solution.py:122
  114.6 47.5 %copy-start.26 = (bf16[128]{0:T(256)(128)(2,1)S(1)}, bf16[128]{0:T(256)(128)(2,1)}, u32[]{:S(2)}) copy-start(bf16[128]{0:T(256)(128)(2,1)} %param.31) | copy-start | bytes 772
  117.2 219.3 %all-gather.18.cloned.1.call-start = ((), (), s32[]{:S(2)}) async-start(), calls=%async_computation.13 | async-start | bytes 2621440 | tf_op jit(solution)/shard_map/all_gather | solution.py:102
  148.6 207.4 %all-gather.22.cloned.1.call-start = ((), (), s32[]{:S(2)}) async-start(), calls=%async_computation.15 | async-start | bytes 10485760 | tf_op jit(solution)/shard_map/all_gather | solution.py:103
  161.9 51.4 %slice-start = ((f32[384,3,1024]{2,0,1:T(8,128)}), f32[384,1,1024]{2,0,1:T(8,128)S(1)}, s32[]{:S(2)}) async-start(f32[384,3,1024]{2,0,1:T(8,128)} %copy-done.10), calls=%async_computation.29 | async-start | bytes 3145728 | tf_op jit(solution)/shard_map/slice | solution.py:117
  161.9 253.9 %all-gather.26.cloned.1.call-start = ((), (), s32[]{:S(2)}) async-start(), calls=%async_computation.17 | async-start | bytes 10485760 | tf_op jit(solution)/shard_map/all_gather | solution.py:104
  213.2 365.7 %reduce-scatter.13.cloned.1.call-start = ((), (), s32[]{:S(2)}) async-start(), calls=%async_computation.19 | async-start | bytes 3932160 | tf_op jit(solution)/shard_map/reduce_scatter | solution.py:244
  339.6 1.1 copy-start.2
  415.8 12.0 copy-start.3
  415.8 12.0 copy-start.27
  426.1 1.6 copy-start.29
  427.8 3.9 copy-start.13
  431.6 2.0 copy-start.12
  432.4 1.1 copy-start
  540.9 1.9 copy-start.11
  540.9 78.5 %reduce-scatter.11.cloned.1.call-start = ((), (), s32[]{:S(2)}) async-start(), calls=%async_computation.18 | async-start | bytes 3932160 | tf_op jit(solution)/shard_map/reduce_scatter | solution.py:241
  545.7 1.7 copy-start.1
  545.7 5.8 copy-start.9
  545.7 73.7 %copy-start.6 = (bf16[384,1024]{1,0:T(8,128)(2,1)S(1)}, bf16[384,1024]{1,0:T(8,128)(2,1)}, u32[]{:S(2)}) copy-start(bf16[384,1024]{1,0:T(8,128)(2,1)} %param.19) | copy-start | bytes 2359300
  545.7 73.7 %copy-start.18 = (f32[384]{0:T(512)S(1)}, f32[384]{0:T(512)}, u32[]{:S(2)}) copy-start(f32[384]{0:T(512)} %copy-done.17) | copy-start | bytes 4612
  545.7 73.7 %copy-start.20 = (f32[1024]{0:T(1024)S(1)}, f32[1024]{0:T(1024)}, u32[]{:S(2)}) copy-start(f32[1024]{0:T(1024)} %copy-done.19) | copy-start | bytes 12292
  545.8 73.7 %copy-start.22 = (f32[384]{0:T(512)S(1)}, f32[384]{0:T(512)}, u32[]{:S(2)}) copy-start(f32[384]{0:T(512)} %copy-done.21) | copy-start | bytes 4612
  545.8 73.6 %copy-start.24 = (f32[1024]{0:T(1024)S(1)}, f32[1024]{0:T(1024)}, u32[]{:S(2)}) copy-start(f32[1024]{0:T(1024)} %copy-done.23) | copy-start | bytes 12292
  545.8 107.2 %reduce-scatter.19.cloned.1.call-start = ((), (), s32[]{:S(2)}) async-start(), calls=%async_computation.22 | async-start | bytes 2621440 | tf_op jit(solution)/shard_map/reduce_scatter | solution.py:269
  551.2 162.2 %reduce-scatter.15.cloned.1.call-start = ((), (), s32[]{:S(2)}) async-start(), calls=%async_computation.20 | async-start | bytes 7864320 | tf_op jit(solution)/shard_map/reduce_scatter | solution.py:266
  626.7 1.5 copy-start.4
  626.7 160.4 %reduce-scatter.23.cloned.1.call-start = ((), (), s32[]{:S(2)}) async-start(), calls=%async_computation.24 | async-start | bytes 10485760 | tf_op jit(solution)/shard_map/reduce_scatter | solution.py:272
  637.5 223.5 %reduce-scatter.27.cloned.1.call-start = ((), (), s32[]{:S(2)}) async-start(), calls=%async_computation.26 | async-start | bytes 10485760 | tf_op jit(solution)/shard_map/reduce_scatter | solution.py:275
  649.1 283.0 %reduce-scatter.21.cloned.1.call-start = ((), (), s32[]{:S(2)}) async-start(), calls=%async_computation.23 | async-start | bytes 1179648 | tf_op jit(solution)/shard_map/reduce_scatter | solution.py:281
  655.2 352.2 %reduce-scatter.17.cloned.1.call-start = ((), (), s32[]{:S(2)}) async-start(), calls=%async_computation.21 | async-start | bytes 3538944 | tf_op jit(solution)/shard_map/reduce_scatter | solution.py:280
  716.8 382.0 %reduce-scatter.25.cloned.1.call-start = ((), (), s32[]{:S(2)}) async-start(), calls=%async_computation.25 | async-start | bytes 4718592 | tf_op jit(solution)/shard_map/reduce_scatter | solution.py:282
  791.2 400.2 %reduce-scatter.29.cloned.1.call-start = ((), (), s32[]{:S(2)}) async-start(), calls=%async_computation.27 | async-start | bytes 4718592 | tf_op jit(solution)/shard_map/reduce_scatter | solution.py:283
  865.0 0.7 copy-start.25
  867.1 10.2 copy-start.14
  867.1 10.4 copy-start.7
  867.1 10.4 copy-start.15
  867.1 10.4 copy-start.28
  877.6 51.7 %copy-start.8 = (bf16[384,1024]{1,0:T(8,128)(2,1)S(1)}, bf16[384,1024]{1,0:T(8,128)(2,1)}, u32[]{:S(2)}) copy-start(bf16[384,1024]{1,0:T(8,128)(2,1)} %param.19) | copy-start | bytes 2359300
Sparse Core Ops, SparseCore 0:
  10.2 46.8 all-gather.11
  58.7 46.6 all-gather.13
  107.5 54.3 all-gather.19
  163.8 49.3 all-gather.23
  215.2 26.6 all-gather.27
  243.3 28.4 all-gather.15
  273.4 22.5 all-gather.17
  297.6 58.2 all-gather.21
  357.5 58.2 all-gather.25
  541.0 37.8 reduce-scatter.12
  581.5 37.8 reduce-scatter.10
  621.8 31.1 reduce-scatter.18
  655.5 57.8 reduce-scatter.14
  715.9 71.2 reduce-scatter.22
  789.6 71.3 reduce-scatter.26
  864.8 64.7 reduce-scatter.20
  933.6 73.6 reduce-scatter.16
  1011.4 87.3 reduce-scatter.24
  1103.0 88.3 reduce-scatter.28
where the time goes:
time: 1210 us; the launch traced here: 1200 us
  waiting for transfers between devices  721 us (60%)
  matrix products  208 us (17%)
  blocking collectives  151 us (12%)
  other arithmetic  55.8 us (5%)
  local copies, waits for them, and re-layouts  45.2 us (4%)
  between operations  15.6 us (1%)
    reduce_scatter x1, waiting for transfers between devices, on_device(): lax.psum_scatter(grad_down, 'dp', scatter_dimension=1, tiled=True)  92.5 us
    reduce_scatter x1, waiting for transfers between devices, on_device(): lax.psum_scatter(grad_up, 'dp', scatter_dimension=0, tiled=True)  91.5 us
    unnamed x2, blocking collectives  80.3 us
    reduce_scatter x1, waiting for transfers between devices, on_device(): lax.psum_scatter(grad_qkv, 'dp', scatter_dimension=0, tiled=True)  75.2 us
    reduce_scatter x1, waiting for transfers between devices, on_device(): lax.psum_scatter(grad_up.astype(jnp.bfloat16), 'seq', scatter_dimension=1...  70.3 us
    reduce_scatter x1, waiting for transfers between devices, on_device(): lax.psum_scatter(grad_down.astype(jnp.bfloat16), 'seq', scatter_dimension...  69.5 us
    reduce_scatter x1, waiting for transfers between devices, on_device(): lax.psum_scatter(grad_qkv.astype(jnp.bfloat16), 'seq', scatter_dimension=...  58.2 us
    all_gather x1, waiting for transfers between devices, collect(): lax.all_gather(down_w, 'seq', axis=0, tiled=True)  49.4 us
  transfers between devices with their start and end apart: 19, of which 16 were waited for; matrix products, arithmetic and copies ran while one was open for 15% of the time, Pallas kernels for 0%

commit v1 on v0

v1 whole, which is shorter than its diff:
```python
import functools
import math

import jax
import jax.numpy as jnp
from jax import lax
from jax.experimental import pallas as pl
from jax.experimental.pallas import tpu as pltpu
from jax.sharding import PartitionSpec as P

HEAD_DIM = 64
EPS = 1e-05
GELU_COEF = 0.044715
NEG = -1e30
LANES = 128
VMEM_BYTES = 60 * 1024 * 1024

f32 = jnp.float32
bf16 = jnp.bfloat16
WHOLE = pl.BlockSpec(memory_space=pltpu.VMEM)
SCALAR = pl.BlockSpec(memory_space=pltpu.SMEM)


def mm(a, b):
    return jnp.dot(a, b, preferred_element_type=f32)


def mm_t(a, b):
    return lax.dot_general(a, b, (((1,), (1,)), ((), ())), preferred_element_type=f32)


def params(**kw):
    return pltpu.CompilerParams(vmem_limit_bytes=VMEM_BYTES, **kw)


def normalize(v):
    width = v.shape[-1]
    centred = v - jnp.sum(v, axis=-1, keepdims=True) * (1.0 / width)
    inv = lax.rsqrt(jnp.sum(centred * centred, axis=-1, keepdims=True) * (1.0 / width) + EPS)
    return centred * inv, inv


def norm_back(grad_out, gain, unit, inv):
    width = unit.shape[-1]
    scaled = grad_out * gain
    mean_one = jnp.sum(scaled, axis=-1, keepdims=True) * (1.0 / width)
    mean_two = jnp.sum(scaled * unit, axis=-1, keepdims=True) * (1.0 / width)
    return inv * (scaled - mean_one - unit * mean_two)


def device_of(index, seq_n):
    return (index // seq_n, index % seq_n)


def greet_all(me, count, seq_n):
    barrier = pltpu.get_barrier_semaphore()

    def hello(i, carry):
        peer = (me + i) % count
        pl.semaphore_signal(
            barrier, inc=1, device_id=device_of(peer, seq_n), device_id_type=pl.DeviceIdType.MESH
        )
        return carry

    lax.fori_loop(1, count, hello, 0)
    pl.semaphore_wait(barrier, count - 1)


def small_gather_body(count, seq_n, x_ref, out_ref, send_sem, recv_sem):
    me = lax.axis_index("dp") * seq_n + lax.axis_index("seq")
    greet_all(me, count, seq_n)

    def copy_to(i):
        peer = (me + i) % count
        return pltpu.make_async_remote_copy(
            src_ref=x_ref,
            dst_ref=out_ref.at[pl.ds(me, 1)],
            send_sem=send_sem.at[i],
            recv_sem=recv_sem.at[i],
            device_id=device_of(peer, seq_n),
            device_id_type=pl.DeviceIdType.MESH,
        )

    def begin(i, carry):
        copy_to(i).start()
        return carry

    def finish(i, carry):
        copy_to(i).wait()
        return carry

    lax.fori_loop(1, count, begin, 0)
    out_ref[pl.ds(me, 1)] = x_ref[...]
    lax.fori_loop(1, count, finish, 0)


def small_gather(x, count, seq_n):
    width = x.shape[-1]
    return pl.pallas_call(
        functools.partial(small_gather_body, count, seq_n),
        out_shape=jax.ShapeDtypeStruct((count, 1, width), f32),
        in_specs=[WHOLE],
        out_specs=WHOLE,
        scratch_shapes=[pltpu.SemaphoreType.DMA((count,)), pltpu.SemaphoreType.DMA((count,))],
        compiler_params=pltpu.CompilerParams(collective_id=1, has_side_effects=True),
        name="small_gather",
    )(x.reshape(1, 1, width))


def small_scatter_body(count, seq_n, v_ref, out_ref, land, send_sem, recv_sem):
    me = lax.axis_index("dp") * seq_n + lax.axis_index("seq")
    greet_all(me, count, seq_n)

    def copy_to(i):
        peer = (me + i) % count
        return pltpu.make_async_remote_copy(
            src_ref=v_ref.at[pl.ds(peer, 1)],
            dst_ref=land.at[pl.ds(i, 1)],
            send_sem=send_sem.at[i],
            recv_sem=recv_sem.at[i],
            device_id=device_of(peer, seq_n),
            device_id_type=pl.DeviceIdType.MESH,
        )

    def begin(i, carry):
        copy_to(i).start()
        return carry

    def finish(i, total):
        copy_to(i).wait()
        return total + land[pl.ds(i, 1)]

    lax.fori_loop(1, count, begin, 0)
    out_ref[...] = lax.fori_loop(1, count, finish, v_ref[pl.ds(me, 1)])


def small_scatter(v, count, seq_n):
    width = v.shape[-1]
    return pl.pallas_call(
        functools.partial(small_scatter_body, count, seq_n),
        out_shape=jax.ShapeDtypeStruct((1, 1, width), f32),
        in_specs=[WHOLE],
        out_specs=WHOLE,
        scratch_shapes=[
            pltpu.VMEM((count, 1, width), f32),
            pltpu.SemaphoreType.DMA((count,)),
            pltpu.SemaphoreType.DMA((count,)),
        ],
        compiler_params=pltpu.CompilerParams(collective_id=2, has_side_effects=True),
        name="small_scatter",
    )(v.reshape(count, 1, width))


def swap(x, bit):
    return lax.ppermute(x, "seq", [(i, i ^ bit) for i in range(4)])


def spread(own):
    far = swap(own, 2)
    return own, swap(own, 1), far, swap(far, 1)


def reduce_rows(near, far):
    got = swap(near, 1)
    across = swap(far[0] + got[1], 2)
    return got, across


def pick(step, refs, dest):
    for k, ref in enumerate(refs):

        @pl.when(step == k)
        def _(ref=ref):
            dest[...] = ref[...]


ORDER = (1, 3, 2, 0)


def rel_of(t):
    return jnp.where(t == 0, 1, jnp.where(t == 1, 3, jnp.where(t == 2, 2, 0)))


def qkv_body(scal, x0, x1, x2, x3, w, gain, shift, bias, h1, qkv, rows):
    pick(pl.program_id(0), (x0, x1, x2, x3), rows)
    unit, _ = normalize(rows[...].astype(f32))
    low = (unit * gain[...] + shift[...]).astype(bf16)
    h1[...] = low
    qkv[...] = (mm(low, w[...]) + bias[...]).astype(bf16)


def qkv_call(scal, pieces, w, gain, shift, bias):
    rows, width = pieces[0].shape
    cols = w.shape[1]
    out = lambda r, sc: (lax.bitwise_xor(sc[0], r), 0)
    return pl.pallas_call(
        qkv_body,
        out_shape=(
            jax.ShapeDtypeStruct((4 * rows, width), bf16),
            jax.ShapeDtypeStruct((4 * rows, cols), bf16),
        ),
        grid_spec=pltpu.PrefetchScalarGridSpec(
            num_scalar_prefetch=1,
            grid=(4,),
            in_specs=[WHOLE] * 8,
            out_specs=(pl.BlockSpec((rows, width), out), pl.BlockSpec((rows, cols), out)),
            scratch_shapes=[pltpu.VMEM((rows, width), bf16)],
        ),
        compiler_params=params(),
        name="qkv",
    )(scal, *pieces, w, gain, shift, bias)


def make_bias(scal, slopes, pair, bias, keys):
    pos = lax.broadcasted_iota(jnp.int32, (keys, LANES), 0)
    inside = pos < scal[1]
    ramp = pos.astype(f32)
    for h in range(2):
        bias[h] = jnp.where(inside, ramp * slopes[2 * pair + h], NEG)


def head_only(x, h):
    lane = lax.broadcasted_iota(jnp.int32, x.shape, 1)
    return jnp.where((lane >= h * HEAD_DIM) & (lane < (h + 1) * HEAD_DIM), x, jnp.zeros_like(x))


def score_t(k_ref, qm, bias, h, length):
    block = qm.shape[0]
    s = mm_t(k_ref[0:length, :], qm)
    b = bias[h, 0:length, :]
    s = s + jnp.concatenate([b] * (block // LANES), axis=1)
    key = lax.broadcasted_iota(jnp.int32, (block, block), 0)
    query = lax.broadcasted_iota(jnp.int32, (block, block), 1)
    last = jnp.where(key <= query, s[length - block :], NEG)
    if length == block:
        return last
    return jnp.concatenate([s[: length - block], last], axis=0)


def attend_body(scal, q, k, v, slopes, o, lse, bias, vt):
    pair, step = pl.program_id(0), pl.program_id(1)
    block = q.shape[0]
    keys = k.shape[0]

    @pl.when(step == 0)
    def _():
        make_bias(scal, slopes, pair, bias, keys)
        vt[...] = v[...].T

    for c in range(keys // block):

        @pl.when(step == c)
        def _(c=c):
            length = (c + 1) * block
            scaled = q[...] * bf16(HEAD_DIM**-0.5)
            outs, logs = [], []
            for h in range(2):
                s = score_t(k, head_only(scaled, h), bias, h, length)
                top = jnp.max(s, axis=0, keepdims=True)
                e = jnp.exp(s - top)
                total = jnp.sum(e, axis=0, keepdims=True)
                mixed = mm(vt[h * HEAD_DIM : (h + 1) * HEAD_DIM, 0:length], e.astype(bf16))
                outs.append(mixed / total)
                logs.append(top + jnp.log(total))
            o[...] = jnp.concatenate(outs, axis=0).T.astype(bf16)
            lse[0, 0:2, :] = jnp.concatenate(logs, axis=0)


def attend_call(scal, slopes, qkv, block):
    keys, cols = qkv.shape
    width = cols // 3
    pairs = width // LANES
    return pl.pallas_call(
        attend_body,
        out_shape=(
            jax.ShapeDtypeStruct((keys, width), bf16),
            jax.ShapeDtypeStruct((pairs, 8, keys), f32),
        ),
        grid_spec=pltpu.PrefetchScalarGridSpec(
            num_scalar_prefetch=1,
            grid=(pairs, keys // block),
            in_specs=[
                pl.BlockSpec((block, LANES), lambda p, c, sc: (c, p)),
                pl.BlockSpec((keys, LANES), lambda p, c, sc: (0, pairs + p)),
                pl.BlockSpec((keys, LANES), lambda p, c, sc: (0, 2 * pairs + p)),
                SCALAR,
            ],
            out_specs=(
                pl.BlockSpec((block, LANES), lambda p, c, sc: (c, p)),
                pl.BlockSpec((1, 8, block), lambda p, c, sc: (p, 0, c)),
            ),
            scratch_shapes=[
                pltpu.VMEM((2, keys, LANES), f32),
                pltpu.VMEM((LANES, keys), bf16),
            ],
        ),
        compiler_params=params(),
        name="attend",
    )(scal, qkv, qkv, qkv, slopes)


def attend_back_body(scal, q, k, v, o, do, lse, slopes, dq, dk, dv, bias, kt, dk_sum, dv_sum):
    pair, step = pl.program_id(0), pl.program_id(1)
    block = q.shape[0]
    keys = k.shape[0]
    scale = HEAD_DIM**-0.5

    @pl.when(step == 0)
    def _():
        make_bias(scal, slopes, pair, bias, keys)
        kt[...] = k[...].T
        dk_sum[...] = jnp.zeros_like(dk_sum)
        dv_sum[...] = jnp.zeros_like(dv_sum)

    for c in range(keys // block):

        @pl.when(step == c)
        def _(c=c):
            length = (c + 1) * block
            scaled = q[...] * bf16(scale)
            both = (do[...].astype(f32) * o[...].astype(f32)).T
            outs = []
            for h in range(2):
                qm = head_only(scaled, h)
                dom = head_only(do[...], h)
                dot_row = jnp.sum(both[h * HEAD_DIM : (h + 1) * HEAD_DIM], axis=0, keepdims=True)
                p = jnp.exp(score_t(k, qm, bias, h, length) - lse[0, h : h + 1, :])
                dp = mm_t(v[0:length, :], dom)
                ds = (p * (dp - dot_row)).astype(bf16)
                dv_sum[0:length, :] += mm(p.astype(bf16), dom)
                dk_sum[0:length, :] += mm(ds, qm)
                outs.append(mm(kt[h * HEAD_DIM : (h + 1) * HEAD_DIM, 0:length], ds))
            dq[...] = (jnp.concatenate(outs, axis=0).T * scale).astype(bf16)

    @pl.when(step == keys // block - 1)
    def _():
        dk[...] = dk_sum[...].astype(bf16)
        dv[...] = dv_sum[...].astype(bf16)


def attend_back_call(scal, slopes, qkv, o, do, lse, block):
    keys, cols = qkv.shape
    width = cols // 3
    pairs = width // LANES
    some = pl.BlockSpec((block, LANES), lambda p, c, sc: (c, p))
    full = pl.BlockSpec((keys, LANES), lambda p, c, sc: (0, p))
    return pl.pallas_call(
        attend_back_body,
        out_shape=(jax.ShapeDtypeStruct((keys, width), bf16),) * 3,
        grid_spec=pltpu.PrefetchScalarGridSpec(
            num_scalar_prefetch=1,
            grid=(pairs, keys // block),
            in_specs=[
                some,
                pl.BlockSpec((keys, LANES), lambda p, c, sc: (0, pairs + p)),
                pl.BlockSpec((keys, LANES), lambda p, c, sc: (0, 2 * pairs + p)),
                some,
                some,
                pl.BlockSpec((1, 8, block), lambda p, c, sc: (p, 0, c)),
                SCALAR,
            ],
            out_specs=(some, full, full),
            scratch_shapes=[
                pltpu.VMEM((2, keys, LANES), f32),
                pltpu.VMEM((LANES, keys), bf16),
                pltpu.VMEM((keys, LANES), f32),
                pltpu.VMEM((keys, LANES), f32),
            ],
        ),
        compiler_params=params(),
        name="attend_back",
    )(scal, qkv, qkv, qkv, o, do, lse, slopes)


def lay_columns(w_ref, first, dest):
    width = w_ref.shape[2]
    for d in range(w_ref.shape[0]):
        dest[:, d * width : (d + 1) * width] = w_ref[d, first : first + dest.shape[0], :]


def out_body(scal, o, w, near, far, flat, *, first):
    t = pl.program_id(0)

    @pl.when(t == 0)
    def _():
        lay_columns(w, first, flat)

    part = mm(o[...], flat[...]).astype(bf16)

    @pl.when(t < 2)
    def _():
        near[0] = part

    @pl.when(t >= 2)
    def _():
        far[0] = part


def near_map(t, *_):
    return (jnp.minimum(t, 1), 0, 0)


def far_map(t, *_):
    return (jnp.maximum(t - 2, 0), 0, 0)


def out_call(scal, o, w, first):
    keys, inner = o.shape
    rows = keys // 4
    width = w.shape[0] * w.shape[2]
    return pl.pallas_call(
        functools.partial(out_body, first=first),
        out_shape=(jax.ShapeDtypeStruct((2, rows, width), bf16),) * 2,
        grid_spec=pltpu.PrefetchScalarGridSpec(
            num_scalar_prefetch=1,
            grid=(4,),
            in_specs=[
                pl.BlockSpec((rows, inner), lambda t, sc: (lax.bitwise_xor(sc[0], rel_of(t)), 0)),
                WHOLE,
            ],
            out_specs=(
                pl.BlockSpec((1, rows, width), near_map),
                pl.BlockSpec((1, rows, width), far_map),
            ),
            scratch_shapes=[pltpu.VMEM((inner, width), bf16)],
        ),
        compiler_params=params(),
        name="out_proj",
    )(scal, o, w)


def mid_body(x, a, b, c, bias, gain, shift, mid, h2):
    value = x[...].astype(f32) + (
        (a[0].astype(f32) + b[0].astype(f32)) + c[...].astype(f32) + bias[...]
    )
    mid[...] = value
    unit, _ = normalize(value)
    h2[...] = (unit * gain[...] + shift[...]).astype(bf16)


def mid_call(x, a, b, c, bias, gain, shift):
    rows, width = x.shape
    one = pl.BlockSpec((rows // 2, width), lambda i: (i, 0))
    first = pl.BlockSpec((1, rows // 2, width), lambda i: (0, i, 0))
    second = pl.BlockSpec((1, rows // 2, width), lambda i: (1, i, 0))
    row = pl.BlockSpec((1, width), lambda i: (0, 0))
    return pl.pallas_call(
        mid_body,
        out_shape=(
            jax.ShapeDtypeStruct((rows, width), f32),
            jax.ShapeDtypeStruct((rows, width), bf16),
        ),
        grid=(2,),
        in_specs=[one, second, first, one, row, row, row],
        out_specs=(one, one),
        compiler_params=params(),
        name="mid_norm",
    )(x, a, b, c, bias, gain, shift)


def gelu_parts(u):
    root = math.sqrt(2.0 / math.pi)
    sq = u * u
    t = jnp.tanh(root * (u + GELU_COEF * (sq * u)))
    half = 0.5 * (1.0 + t)
    slope = half + 0.5 * u * (1.0 - t * t) * (root * (1.0 + 3.0 * GELU_COEF * sq))
    return u * half, slope


def mlp_body(
    h0, h1, h2, h3, g0, g1, g2, g3, w1, w2, b1,
    y_near, y_far, d_near, d_far, a_all, du_all, h_all, g_all, bias_sum,
    flat, hb, gb,
):
    t = pl.program_id(0)

    @pl.when(t == 0)
    def _():
        lay_columns(w2, 0, flat)
        bias_sum[...] = jnp.zeros_like(bias_sum)

    pick(rel_of(t), (h0, h1, h2, h3), hb)
    pick(rel_of(t), (g0, g1, g2, g3), gb)
    h_all[...] = hb[...]
    g_all[...] = gb[...]
    inner = w1.shape[1]
    chunk = 256
    for c in range(inner // chunk):
        cols = slice(c * chunk, (c + 1) * chunk)
        u = mm(hb[...], w1[:, cols]) + b1[:, cols]
        value, slope = gelu_parts(u)
        a_all[:, cols] = value.astype(bf16)
        du = (mm_t(gb[...], flat[cols, :]) * slope).astype(bf16)
        du_all[:, cols] = du
        bias_sum[:, cols] += jnp.sum(du.astype(f32), axis=0, keepdims=True)
    y = mm(a_all[...], flat[...]).astype(bf16)
    d = mm_t(du_all[...], w1[...]).astype(bf16)

    @pl.when(t < 2)
    def _():
        y_near[0] = y
        d_near[0] = d

    @pl.when(t >= 2)
    def _():
        y_far[0] = y
        d_far[0] = d


def mlp_call(h_pieces, g_pieces, w1, w2, b1):
    rows, width = h_pieces[0].shape
    inner = w1.shape[1]
    pair = jax.ShapeDtypeStruct((2, rows, width), bf16)
    near = pl.BlockSpec((1, rows, width), near_map)
    far = pl.BlockSpec((1, rows, width), far_map)
    block = lambda n: pl.BlockSpec((rows, n), lambda t: (t, 0))
    return pl.pallas_call(
        mlp_body,
        out_shape=(
            pair,
            pair,
            pair,
            pair,
            jax.ShapeDtypeStruct((4 * rows, inner), bf16),
            jax.ShapeDtypeStruct((4 * rows, inner), bf16),
            jax.ShapeDtypeStruct((4 * rows, width), bf16),
            jax.ShapeDtypeStruct((4 * rows, width), bf16),
            jax.ShapeDtypeStruct((1, inner), f32),
        ),
        grid=(4,),
        in_specs=[WHOLE] * 11,
        out_specs=(
            near, far, near, far, block(inner), block(inner), block(width), block(width),
            pl.BlockSpec((1, inner), lambda t: (0, 0)),
        ),
        scratch_shapes=[
            pltpu.VMEM((inner, width), bf16),
            pltpu.VMEM((rows, width), bf16),
            pltpu.VMEM((rows, width), bf16),
        ],
        compiler_params=params(),
        name="mlp",
    )(*h_pieces, *g_pieces, w1, w2, b1)


def outer_body(left, right, out, turned, *, blocks):
    @pl.when(pl.program_id(0) == 0)
    def _():
        turned[...] = left[...].T

    part = mm(turned[...], right[...]).astype(bf16)
    if blocks:
        width = out.shape[2]
        for d in range(out.shape[0]):
            out[d] = part[:, d * width : (d + 1) * width]
    else:
        out[...] = part


def outer_call(left, right, parts, name):
    rows, m = left.shape
    n = right.shape[1]
    step = 256
    if parts > 1:
        width = n // parts
        out_shape = jax.ShapeDtypeStruct((parts, m, width), bf16)
        out_spec = pl.BlockSpec((step // width, m, width), lambda j: (j, 0, 0))
    else:
        out_shape = jax.ShapeDtypeStruct((m, n), bf16)
        out_spec = pl.BlockSpec((m, step), lambda j: (0, j))
    return pl.pallas_call(
        functools.partial(outer_body, blocks=parts > 1),
        out_shape=out_shape,
        grid=(n // step,),
        in_specs=[WHOLE, pl.BlockSpec((rows, step), lambda j: (0, j))],
        out_specs=out_spec,
        scratch_shapes=[pltpu.VMEM((m, rows), bf16)],
        compiler_params=params(),
        name=name,
    )(left, right)


def mid_back_body(mid, a, b, c, g, gain, dmid, dbr, sums):
    @pl.when(pl.program_id(0) == 0)
    def _():
        sums[...] = jnp.zeros_like(sums)

    unit, inv = normalize(mid[...])
    e = (a[0].astype(f32) + b[0].astype(f32)) + c[...].astype(f32)
    grad = g[...].astype(f32)
    value = grad + norm_back(e, gain[...], unit, inv)
    dmid[...] = value
    low = value.astype(bf16)
    dbr[...] = low
    sums[0:1, :] += jnp.sum(e * unit, axis=0, keepdims=True)
    sums[1:2, :] += jnp.sum(e, axis=0, keepdims=True)
    sums[2:3, :] += jnp.sum(low.astype(f32), axis=0, keepdims=True)
    sums[3:4, :] += jnp.sum(grad, axis=0, keepdims=True)


def mid_back_call(mid, a, b, c, g, gain):
    rows, width = mid.shape
    one = pl.BlockSpec((rows // 2, width), lambda i: (i, 0))
    first = pl.BlockSpec((1, rows // 2, width), lambda i: (0, i, 0))
    second = pl.BlockSpec((1, rows // 2, width), lambda i: (1, i, 0))
    row = pl.BlockSpec((1, width), lambda i: (0, 0))
    return pl.pallas_call(
        mid_back_body,
        out_shape=(
            jax.ShapeDtypeStruct((rows, width), f32),
            jax.ShapeDtypeStruct((rows, width), bf16),
            jax.ShapeDtypeStruct((8, width), f32),
        ),
        grid=(2,),
        in_specs=[one, second, first, one, one, row],
        out_specs=(one, one, pl.BlockSpec((8, width), lambda i: (0, 0))),
        compiler_params=params(),
        name="mid_back",
    )(mid, a, b, c, g, gain)


def out_back_body(scal, b0, b1, b2, b3, o, w, do, grad, flat, rows, total, *, first):
    r = pl.program_id(0)

    @pl.when(r == 0)
    def _():
        lay_columns(w, first, flat)
        total[...] = jnp.zeros_like(total)

    pick(r, (b0, b1, b2, b3), rows)
    do[...] = mm_t(rows[...], flat[...]).astype(bf16)
    total[...] += mm(o[...].T, rows[...])

    @pl.when(r == 3)
    def _():
        width = grad.shape[2]
        for d in range(grad.shape[0]):
            grad[d] = total[:, d * width : (d + 1) * width].astype(bf16)


def out_back_call(scal, pieces, o, w, first):
    rows, width = pieces[0].shape
    inner = o.shape[1]
    at = pl.BlockSpec((rows, inner), lambda r, sc: (lax.bitwise_xor(sc[0], r), 0))
    grad = (w.shape[0], inner, w.shape[2])
    return pl.pallas_call(
        functools.partial(out_back_body, first=first),
        out_shape=(jax.ShapeDtypeStruct(o.shape, bf16), jax.ShapeDtypeStruct(grad, bf16)),
        grid_spec=pltpu.PrefetchScalarGridSpec(
            num_scalar_prefetch=1,
            grid=(4,),
            in_specs=[WHOLE] * 4 + [at, WHOLE],
            out_specs=(at, pl.BlockSpec(grad, lambda r, sc: (0, 0, 0))),
            scratch_shapes=[
                pltpu.VMEM((inner, width), bf16),
                pltpu.VMEM((rows, width), bf16),
                pltpu.VMEM((inner, width), f32),
            ],
        ),
        compiler_params=params(),
        name="out_back",
    )(scal, *pieces, o, w)


def qkv_back_body(scal, dq, dk, dv, w, near, far, merged, sums):
    t = pl.program_id(0)

    @pl.when(t == 0)
    def _():
        sums[...] = jnp.zeros_like(sums)

    low = jnp.concatenate([dq[...], dk[...], dv[...]], axis=1)
    merged[...] = low
    part = mm_t(low, w[...]).astype(bf16)
    sums[...] += jnp.sum(low.astype(f32), axis=0, keepdims=True)

    @pl.when(t < 2)
    def _():
        near[0] = part

    @pl.when(t >= 2)
    def _():
        far[0] = part


def qkv_back_call(scal, dq, dk, dv, w):
    keys, inner = dq.shape
    rows = keys // 4
    width = w.shape[0]
    where = lambda t, sc: (lax.bitwise_xor(sc[0], rel_of(t)), 0)
    at = pl.BlockSpec((rows, inner), where)
    return pl.pallas_call(
        qkv_back_body,
        out_shape=(
            jax.ShapeDtypeStruct((2, rows, width), bf16),
            jax.ShapeDtypeStruct((2, rows, width), bf16),
            jax.ShapeDtypeStruct((keys, 3 * inner), bf16),
            jax.ShapeDtypeStruct((1, 3 * inner), f32),
        ),
        grid_spec=pltpu.PrefetchScalarGridSpec(
            num_scalar_prefetch=1,
            grid=(4,),
            in_specs=[at, at, at, WHOLE],
            out_specs=(
                pl.BlockSpec((1, rows, width), near_map),
                pl.BlockSpec((1, rows, width), far_map),
                pl.BlockSpec((rows, 3 * inner), where),
                pl.BlockSpec((1, 3 * inner), lambda t, sc: (0, 0)),
            ),
        ),
        compiler_params=params(),
        name="qkv_back",
    )(scal, dq, dk, dv, w)


def in_back_body(x, a, b, c, dmid, gain, grad, sums):
    @pl.when(pl.program_id(0) == 0)
    def _():
        sums[...] = jnp.zeros_like(sums)

    unit, inv = normalize(x[...].astype(f32))
    e = (a[0].astype(f32) + b[0].astype(f32)) + c[...].astype(f32)
    grad[...] = (dmid[...] + norm_back(e, gain[...], unit, inv)).astype(bf16)
    sums[0:1, :] += jnp.sum(e * unit, axis=0, keepdims=True)
    sums[1:2, :] += jnp.sum(e, axis=0, keepdims=True)


def in_back_call(x, a, b, c, dmid, gain):
    rows, width = x.shape
    one = pl.BlockSpec((rows // 2, width), lambda i: (i, 0))
    first = pl.BlockSpec((1, rows // 2, width), lambda i: (0, i, 0))
    second = pl.BlockSpec((1, rows // 2, width), lambda i: (1, i, 0))
    row = pl.BlockSpec((1, width), lambda i: (0, 0))
    return pl.pallas_call(
        in_back_body,
        out_shape=(
            jax.ShapeDtypeStruct((rows, width), bf16),
            jax.ShapeDtypeStruct((8, width), f32),
        ),
        grid=(2,),
        in_specs=[one, second, first, one, one, row],
        out_specs=(one, pl.BlockSpec((8, width), lambda i: (0, 0))),
        compiler_params=params(),
        name="in_back",
    )(x, a, b, c, dmid, gain)


def after(value, *others):
    return lax.optimization_barrier((value, *others))[0]


def on_device(
    dp_n,
    seq_n,
    tokens,
    lengths,
    cotangent,
    ln1_gain,
    ln1_shift,
    w_qkv,
    b_qv,
    w_out,
    b_out,
    ln2_gain,
    ln2_shift,
    w_fc1,
    b_fc1,
    w_fc2,
    b_fc2,
):
    count = dp_n * seq_n
    rows, width = tokens.shape
    heads = width // HEAD_DIM
    inner = w_out.shape[0]
    ff = w_fc1.shape[1]
    s = lax.axis_index("seq")
    length = lengths[0]

    wq = lax.all_gather(
        jnp.concatenate([w_qkv[:, c, :] for c in range(3)], axis=1), "dp", axis=0, tiled=True
    )
    col = w_fc2.shape[1]
    both = jnp.concatenate([w_fc2, w_out], axis=0)
    if col % LANES == 0:
        parts = dp_n
        w_cols = lax.all_gather(both, "dp", axis=0, tiled=False)
    else:
        parts = 1
        w_cols = lax.all_gather(both, "dp", axis=1, tiled=True)[None]
    w1 = lax.all_gather(w_fc1, "dp", axis=0, tiled=True)

    small = (ln1_gain, ln1_shift, b_qv, b_out, ln2_gain, ln2_shift, b_fc1, b_fc2)
    sizes = [v.shape[0] for v in small]
    ends = [sum(sizes[: i + 1]) for i in range(len(sizes))]
    packed = small_gather(jnp.concatenate([v.astype(f32) for v in small]), count, seq_n)
    packed = packed.reshape(count, ends[-1])
    gain1, shift1, bias_qv, bias_out, gain2, shift2, bias_up, bias_down = (
        packed[:, e - n : e].reshape(1, count * n) for e, n in zip(ends, sizes)
    )

    scal = jnp.stack([s.astype(jnp.int32), length])
    slopes = 2.0 ** (-8.0 * (jnp.arange(heads, dtype=jnp.int32) + 1).astype(f32) / heads)
    slopes = lax.dynamic_slice(slopes, (s * (heads // seq_n),), (heads // seq_n,))
    own_bias = lambda v, n: lax.dynamic_slice(v, (0, s * n), (1, n))
    qkv_bias = jnp.concatenate(
        [
            own_bias(bias_qv[:, :width], inner),
            jnp.zeros((1, inner), f32),
            own_bias(bias_qv[:, width:], inner),
        ],
        axis=1,
    )

    x_pieces = spread(tokens)
    valid = s * rows + jnp.arange(rows, dtype=jnp.int32) < length
    grad_low = jnp.where(valid[:, None], cotangent, jnp.zeros_like(cotangent))
    g_pieces = spread(after(grad_low, x_pieces[3]))

    block = 256
    h1, qkv = qkv_call(scal, x_pieces, wq, gain1, shift1, qkv_bias)
    o, lse = attend_call(scal, slopes, qkv, block)
    near, far = out_call(scal, o, w_cols, ff)
    got, across = reduce_rows(near, far)
    mid, h2 = mid_call(tokens, far, got, across, bias_out, gain2, shift2)
    h_pieces = spread(h2)
    y_near, y_far, d_near, d_far, a_all, du_all, h_all, g_all, up_sum = mlp_call(
        h_pieces, g_pieces, w1, w_cols, own_bias(bias_up, ff)
    )
    got, across = reduce_rows(d_near, d_far)
    grad_down = outer_call(a_all, g_all, parts, "grad_fc2")
    grad_up = outer_call(h_all, du_all, 1, "grad_fc1")
    dmid, dbr, mid_sums = mid_back_call(mid, d_far, got, across, grad_low, gain2)
    b_pieces = spread(dbr)

    y_near = after(y_near, b_pieces[3])
    got, across = reduce_rows(y_near, y_far)
    output = (
        mid + ((y_far[1].astype(f32) + got[0].astype(f32)) + across.astype(f32) + bias_down)
    ).astype(bf16)

    do, grad_out = out_back_call(scal, b_pieces, o, w_cols, ff)
    dq, dk, dv = attend_back_call(scal, slopes, qkv, o, do, lse, block)
    near, far, merged, qkv_sums = qkv_back_call(scal, dq, dk, dv, wq)
    got, across = reduce_rows(near, far)
    grad_qkv = outer_call(h1, merged, 1, "grad_qkv")
    grad_tokens, in_sums = in_back_call(tokens, far, got, across, dmid, gain1)

    def shared(part):
        if parts > 1:
            return lax.psum_scatter(part, "dp", scatter_dimension=0, tiled=False).astype(f32)
        return lax.psum_scatter(part, "dp", scatter_dimension=1, tiled=True).astype(f32)

    grad_down = shared(grad_down if parts > 1 else grad_down)
    grad_up = lax.psum_scatter(grad_up, "dp", scatter_dimension=0, tiled=True).astype(f32)
    grad_out = shared(grad_out if parts > 1 else grad_out[0])
    grad_qkv = lax.psum_scatter(grad_qkv, "dp", scatter_dimension=0, tiled=True)
    grad_qkv = grad_qkv.astype(f32).reshape(w_qkv.shape)

    def own_slot(v, total):
        return lax.dynamic_update_slice(jnp.zeros((1, total), f32), v, (0, s * v.shape[1]))

    sums = (
        in_sums[0:1],
        in_sums[1:2],
        jnp.concatenate(
            [own_slot(qkv_sums[:, :inner], width), own_slot(qkv_sums[:, 2 * inner :], width)], axis=1
        ),
        mid_sums[2:3],
        mid_sums[0:1],
        mid_sums[1:2],
        own_slot(up_sum, seq_n * ff),
        mid_sums[3:4],
    )
    grads = jnp.concatenate([v.reshape(count, n) for v, n in zip(sums, sizes)], axis=1)
    grads = small_scatter(grads, count, seq_n).reshape(ends[-1])
    g_gain1, g_shift1, g_qv, g_bout, g_gain2, g_shift2, g_up, g_down = (
        grads[e - n : e] for e, n in zip(ends, sizes)
    )
    return (
        output,
        grad_tokens,
        g_gain1,
        g_shift1,
        grad_qkv,
        g_qv,
        grad_out,
        g_bout,
        g_gain2,
        g_shift2,
        grad_up,
        g_up,
        grad_down,
        g_down,
    )


def solution(mesh):
    rows = P(("dp", "seq"), None)
    vec = P(("dp", "seq"))
    merged = P("dp", None, "seq")
    return jax.shard_map(
        functools.partial(on_device, mesh.shape["dp"], mesh.shape["seq"]),
        mesh=mesh,
        in_specs=(
            rows, P("dp"), rows, vec, vec, merged, vec, P("seq", "dp"), vec, vec, vec,
            P("dp", "seq"), vec, P("seq", "dp"), vec,
        ),
        out_specs=(
            rows, rows, vec, vec, merged, vec, P("seq", "dp"), vec, vec, vec,
            P("dp", "seq"), vec, P("seq", "dp"), vec,
        ),
        check_vma=False,
    )
```

time: 1210 us -> 498 us (0.41)
  waiting for transfers between devices: 721 us -> 264 us
  matrix products: 208 us -> 0 us
  Pallas kernels: 0 us -> 166 us
  blocking collectives: 151 us -> 0 us
  other arithmetic: 55.8 us -> 17.5 us
  local copies, waits for them, and re-layouts: 45.2 us -> 19.9 us
  starting transfers between devices: 1.23 us -> 14.9 us
    reduce_scatter x10 -> x4, waiting for transfers between devices: 528 us -> 131 us  [the longest x2 91.4 us: shared(): lax.psum_scatter(part, 'dp', scatter_dimension=0, tiled=False).astype(f32)]
    dot_general x68 -> x0, matrix products: 208 us -> none  [the longest x16 40.1 us: scores_of(): jnp.einsum('hqd,hkd->hqk', query_pair, key_pair, preferred_element_type=f32)]
    pallas_call x0 -> x15, Pallas kernels: none -> 166 us  [the longest x1 26.1 us: mlp_call(): pl.pallas_call(mlp_body, out_shape=(pair, pair, pair, pair, jax.ShapeDtyp...]
    all_gather x9 -> x3, waiting for transfers between devices: 191 us -> 45.6 us  [the longest x1 26.1 us: on_device(): w_cols = lax.all_gather(both, 'dp', axis=0, tiled=False)]
    ppermute x0 -> x20, waiting for transfers between devices: none -> 87.4 us  [swap(): return lax.ppermute(x, 'seq', [(i, i ^ bit) for i in range(4)])]
    unnamed x2 -> x0, blocking collectives: 80.3 us -> none
    all_gather x2 -> x0, blocking collectives: 71.1 us -> none  [the longest x1 39.8 us: on_device(): lax.all_gather(b_fc1, ('dp', 'seq'), axis=0, tiled=True)]
    convert_element_type x37 -> x4, other arithmetic: 26.2 us -> 7.87 us  [the longest x2 3.28 us: shared(): lax.psum_scatter(part, 'dp', scatter_dimension=0, tiled=False).astype(f32)]
  transfers between devices with their start and end apart: 19 -> 27, of which waited for: 16 -> 13; matrix products, arithmetic and copies ran while one was open for 15% -> 6% of each run, Pallas kernels for 0% -> 25%
where the time goes in v1:
time: 498 us; the launch traced here: 497 us
  waiting for transfers between devices  264 us (53%)
  Pallas kernels  166 us (33%)
  local copies, waits for them, and re-layouts  19.9 us (4%)
  other arithmetic  17.5 us (4%)
  between operations  15.2 us (3%)
  starting transfers between devices  14.9 us (3%)
    reduce_scatter x2, waiting for transfers between devices, shared(): lax.psum_scatter(part, 'dp', scatter_dimension=0, tiled=False).astype(f32)  91.4 us
    ppermute x20, waiting for transfers between devices, swap(): return lax.ppermute(x, 'seq', [(i, i ^ bit) for i in range(4)])  87.4 us
    reduce_scatter x1, waiting for transfers between devices, on_device(): grad_qkv = lax.psum_scatter(grad_qkv, 'dp', scatter_dimension=0, tiled=True)  39.2 us
    all_gather x1, waiting for transfers between devices, on_device(): w_cols = lax.all_gather(both, 'dp', axis=0, tiled=False)  26.1 us
    pallas_call x1, Pallas kernels, mlp_call(): pl.pallas_call(mlp_body, out_shape=(pair, pair, pair, pair, jax.ShapeDtyp...  26.1 us
    pallas_call x3, Pallas kernels, outer_call(): pl.pallas_call(functools.partial(outer_body, blocks=parts > 1), out_shape...  23.7 us
    pallas_call x1, Pallas kernels, attend_back_call(): pl.pallas_call(attend_back_body, out_shape=(jax.ShapeDtypeStruct((keys, w...  21.5 us
    pallas_call x1, Pallas kernels, attend_call(): pl.pallas_call(attend_body, out_shape=(jax.ShapeDtypeStruct((keys, width)...  20.7 us
  transfers between devices with their start and end apart: 27, of which 13 were waited for; matrix products, arithmetic and copies ran while one was open for 6% of the time, Pallas kernels for 25%

profile of v1, /device:TPU:0, one launch (start us, length us, event | category | flops | bytes accessed | tf_op | source)
XLA Modules:
  0.0 497.0 jit_solution(13153505235587211188)
XLA Ops:
  7.3 1.0 slice_bitcast_fusion.2
  8.3 0.7 pad_maximum_fusion.1
  9.1 1.7 pad_maximum_fusion
  10.9 3.1 collective-permute-start.1
  14.7 18.5 %small_gather.1 = f32[32,1,384]{2,1,0:T(1,128)} custom-call(f32[1,1,384]{2,1,0:T(1,128)} %reshape.139.x_ref), custom_call_target="tpu_custom_call" | custom-call | tf_op jit(solution)/shard_map/small_gather/pallas_call | solution.py:99
  33.2 0.8 copy.34
  35.0 0.7 reshape.120.gain
  35.7 0.7 reshape.121.shift
  36.5 0.6 dynamic_slice.14.slopes
  38.2 19.5 %all-gather.5.cloned.1.call-done.w = bf16[1024,768]{1,0:T(8,128)(2,1)} async-done(((bf16[128,768]{1,0:T(8,128)(2,1)}), bf16[1024,768]{1,0:T(8,128)(2,1)}) %all-gather.5.cloned.1.call-update) | async-done | bytes 1572880 | tf_op jit(solution)/shard_map/all_gather | solution.py:779
  57.7 8.7 %qkv.1 = (bf16[1536,1024]{1,0:T(8,128)(2,1)}, bf16[1536,768]{1,0:T(8,128)(2,1)}) custom-call(s32[2]{0:T(128)} %pad_add_fusion.scal, bf16[384,1024]{1,0:T(8,128)(2,1)} %x.3, bf16[384,1024]{1,0:T(8,128)(2,1)} %copy-done.10, bf16[384,1024]{1,0:T(8,128)(2,1)} %copy-done.9, bf16[384,1024]{1,0:T(8,128)(2,1)} %copy-done.12, ...), custom_call_target="tpu_custom_call" | custom-call | tf_op jit(solution)/shard_map/qkv/pallas_call | solution.py:196
  66.5 20.7 %attend.1 = (bf16[1536,256]{1,0:T(8,128)(2,1)}, f32[2,8,1536]{2,1,0:T(8,128)}) custom-call(s32[2]{0:T(128)} %pad_add_fusion.scal, bf16[1536,768]{1,0:T(8,128)(2,1)} %get-tuple-element.47.q.k.v, bf16[1536,768]{1,0:T(8,128)(2,1)} %get-tuple-element.47.q.k.v, bf16[1536,768]{1,0:T(8,128)(2,1)} %get-tuple-element.47.q.k.v, f32[4]{0:T(128)} %dynamic_slice.14.slopes), custom_call_target="tpu_custom_call" | custom-call | tf_op jit(solution)/shard_map/attend/pallas_call | solution.py:273
  87.2 26.1 %all-gather.9.cloned.1.call-done = bf16[10240,128]{1,0:T(8,128)(2,1)} async-done(((bf16[1280,128]{1,0:T(8,128)(2,1)}), bf16[10240,128]{1,0:T(8,128)(2,1)}) %all-gather.9.cloned.1.call-update) | async-done | bytes 2621456 | tf_op jit(solution)/shard_map/all_gather | solution.py:786
  113.3 6.7 %out_proj.1 = (bf16[2,384,1024]{2,1,0:T(8,128)(2,1)}, bf16[2,384,1024]{2,1,0:T(8,128)(2,1)}) custom-call(s32[2]{0:T(128)} %pad_add_fusion.scal, bf16[1536,256]{1,0:T(8,128)(2,1)} %get-tuple-element.48.o, bf16[8,1280,128]{2,1,0:T(8,128)(2,1)} %bitcast.54), custom_call_target="tpu_custom_call" | custom-call | tf_op jit(solution)/shard_map/out_proj/pallas_call | solution.py:411
  120.2 3.4 collective-permute-done.3.b
  123.6 2.6 fusion.6
  126.2 1.5 collective-permute-start.4
  127.7 0.7 reshape.123.bias
  128.4 0.7 reshape.124.gain
  129.0 0.7 reshape.125.shift
  129.9 0.6 collective-permute-start.9
  130.5 16.5 %collective-permute-done.4.c = bf16[384,1024]{1,0:T(8,128)(2,1)} collective-permute-done((bf16[384,1024]{1,0:T(8,128)(2,1)}, bf16[384,1024]{1,0:T(8,128)(2,1)}, u32[]{:S(2)}, u32[]{:S(2)}) %collective-permute-start.4) | collective-permute-done | bytes 786464 | tf_op jit(solution)/shard_map/ppermute | solution.py:155
  147.0 3.1 mid_norm.1
  150.1 1.5 collective-permute-start.6
  151.6 12.1 %collective-permute-done.9.g2 = bf16[384,1024]{1,0:T(8,128)(2,1)S(1)} collective-permute-done((bf16[384,1024]{1,0:T(8,128)(2,1)S(1)}, bf16[384,1024]{1,0:T(8,128)(2,1)S(1)}, u32[]{:S(2)}, u32[]{:S(2)}) %collective-permute-start.9) | collective-permute-done | bytes 786464 | tf_op jit(solution)/shard_map/ppermute | solution.py:155
  164.2 15.5 %collective-permute-done.6.h2 = bf16[384,1024]{1,0:T(8,128)(2,1)S(1)} collective-permute-done((bf16[384,1024]{1,0:T(8,128)(2,1)}, bf16[384,1024]{1,0:T(8,128)(2,1)S(1)}, u32[]{:S(2)}, u32[]{:S(2)}) %collective-permute-start.6) | collective-permute-done | bytes 786464 | tf_op jit(solution)/shard_map/ppermute | solution.py:155
  179.8 0.7 constant_dynamic-slice_fusion.b1
  180.5 1.6 collective-permute-done.7.h3
  182.2 26.1 %mlp.1 = (bf16[2,384,1024]{2,1,0:T(8,128)(2,1)}, bf16[2,384,1024]{2,1,0:T(8,128)(2,1)}, bf16[2,384,1024]{2,1,0:T(8,128)(2,1)}, bf16[2,384,1024]{2,1,0:T(8,128)(2...) custom-call(bf16[384,1024]{1,0:T(8,128)(2,1)} %get-tuple-element.52., ...), custom_call_target="tpu_custom_call" | custom-call | tf_op jit(solution)/shard_map/mlp/pallas_call | solution.py:517
  208.3 8.2 %grad_fc1.1 = bf16[1024,1024]{1,0:T(8,128)(2,1)} custom-call(bf16[1536,1024]{1,0:T(8,128)(2,1)} %get-tuple-element.76.left, bf16[1536,1024]{1,0:T(8,128)(2,1)} %get-tuple-element.77.right), custom_call_target="tpu_custom_call" | custom-call | tf_op jit(solution)/shard_map/grad_fc1/pallas_call | solution.py:571
  216.8 8.2 %grad_fc2.1 = bf16[8,1024,128]{2,1,0:T(8,128)(2,1)} custom-call(bf16[1536,1024]{1,0:T(8,128)(2,1)} %get-tuple-element.78.left, bf16[1536,1024]{1,0:T(8,128)(2,1)} %get-tuple-element.79.right), custom_call_target="tpu_custom_call" | custom-call | tf_op jit(solution)/shard_map/grad_fc2/pallas_call | solution.py:571
  225.0 1.9 copy-done.5
  227.0 1.6 collective-permute-start.12
  228.6 18.3 %collective-permute-done.12.c = bf16[384,1024]{1,0:T(8,128)(2,1)S(1)} collective-permute-done((bf16[384,1024]{1,0:T(8,128)(2,1)S(1)}, bf16[384,1024]{1,0:T(8,128)(2,1)S(1)}, u32[]{:S(2)}, u32[]{:S(2)}) %collective-permute-start.12) | collective-permute-done | bytes 786464 | tf_op jit(solution)/shard_map/ppermute | solution.py:155
  246.9 0.9 copy-done.18
  247.8 4.5 mid_back.1
  252.3 1.6 collective-permute-start.13
  253.8 17.8 %collective-permute-done.13.b2 = bf16[384,1024]{1,0:T(8,128)(2,1)S(1)} collective-permute-done((bf16[384,1024]{1,0:T(8,128)(2,1)}, bf16[384,1024]{1,0:T(8,128)(2,1)S(1)}, u32[]{:S(2)}, u32[]{:S(2)}) %collective-permute-start.13) | collective-permute-done | bytes 786464 | tf_op jit(solution)/shard_map/ppermute | solution.py:155
  271.6 2.3 collective-permute-done.14.b3
  273.9 1.0 copy-done.19
  274.9 8.0 %out_back.1 = (bf16[1536,256]{1,0:T(8,128)(2,1)}, bf16[8,256,128]{2,1,0:T(8,128)(2,1)}) custom-call(s32[2]{0:T(128)} %pad_add_fusion.scal, bf16[384,1024]{1,0:T(8,128)(2,1)} %get-tuple-element.58.b0, bf16[384,1024]{1,0:T(8,128)(2,1)} %copy-done.17, bf16[384,1024]{1,0:T(8,128)(2,1)} %copy-done.16, bf16[384,1024]{1,0:T(8,128)(2,1)} %copy-done.19, ...), custom_call_target="tpu_custom_call" | custom-call | tf_op jit(solution)/shard_map/out_back/pallas_call | solution.py:646
  283.2 21.5 %attend_back.1 = (bf16[1536,256]{1,0:T(8,128)(2,1)}, bf16[1536,256]{1,0:T(8,128)(2,1)}, bf16[1536,256]{1,0:T(8,128)(2,1)}) custom-call(s32[2]{0:T(128)} %pad_add_fusion.scal, bf16[1536,768]{1,0:T(8,128)(2,1)} %get-tuple-element.47.q.k.v, bf16[1536,768]{1,0:T(8,128)(2,1)} %get-tuple-element.47.q.k.v, bf16[1536,768]{1,0:T(8,128)(2,1)} %get-tuple-element.47.q.k.v, ...), custom_call_target="tpu_custom_call" | custom-call | tf_op jit(solution)/shard_map/attend_back/pallas_call | solution.py:347
  304.7 8.2 %qkv_back.1 = (bf16[2,384,1024]{2,1,0:T(8,128)(2,1)}, bf16[2,384,1024]{2,1,0:T(8,128)(2,1)}, bf16[1536,768]{1,0:T(8,128)(2,1)}, f32[1,768]{1,0:T(1,128)}) custom-call(s32[2]{0:T(128)} %pad_add_fusion.scal, bf16[1536,256]{1,0:T(8,128)(2,1)} %get-tuple-element.62.dq, bf16[1536,256]{1,0:T(8,128)(2,1)} %get-tuple-element.63.dk, ...), custom_call_target="tpu_custom_call" | custom-call | tf_op jit(solution)/shard_map/qkv_back/pallas_call | solution.py:692
  313.1 7.3 %grad_qkv.1 = bf16[1024,768]{1,0:T(8,128)(2,1)} custom-call(bf16[1536,1024]{1,0:T(8,128)(2,1)} %get-tuple-element.73.left, bf16[1536,768]{1,0:T(8,128)(2,1)} %get-tuple-element.74.right), custom_call_target="tpu_custom_call" | custom-call | tf_op jit(solution)/shard_map/grad_qkv/pallas_call | solution.py:571
  321.8 1.1 fusion.3
  322.9 1.4 collective-permute-start.19
  324.4 1.8 convert_element_type.48
  326.2 28.2 %reduce-scatter.11.cloned.1.call-done = bf16[1,1024,128]{2,1,0:T(8,128)(2,1)} async-done(((bf16[8,1024,128]{2,1,0:T(8,128)(2,1)}), bf16[1,1024,128]{2,1,0:T(8,128)(2,1)}) %reduce-scatter.11.cloned.1.call-update) | async-done | bytes 262160 | tf_op jit(solution)/shard_map/reduce_scatter | solution.py:850
  354.5 1.8 bitcast_convert_fusion
  356.3 63.1 %reduce-scatter.7.cloned.1.call-done = bf16[1,256,128]{2,1,0:T(8,128)(2,1)} async-done(((bf16[8,256,128]{2,1,0:T(8,128)(2,1)}), bf16[1,256,128]{2,1,0:T(8,128)(2,1)}) %reduce-scatter.7.cloned.1.call-update) | async-done | bytes 65552 | tf_op jit(solution)/shard_map/reduce_scatter | solution.py:850
  419.4 1.5 bitcast_convert_fusion.1
  420.9 2.1 fusion.4
  423.0 1.5 collective-permute-start.16
  424.5 4.0 in_back.1
  428.5 0.9 slice_reduce_fusion.4
  429.6 0.7 reshape.135.v_ref
  430.2 12.1 %small_scatter.1 = f32[1,1,384]{2,1,0:T(1,128)} custom-call(f32[32,1,384]{2,1,0:T(1,128)} %reshape.135.v_ref), custom_call_target="tpu_custom_call" | custom-call | tf_op jit(solution)/shard_map/small_scatter/pallas_call | solution.py:139
  442.4 1.3 slice_bitcast_fusion.8
  443.6 1.2 slice_bitcast_fusion.4
  444.8 1.4 slice_bitcast_fusion.3
  446.2 2.8 fusion.2
  449.0 39.2 %reduce-scatter.5.cloned.1.call-done = bf16[128,768]{1,0:T(8,128)(2,1)} async-done(((bf16[1024,768]{1,0:T(8,128)(2,1)}), bf16[128,768]{1,0:T(8,128)(2,1)}) %reduce-scatter.5.cloned.1.call-update) | async-done | bytes 196624 | tf_op jit(solution)/shard_map/reduce_scatter | solution.py:856
  488.2 1.1 copy.30
  489.2 0.9 copy.31
  (132 shorter events, 6.1 us)
Async XLA Ops:
  7.2 3.7 copy-start.1
  7.2 6.8 %copy-start.23 = (bf16[32]{0:T(256)(128)(2,1)S(1)}, bf16[32]{0:T(256)(128)(2,1)}, u32[]{:S(2)}) copy-start(bf16[32]{0:T(256)(128)(2,1)} %param.18) | copy-start | bytes 196
  7.2 6.8 %copy-start.24 = (bf16[32]{0:T(256)(128)(2,1)S(1)}, bf16[32]{0:T(256)(128)(2,1)}, u32[]{:S(2)}) copy-start(bf16[32]{0:T(256)(128)(2,1)} %param.19) | copy-start | bytes 196
  7.2 6.8 %copy-start.25 = (bf16[64]{0:T(256)(128)(2,1)S(1)}, bf16[64]{0:T(256)(128)(2,1)}, u32[]{:S(2)}) copy-start(bf16[64]{0:T(256)(128)(2,1)} %param.21) | copy-start | bytes 388
  7.2 6.8 %copy-start.26 = (bf16[32]{0:T(256)(128)(2,1)S(1)}, bf16[32]{0:T(256)(128)(2,1)}, u32[]{:S(2)}) copy-start(bf16[32]{0:T(256)(128)(2,1)} %param.23) | copy-start | bytes 196
  7.2 6.8 %copy-start.27 = (bf16[32]{0:T(256)(128)(2,1)S(1)}, bf16[32]{0:T(256)(128)(2,1)}, u32[]{:S(2)}) copy-start(bf16[32]{0:T(256)(128)(2,1)} %param.24) | copy-start | bytes 196
  7.2 6.8 %copy-start.28 = (bf16[32]{0:T(256)(128)(2,1)S(1)}, bf16[32]{0:T(256)(128)(2,1)}, u32[]{:S(2)}) copy-start(bf16[32]{0:T(256)(128)(2,1)} %param.25) | copy-start | bytes 196
  7.3 6.8 %copy-start.29 = (bf16[128]{0:T(256)(128)(2,1)S(1)}, bf16[128]{0:T(256)(128)(2,1)}, u32[]{:S(2)}) copy-start(bf16[128]{0:T(256)(128)(2,1)} %param.27) | copy-start | bytes 772
  7.3 6.8 %copy-start.30 = (bf16[32]{0:T(256)(128)(2,1)S(1)}, bf16[32]{0:T(256)(128)(2,1)}, u32[]{:S(2)}) copy-start(bf16[32]{0:T(256)(128)(2,1)} %param.29) | copy-start | bytes 196
  7.3 50.4 %all-gather.5.cloned.1.call-start = ((), (), s32[]{:S(2)}) async-start(), calls=%async_computation.4 | async-start | bytes 1769472 | tf_op jit(solution)/shard_map/all_gather | solution.py:779
  9.0 104.2 %all-gather.9.cloned.1.call-start = ((), (), s32[]{:S(2)}) async-start(), calls=%async_computation.10 | async-start | bytes 2949120 | tf_op jit(solution)/shard_map/all_gather | solution.py:786
  10.8 169.7 %all-gather.7.cloned.1.call-start = ((), (), s32[]{:S(2)}) async-start(), calls=%async_computation.5 | async-start | bytes 2359296 | tf_op jit(solution)/shard_map/all_gather | solution.py:790
  10.9 23.1 %collective-permute-start.1 = (bf16[384,1024]{1,0:T(8,128)(2,1)S(1)}, bf16[384,1024]{1,0:T(8,128)(2,1)S(1)}, u32[]{:S(2)}, u32[]{:S(2)}) collective-permute-start(bf16[384,1024]{1,0:T(8,128)(2,1)S(1)} %copy-done.1), channel_id=1, source_target_pairs={{0,2},{1,3},{2,0},{3,1},{4,6},{5,7},{6,4},{7,5},{8,10},{9,11},{10,... | collective-permute-start | bytes 2359304 | tf_op jit(solution)/shard_map/ppermute | solution.py:155
  14.0 24.3 %collective-permute-start = (bf16[384,1024]{1,0:T(8,128)(2,1)S(1)}, bf16[384,1024]{1,0:T(8,128)(2,1)S(1)}, u32[]{:S(2)}, u32[]{:S(2)}) collective-permute-start(bf16[384,1024]{1,0:T(8,128)(2,1)S(1)} %copy-done.1), channel_id=1, source_target_pairs={{0,1},{1,0},{2,3},{3,2},{4,5},{5,4},{6,7},{7,6},{8,9},{9,8},{10,11... | collective-permute-start | bytes 2359304 | tf_op jit(solution)/shard_map/ppermute | solution.py:155
  34.0 23.7 %copy-start.9 = (bf16[384,1024]{1,0:T(8,128)(2,1)}, bf16[384,1024]{1,0:T(8,128)(2,1)S(1)}, u32[]{:S(2)}) copy-start(bf16[384,1024]{1,0:T(8,128)(2,1)S(1)} %collective-permute-done.1.x2) | copy-start | bytes 2359300
  34.0 4.2 collective-permute-start.2
  38.2 19.5 %copy-start.10 = (bf16[384,1024]{1,0:T(8,128)(2,1)}, bf16[384,1024]{1,0:T(8,128)(2,1)S(1)}, u32[]{:S(2)}) copy-start(bf16[384,1024]{1,0:T(8,128)(2,1)S(1)} %collective-permute-done.x1) | copy-start | bytes 2359300
  38.2 19.5 %copy-start.12 = (bf16[384,1024]{1,0:T(8,128)(2,1)}, bf16[384,1024]{1,0:T(8,128)(2,1)S(1)}, u32[]{:S(2)}) copy-start(bf16[384,1024]{1,0:T(8,128)(2,1)S(1)} %collective-permute-done.2.x3) | copy-start | bytes 2359300
  120.0 9.8 %copy-start.15 = (bf16[384,1024]{1,0:T(8,128)(2,1)S(1)}, bf16[384,1024]{1,0:T(8,128)(2,1)}, u32[]{:S(2)}) copy-start(bf16[384,1024]{1,0:T(8,128)(2,1)} %param.17) | copy-start | bytes 2359300
  120.0 3.6 collective-permute-start.3
  120.0 204.4 %reduce-scatter.9.cloned.1.call-start = ((), (), s32[]{:S(2)}) async-start(), calls=%async_computation.8 | async-start | bytes 2359296 | tf_op jit(solution)/shard_map/reduce_scatter | solution.py:854
  123.6 6.3 %copy-start.6 = (bf16[2,384,1024]{2,1,0:T(8,128)(2,1)}, bf16[2,384,1024]{2,1,0:T(8,128)(2,1)S(1)}, u32[]{:S(2)}) copy-start(bf16[2,384,1024]{2,1,0:T(8,128)(2,1)S(1)} %collective-permute-done.3.b) | copy-start | bytes 4718596
  126.2 20.7 %collective-permute-start.4 = (bf16[384,1024]{1,0:T(8,128)(2,1)}, bf16[384,1024]{1,0:T(8,128)(2,1)}, u32[]{:S(2)}, u32[]{:S(2)}) collective-permute-start(bf16[384,1024]{1,0:T(8,128)(2,1)} %fusion.6), channel_id=1, source_target_pairs={{0,2},{1,3},{2,0},{3,1},{4,6},{5,7},{6,4},{7,5},{8,10},{9,11},{10,... | collective-permute-start | bytes 2359304 | tf_op jit(solution)/shard_map/ppermute | solution.py:155
  129.9 21.7 %copy-start = (bf16[384,1024]{1,0:T(8,128)(2,1)}, bf16[384,1024]{1,0:T(8,128)(2,1)S(1)}, u32[]{:S(2)}) copy-start(bf16[384,1024]{1,0:T(8,128)(2,1)S(1)} %broadcast_select_fusion.g0.g) | copy-start | bytes 2359300
  129.9 33.8 %collective-permute-start.9 = (bf16[384,1024]{1,0:T(8,128)(2,1)S(1)}, bf16[384,1024]{1,0:T(8,128)(2,1)S(1)}, u32[]{:S(2)}, u32[]{:S(2)}) collective-permute-start(bf16[384,1024]{1,0:T(8,128)(2,1)S(1)} %broadcast_select_fusion.g0.g), channel_id=1, source_target_pairs={{0,2},{1,3},{2,0},{3,1},{4,6},{5,7},{6,4},{7,5},{8,10},{9,11},{10,... | collective-permute-start | bytes 2359304 | tf_op jit(solution)/shard_map/ppermute | solution.py:155
  150.1 29.6 %collective-permute-start.6 = (bf16[384,1024]{1,0:T(8,128)(2,1)}, bf16[384,1024]{1,0:T(8,128)(2,1)S(1)}, u32[]{:S(2)}, u32[]{:S(2)}) collective-permute-start(bf16[384,1024]{1,0:T(8,128)(2,1)} %get-tuple-element.52.h0), channel_id=1, source_target_pairs={{0,2},{1,3},{2,0},{3,1},{4,6},{5,7},{6,4},{7,5},{8,10},{9,11},{10,... | collective-permute-start | bytes 2359304 | tf_op jit(solution)/shard_map/ppermute | solution.py:155
  151.6 28.9 %collective-permute-start.8 = (bf16[384,1024]{1,0:T(8,128)(2,1)S(1)}, bf16[384,1024]{1,0:T(8,128)(2,1)S(1)}, u32[]{:S(2)}, u32[]{:S(2)}) collective-permute-start(bf16[384,1024]{1,0:T(8,128)(2,1)S(1)} %broadcast_select_fusion.g0.g), channel_id=1, source_target_pairs={{0,1},{1,0},{2,3},{3,2},{4,5},{5,4},{6,7},{7,6},{8,9},{9,8},{10,11... | collective-permute-start | bytes 2359304 | tf_op jit(solution)/shard_map/ppermute | solution.py:155
  163.7 18.4 %copy-start.11 = (bf16[384,1024]{1,0:T(8,128)(2,1)}, bf16[384,1024]{1,0:T(8,128)(2,1)S(1)}, u32[]{:S(2)}) copy-start(bf16[384,1024]{1,0:T(8,128)(2,1)S(1)} %collective-permute-done.9.g2) | copy-start | bytes 2359300
  163.7 16.8 %collective-permute-start.10 = (bf16[384,1024]{1,0:T(8,128)(2,1)S(1)}, bf16[384,1024]{1,0:T(8,128)(2,1)}, u32[]{:S(2)}, u32[]{:S(2)}) collective-permute-start(bf16[384,1024]{1,0:T(8,128)(2,1)S(1)} %collective-permute-done.9.g2), channel_id=1, source_target_pairs={{0,1},{1,0},{2,3},{3,2},{4,5},{5,4},{6,7},{7,6},{8,9},{9,8},{10,11... | collective-permute-start | bytes 2359304 | tf_op jit(solution)/shard_map/ppermute | solution.py:155
  163.7 16.8 %collective-permute-start.5 = (bf16[384,1024]{1,0:T(8,128)(2,1)}, bf16[384,1024]{1,0:T(8,128)(2,1)}, u32[]{:S(2)}, u32[]{:S(2)}) collective-permute-start(bf16[384,1024]{1,0:T(8,128)(2,1)} %get-tuple-element.52.h0), channel_id=1, source_target_pairs={{0,1},{1,0},{2,3},{3,2},{4,5},{5,4},{6,7},{7,6},{8,9},{9,8},{10,11... | collective-permute-start | bytes 2359304 | tf_op jit(solution)/shard_map/ppermute | solution.py:155
  179.7 2.4 copy-start.13
  179.7 2.4 collective-permute-start.7
  180.5 1.7 copy-start.14
  216.5 138.0 %reduce-scatter.11.cloned.1.call-start = ((), (), s32[]{:S(2)}) async-start(), calls=%async_computation.9 | async-start | bytes 2359296 | tf_op jit(solution)/shard_map/reduce_scatter | solution.py:850
  216.6 8.5 %collective-permute-start.11 = (bf16[2,384,1024]{2,1,0:T(8,128)(2,1)}, bf16[2,384,1024]{2,1,0:T(8,128)(2,1)S(1)}, u32[]{:S(2)}, u32[]{:S(2)}) collective-permute-start(bf16[2,384,1024]{2,1,0:T(8,128)(2,1)} %get-tuple-element.57), channel_id=1, source_target_pairs={{0,1},{1,0},{2,3},{3,2},{4,5},{5,4},{6,7},{7,6},{8,9},{9,8},{10,11... | collective-permute-start | bytes 4718600 | tf_op jit(solution)/shard_map/ppermute | solution.py:155
  224.9 2.0 copy-start.5
  225.0 194.4 %reduce-scatter.7.cloned.1.call-start = ((), (), s32[]{:S(2)}) async-start(), calls=%async_computation.7 | async-start | bytes 589824 | tf_op jit(solution)/shard_map/reduce_scatter | solution.py:850
  225.0 21.9 %copy-start.7 = (bf16[2,384,1024]{2,1,0:T(8,128)(2,1)}, bf16[2,384,1024]{2,1,0:T(8,128)(2,1)S(1)}, u32[]{:S(2)}) copy-start(bf16[2,384,1024]{2,1,0:T(8,128)(2,1)S(1)} %collective-permute-done.11.b) | copy-start | bytes 4718596
  227.0 19.9 %collective-permute-start.12 = (bf16[384,1024]{1,0:T(8,128)(2,1)S(1)}, bf16[384,1024]{1,0:T(8,128)(2,1)S(1)}, u32[]{:S(2)}, u32[]{:S(2)}) collective-permute-start(bf16[384,1024]{1,0:T(8,128)(2,1)S(1)} %fusion.5), channel_id=1, source_target_pairs={{0,2},{1,3},{2,0},{3,1},{4,6},{5,7},{6,4},{7,5},{8,10},{9,11},{10,... | collective-permute-start | bytes 2359304 | tf_op jit(solution)/shard_map/ppermute | solution.py:155
  246.9 0.9 copy-start.18
  252.3 19.3 %collective-permute-start.13 = (bf16[384,1024]{1,0:T(8,128)(2,1)}, bf16[384,1024]{1,0:T(8,128)(2,1)S(1)}, u32[]{:S(2)}, u32[]{:S(2)}) collective-permute-start(bf16[384,1024]{1,0:T(8,128)(2,1)} %get-tuple-element.58.b0), channel_id=1, source_target_pairs={{0,2},{1,3},{2,0},{3,1},{4,6},{5,7},{6,4},{7,5},{8,10},{9,11},{10,... | collective-permute-start | bytes 2359304 | tf_op jit(solution)/shard_map/ppermute | solution.py:155
  253.8 17.8 %collective-permute-start.17 = (bf16[384,1024]{1,0:T(8,128)(2,1)}, bf16[384,1024]{1,0:T(8,128)(2,1)S(1)}, u32[]{:S(2)}, u32[]{:S(2)}) collective-permute-start(bf16[384,1024]{1,0:T(8,128)(2,1)} %get-tuple-element.58.b0), channel_id=1, source_target_pairs={{0,1},{1,0},{2,3},{3,2},{4,5},{5,4},{6,7},{7,6},{8,9},{9,8},{10,11... | collective-permute-start | bytes 2359304 | tf_op jit(solution)/shard_map/ppermute | solution.py:155
  271.6 2.3 copy-start.16
  271.6 2.3 collective-permute-start.14
  271.6 2.3 copy-start.17
  273.9 1.0 copy-start.19
  282.9 205.3 %reduce-scatter.5.cloned.1.call-start = ((), (), s32[]{:S(2)}) async-start(), calls=%async_computation.6 | async-start | bytes 1769472 | tf_op jit(solution)/shard_map/reduce_scatter | solution.py:856
  312.9 8.6 %collective-permute-start.18 = (bf16[2,384,1024]{2,1,0:T(8,128)(2,1)}, bf16[2,384,1024]{2,1,0:T(8,128)(2,1)S(1)}, u32[]{:S(2)}, u32[]{:S(2)}) collective-permute-start(bf16[2,384,1024]{2,1,0:T(8,128)(2,1)} %get-tuple-element.66), channel_id=1, source_target_pairs={{0,1},{1,0},{2,3},{3,2},{4,5},{5,4},{6,7},{7,6},{8,9},{9,8},{10,11... | collective-permute-start | bytes 4718600 | tf_op jit(solution)/shard_map/ppermute | solution.py:155
  320.4 0.7 copy-start.21
  320.4 0.8 copy-start.20
  320.4 1.1 copy-start.22
  320.4 1.5 copy-start.3
  320.4 100.5 %collective-permute-start.15 = (bf16[2,384,1024]{2,1,0:T(8,128)(2,1)}, bf16[2,384,1024]{2,1,0:T(8,128)(2,1)}, u32[]{:S(2)}, u32[]{:S(2)}) collective-permute-start(bf16[2,384,1024]{2,1,0:T(8,128)(2,1)} %get-tuple-element.59), channel_id=1, source_target_pairs={{0,1},{1,0},{2,3},{3,2},{4,5},{5,4},{6,7},{7,6},{8,9},{9,8},{10,11... | collective-permute-start | bytes 4718600 | tf_op jit(solution)/shard_map/ppermute | solution.py:155
  321.5 4.8 copy-start.4
  322.9 98.0 %copy-start.8 = (bf16[2,384,1024]{2,1,0:T(8,128)(2,1)S(1)}, bf16[2,384,1024]{2,1,0:T(8,128)(2,1)}, u32[]{:S(2)}) copy-start(bf16[2,384,1024]{2,1,0:T(8,128)(2,1)} %get-tuple-element.54) | copy-start | bytes 4718596
  322.9 101.6 %collective-permute-start.19 = (bf16[384,1024]{1,0:T(8,128)(2,1)}, bf16[384,1024]{1,0:T(8,128)(2,1)}, u32[]{:S(2)}, u32[]{:S(2)}) collective-permute-start(bf16[384,1024]{1,0:T(8,128)(2,1)} %fusion.3), channel_id=1, source_target_pairs={{0,2},{1,3},{2,0},{3,1},{4,6},{5,7},{6,4},{7,5},{8,10},{9,11},{10,... | collective-permute-start | bytes 2359304 | tf_op jit(solution)/shard_map/ppermute | solution.py:155
  423.0 23.2 %collective-permute-start.16 = (bf16[384,1024]{1,0:T(8,128)(2,1)}, bf16[384,1024]{1,0:T(8,128)(2,1)}, u32[]{:S(2)}, u32[]{:S(2)}) collective-permute-start(bf16[384,1024]{1,0:T(8,128)(2,1)} %fusion.4), channel_id=1, source_target_pairs={{0,2},{1,3},{2,0},{3,1},{4,6},{5,7},{6,4},{7,5},{8,10},{9,11},{10,... | collective-permute-start | bytes 2359304 | tf_op jit(solution)/shard_map/ppermute | solution.py:155
  424.5 21.7 %copy-start.2 = (f32[384,1024]{1,0:T(8,128)S(1)}, f32[384,1024]{1,0:T(8,128)}, u32[]{:S(2)}) copy-start(f32[384,1024]{1,0:T(8,128)} %get-tuple-element.51.mid) | copy-start | bytes 4718596
Sparse Core Ops, SparseCore 0:
  10.8 46.8 all-gather.4
  60.5 52.7 all-gather.8
  120.1 47.8 all-gather.6
  216.6 67.1 reduce-scatter.8
  287.2 67.2 reduce-scatter.10
  357.7 61.6 reduce-scatter.6
  422.8 65.3 reduce-scatter.4

commit v2 on v1

--- a/solution.py
+++ b/solution.py
@@ -743,6 +743,309 @@
         compiler_params=params(),
         name="in_back",
     )(x, a, b, c, dmid, gain)
+
+
+def remote(src, dst, send, recv, dp, seq):
+    return pltpu.make_async_remote_copy(
+        src_ref=src,
+        dst_ref=dst,
+        send_sem=send,
+        recv_sem=recv,
+        device_id=(dp, seq),
+        device_id_type=pl.DeviceIdType.MESH,
+    )
+
+
+def greet(peers):
+    barrier = pltpu.get_barrier_semaphore()
+    for dp, seq in peers:
+        pl.semaphore_signal(
+            barrier, inc=1, device_id=(dp, seq), device_id_type=pl.DeviceIdType.MESH
+        )
+    pl.semaphore_wait(barrier, len(peers))
+
+
+class GradSum:
+    def __init__(self, part, acc, landx, landr, landl, sems, dp, seq):
+        self.part, self.acc = part, acc
+        self.landx, self.landr, self.landl = landx, landr, landl
+        self.sems, self.dp, self.seq = sems, dp, seq
+        self.z, self.x = dp // 2, dp % 2
+
+    def cross(self, k):
+        return remote(
+            self.part.at[2 * k + (1 - self.x)],
+            self.landx.at[k],
+            self.sems.at[0, k],
+            self.sems.at[1, k],
+            2 * self.z + (1 - self.x),
+            self.seq,
+        )
+
+    def right(self, b, src):
+        return remote(
+            src.at[b],
+            self.landr.at[b],
+            self.sems.at[2, b],
+            self.sems.at[3, b],
+            2 * ((self.z + 1) % 4) + self.x,
+            self.seq,
+        )
+
+    def left(self, b, src):
+        return remote(
+            src.at[b],
+            self.landl.at[b],
+            self.sems.at[4, b],
+            self.sems.at[5, b],
+            2 * ((self.z + 3) % 4) + self.x,
+            self.seq,
+        )
+
+    def start(self):
+        for k in (3, 0, 2, 1):
+            self.cross(k).start()
+
+    def add_cross(self):
+        for k in (3, 0, 2, 1):
+            self.cross(k).wait_recv()
+            own = self.part[2 * k + self.x].astype(f32)
+            self.acc[k] = (own + self.landx[k].astype(f32)).astype(bf16)
+
+    def stage(self, k):
+        @pl.when(self.z == k)
+        def _():
+            for b in range(3, k, -1):
+                src = self.acc
+                if k > 0:
+                    src = self.landr
+                    self.right(b, src).wait_recv()
+                    src[b] = (src[b].astype(f32) + self.acc[b].astype(f32)).astype(bf16)
+                self.right(b, src).start()
+
+        @pl.when(self.z == 3 - k)
+        def _():
+            for b in range(0, 3 - k):
+                src = self.acc
+                if k > 0:
+                    src = self.landl
+                    self.left(b, src).wait_recv()
+                    src[b] = (src[b].astype(f32) + self.acc[b].astype(f32)).astype(bf16)
+                self.left(b, src).start()
+
+    def finish(self, out):
+        z = self.z
+        out[...] = self.acc[z].astype(f32)
+
+        @pl.when(z > 0)
+        def _():
+            self.right(z, self.landr).wait_recv()
+            out[...] += self.landr[z].astype(f32)
+
+        @pl.when(z < 3)
+        def _():
+            self.left(z, self.landl).wait_recv()
+            out[...] += self.landl[z].astype(f32)
+
+    def drain(self):
+        for k in range(4):
+            self.cross(k).wait_send()
+        for k in range(3):
+
+            @pl.when(self.z == k)
+            def _(k=k):
+                for b in range(3, k, -1):
+                    self.right(b, self.landr).wait_send()
+
+            @pl.when(self.z == 3 - k)
+            def _(k=k):
+                for b in range(0, 3 - k):
+                    self.left(b, self.landl).wait_send()
+
+    @staticmethod
+    def scratch(m, n):
+        return [pltpu.VMEM((4, m, n), bf16)] * 4 + [pltpu.SemaphoreType.DMA((6, 4))]
+
+
+SMALL_ROWS = 16
+
+
+def tail_body(
+    near, far, x, dmid, gain, gq, go, mid_sums, up_sum, qkv_sums,
+    grad, gq_out, go_out, small_out,
+    q_acc, q_x, q_r, q_l, q_sem, o_acc, o_x, o_r, o_l, o_sem,
+    land_c, sum_y, land_y, row_sems, small, small_land, own, seq_land, small_sems, seq_sems,
+):
+    dp, seq = lax.axis_index("dp"), lax.axis_index("seq")
+    mate, across = seq + 1 - 2 * (seq % 2), (seq + 2) % 4
+    far_mate = (mate + 2) % 4
+    greet([((dp + i) % 8, seq) for i in range(1, 8)] + [(dp, mate), (dp, across), (dp, far_mate)])
+    rows, width = x.shape
+
+    cores = [
+        remote(near.at[k], land_c.at[k], row_sems.at[0, k], row_sems.at[1, k], dp, mate)
+        for k in range(2)
+    ]
+    cores[1].start()
+    cores[0].start()
+    sum_q = GradSum(gq, q_acc, q_x, q_r, q_l, q_sem, dp, seq)
+    sum_o = GradSum(go, o_acc, o_x, o_r, o_l, o_sem, dp, seq)
+    sum_o.start()
+    sum_q.start()
+
+    cores[1].wait_recv()
+    chunk = 128
+    for i in range(rows // chunk):
+        at = slice(i * chunk, (i + 1) * chunk)
+        sum_y[at, :] = (far[0, at, :].astype(f32) + land_c[1, at, :].astype(f32)).astype(bf16)
+    over = remote(sum_y, land_y, row_sems.at[0, 2], row_sems.at[1, 2], dp, across)
+    over.start()
+
+    small[...] = jnp.zeros_like(small)
+    for d in range(8):
+        at = slice(d * LANES, (d + 1) * LANES)
+        for row, src in ((4, mid_sums[2:3, at]), (5, mid_sums[0:1, at]), (6, mid_sums[1:2, at])):
+            small[d, row : row + 1, :] = src
+        small[d, 11:12, :] = mid_sums[3:4, at]
+    for i in range(2):
+        at = slice(i * LANES, (i + 1) * LANES)
+        small[pl.ds(seq, 1), 2 + i, :] = qkv_sums[:, at]
+        at = slice((4 + i) * LANES, (5 + i) * LANES)
+        small[pl.ds(4 + seq, 1), 2 + i, :] = qkv_sums[:, at]
+    for i in range(8):
+        at = slice(i * LANES, (i + 1) * LANES)
+        small[pl.ds(2 * seq + i // 4, 1), 7 + i % 4, :] = up_sum[:, at]
+
+    sum_o.add_cross()
+    sum_o.stage(0)
+    sum_o.stage(1)
+    sum_q.add_cross()
+    sum_q.stage(0)
+    sum_o.stage(2)
+
+    cores[0].wait_recv()
+    over.wait_recv()
+    gain_sum = jnp.zeros((1, width), f32)
+    shift_sum = jnp.zeros((1, width), f32)
+    for i in range(rows // chunk):
+        at = slice(i * chunk, (i + 1) * chunk)
+        unit, inv = normalize(x[at, :].astype(f32))
+        e = (far[1, at, :].astype(f32) + land_c[0, at, :].astype(f32)) + land_y[at, :].astype(f32)
+        grad[at, :] = (dmid[at, :] + norm_back(e, gain[...], unit, inv)).astype(bf16)
+        gain_sum += jnp.sum(e * unit, axis=0, keepdims=True)
+        shift_sum += jnp.sum(e, axis=0, keepdims=True)
+    for d in range(8):
+        at = slice(d * LANES, (d + 1) * LANES)
+        small[d, 0:1, :] = gain_sum[:, at]
+        small[d, 1:2, :] = shift_sum[:, at]
+
+    def small_to(i):
+        peer = (dp + i) % 8
+        return remote(
+            small.at[peer], small_land.at[i], small_sems.at[0, i], small_sems.at[1, i], peer, seq
+        )
+
+    for i in range(1, 8):
+        small_to(i).start()
+    sum_q.stage(1)
+    sum_q.stage(2)
+    sum_o.finish(go_out)
+    total = small[dp]
+    for i in range(1, 8):
+        small_to(i).wait_recv()
+        total = total + small_land[i]
+    own[...] = total
+
+    def seq_to(i, peer):
+        return remote(own, seq_land.at[i], seq_sems.at[0, i], seq_sems.at[1, i], dp, peer)
+
+    group = [seq_to(0, mate), seq_to(1, across), seq_to(2, far_mate)]
+    for copy in group:
+        copy.start()
+    sum_q.finish(gq_out)
+    for copy in group:
+        copy.wait_recv()
+    small_out[...] = (own[...] + seq_land[0]) + (seq_land[1] + seq_land[2])
+
+    for copy in group + cores + [over]:
+        copy.wait_send()
+    for i in range(1, 8):
+        small_to(i).wait_send()
+    sum_o.drain()
+    sum_q.drain()
+
+
+def tail_call(near, far, x, dmid, gain, gq, go, mid_sums, up_sum, qkv_sums):
+    rows, width = x.shape
+    sem = pltpu.SemaphoreType.DMA
+    return pl.pallas_call(
+        tail_body,
+        out_shape=(
+            jax.ShapeDtypeStruct((rows, width), bf16),
+            jax.ShapeDtypeStruct(gq.shape[1:], f32),
+            jax.ShapeDtypeStruct(go.shape[1:], f32),
+            jax.ShapeDtypeStruct((SMALL_ROWS, LANES), f32),
+        ),
+        in_specs=[WHOLE] * 10,
+        out_specs=(WHOLE,) * 4,
+        scratch_shapes=GradSum.scratch(*gq.shape[1:])
+        + GradSum.scratch(*go.shape[1:])
+        + [
+            pltpu.VMEM((2, rows, width), bf16),
+            pltpu.VMEM((rows, width), bf16),
+            pltpu.VMEM((rows, width), bf16),
+            sem((2, 3)),
+            pltpu.VMEM((8, SMALL_ROWS, LANES), f32),
+            pltpu.VMEM((8, SMALL_ROWS, LANES), f32),
+            pltpu.VMEM((SMALL_ROWS, LANES), f32),
+            pltpu.VMEM((3, SMALL_ROWS, LANES), f32),
+            sem((2, 8)),
+            sem((2, 3)),
+        ],
+        compiler_params=params(collective_id=3, has_side_effects=True),
+        name="tail",
+    )(near, far, x, dmid, gain, gq, go, mid_sums, up_sum, qkv_sums)
+
+
+def finish_body(
+    scal, grad, gq, go, small,
+    grad_out, gq_out, go_out, gain1, shift1, qv, bout, gain2, shift2, up, down,
+):
+    seq = scal[0]
+    grad_out[...] = grad[...]
+    go_out[...] = go[...]
+    cols = gq_out.shape[2]
+    for c in range(3):
+        gq_out[:, c, :] = gq[:, c * cols : (c + 1) * cols]
+    for ref, row in ((gain1, 0), (shift1, 1), (bout, 4), (gain2, 5), (shift2, 6), (down, 11)):
+        n = ref.shape[1]
+        value = small[row : row + 1, 0:n]
+        for i in range(1, 4):
+            value = jnp.where(seq == i, small[row : row + 1, i * n : (i + 1) * n], value)
+        ref[...] = value
+    value = small[2:3, 0:64]
+    for i in range(1, 4):
+        at = 64 * (i % 2)
+        value = jnp.where(seq == i, small[2 + i // 2 : 3 + i // 2, at : at + 64], value)
+    qv[...] = value
+    up[...] = small[pl.ds(7 + seq, 1), :]
+
+
+def finish_call(scal, grad, gq, go, small):
+    one = lambda n: jax.ShapeDtypeStruct((1, n), f32)
+    return pl.pallas_call(
+        finish_body,
+        out_shape=(
+            jax.ShapeDtypeStruct(grad.shape, bf16),
+            jax.ShapeDtypeStruct((gq.shape[0], 3, gq.shape[1] // 3), f32),
+            jax.ShapeDtypeStruct(go.shape, f32),
+            one(32), one(32), one(64), one(32), one(32), one(32), one(LANES), one(32),
+        ),
+        in_specs=[SCALAR] + [WHOLE] * 4,
+        out_specs=(WHOLE,) * 11,
+        compiler_params=params(),
+        name="finish",
+    )(scal, grad, gq, go, small)
 
 
 def after(value, *others):
@@ -816,9 +1119,10 @@
     grad_low = jnp.where(valid[:, None], cotangent, jnp.zeros_like(cotangent))
     g_pieces = spread(after(grad_low, x_pieces[3]))
 
-    block = 256
+    block = 384
     h1, qkv = qkv_call(scal, x_pieces, wq, gain1, shift1, qkv_bias)
     o, lse = attend_call(scal, slopes, qkv, block)
+    o = after(o, g_pieces[2], g_pieces[3])
     near, far = out_call(scal, o, w_cols, ff)
     got, across = reduce_rows(near, far)
     mid, h2 = mid_call(tokens, far, got, across, bias_out, gain2, shift2)
@@ -841,9 +1145,7 @@
     do, grad_out = out_back_call(scal, b_pieces, o, w_cols, ff)
     dq, dk, dv = attend_back_call(scal, slopes, qkv, o, do, lse, block)
     near, far, merged, qkv_sums = qkv_back_call(scal, dq, dk, dv, wq)
-    got, across = reduce_rows(near, far)
     grad_qkv = outer_call(h1, merged, 1, "grad_qkv")
-    grad_tokens, in_sums = in_back_call(tokens, far, got, across, dmid, gain1)
 
     def shared(part):
         if parts > 1:
@@ -852,6 +1154,22 @@
 
     grad_down = shared(grad_down if parts > 1 else grad_down)
     grad_up = lax.psum_scatter(grad_up, "dp", scatter_dimension=0, tiled=True).astype(f32)
+    if dp_n == 8 and seq_n == 4 and width == 8 * LANES and ff == width and inner == 2 * LANES:
+        tail = tail_call(
+            near, far, tokens, dmid, gain1, grad_qkv.reshape(8, -1, 3 * inner), grad_out,
+            mid_sums, up_sum, qkv_sums,
+        )
+        grad_tokens, grad_qkv, grad_out, *vectors = finish_call(scal, *tail)
+        g_gain1, g_shift1, g_qv, g_bout, g_gain2, g_shift2, g_up, g_down = (
+            v.reshape(n) for v, n in zip(vectors, sizes)
+        )
+        return (
+            output, grad_tokens, g_gain1, g_shift1, grad_qkv, g_qv, grad_out, g_bout,
+            g_gain2, g_shift2, grad_up, g_up, grad_down, g_down,
+        )
+
+    got, across = reduce_rows(near, far)
+    grad_tokens, in_sums = in_back_call(tokens, far, got, across, dmid, gain1)
     grad_out = shared(grad_out if parts > 1 else grad_out[0])
     grad_qkv = lax.psum_scatter(grad_qkv, "dp", scatter_dimension=0, tiled=True)
     grad_qkv = grad_qkv.astype(f32).reshape(w_qkv.shape)

time: 498 us -> 382 us (0.77)
  waiting for transfers between devices: 264 us -> 123 us
  Pallas kernels: 166 us -> 203 us
  local copies, waits for them, and re-layouts: 19.9 us -> 11.6 us
    reduce_scatter x2 -> x1, waiting for transfers between devices: 91.4 us -> 0.01 us  [shared(): lax.psum_scatter(part, 'dp', scatter_dimension=0, tiled=False).astype(f32)]
    pallas_call x2, Pallas kernels: 16.1 us -> 58.3 us  [the longest x1 55.6 us: tail_call(): pl.pallas_call(tail_body, out_shape=(jax.ShapeDtypeStruct((rows, width),...]
    reduce_scatter x1 -> x0, waiting for transfers between devices: 39.2 us -> none  [on_device(): grad_qkv = lax.psum_scatter(grad_qkv, 'dp', scatter_dimension=0, tiled=True)]
    all_gather x1, waiting for transfers between devices: 19.5 us -> 0.01 us  [on_device(): lax.all_gather(jnp.concatenate([w_qkv[:, c, :] for c in range(3)], axis=1...]
    pallas_call x1, Pallas kernels: 20.7 us -> 15.1 us  [attend_call(): pl.pallas_call(attend_body, out_shape=(jax.ShapeDtypeStruct((keys, width)...]
    ppermute x20 -> x18, waiting for transfers between devices: 87.4 us -> 93 us  [swap(): return lax.ppermute(x, 'seq', [(i, i ^ bit) for i in range(4)])]
    ppermute x20 -> x18, starting transfers between devices: 14.2 us -> 13.3 us  [swap(): return lax.ppermute(x, 'seq', [(i, i ^ bit) for i in range(4)])]
  transfers between devices with their start and end apart: 27 -> 23, of which waited for: 13 -> 12; matrix products, arithmetic and copies ran while one was open for 6% -> 5% of each run, Pallas kernels for 25% -> 42%
where the time goes in v2:
time: 382 us; the launch traced here: 381 us
  Pallas kernels  203 us (53%)
  waiting for transfers between devices  123 us (32%)
  other arithmetic  15.1 us (4%)
  between operations  14.7 us (4%)
  starting transfers between devices  13.7 us (4%)
  local copies, waits for them, and re-layouts  11.6 us (3%)
    ppermute x18, waiting for transfers between devices, swap(): return lax.ppermute(x, 'seq', [(i, i ^ bit) for i in range(4)])  93 us
    pallas_call x1, Pallas kernels, tail_call(): pl.pallas_call(tail_body, out_shape=(jax.ShapeDtypeStruct((rows, width),...  55.6 us
    all_gather x1, waiting for transfers between devices, on_device(): w_cols = lax.all_gather(both, 'dp', axis=0, tiled=False)  30.2 us
    pallas_call x1, Pallas kernels, mlp_call(): pl.pallas_call(mlp_body, out_shape=(pair, pair, pair, pair, jax.ShapeDtyp...  26.1 us
    pallas_call x3, Pallas kernels, outer_call(): pl.pallas_call(functools.partial(outer_body, blocks=parts > 1), out_shape...  23.7 us
    pallas_call x1, Pallas kernels, attend_back_call(): pl.pallas_call(attend_back_body, out_shape=(jax.ShapeDtypeStruct((keys, w...  21.4 us
    pallas_call x1, Pallas kernels, small_gather(): pl.pallas_call(functools.partial(small_gather_body, count, seq_n), out_sh...  19 us
    pallas_call x1, Pallas kernels, attend_call(): pl.pallas_call(attend_body, out_shape=(jax.ShapeDtypeStruct((keys, width)...  15.1 us
  transfers between devices with their start and end apart: 23, of which 12 were waited for; matrix products, arithmetic and copies ran while one was open for 5% of the time, Pallas kernels for 42%

profile of v2, /device:TPU:0, one launch (start us, length us, event | category | flops | bytes accessed | tf_op | source)
XLA Modules:
  0.0 381.3 jit_solution(5674333288119972716)
XLA Ops:
  7.2 1.0 slice_bitcast_fusion.2
  8.3 0.7 pad_maximum_fusion.1
  9.1 1.7 pad_maximum_fusion
  10.9 3.1 collective-permute-start.1
  14.0 17.5 %collective-permute-done.1.x2 = bf16[384,1024]{1,0:T(8,128)(2,1)S(1)} collective-permute-done((bf16[384,1024]{1,0:T(8,128)(2,1)S(1)}, bf16[384,1024]{1,0:T(8,128)(2,1)S(1)}, u32[]{:S(2)}, u32[]{:S(2)}) %collective-permute-start.1) | collective-permute-done | bytes 786464 | tf_op jit(solution)/shard_map/ppermute | solution.py:155
  32.2 1.3 broadcast_select_fusion.g0.g
  33.5 0.3 collective-permute-done.2.x3
  33.8 1.7 collective-permute-start.3
  35.7 0.6 reshape.119.x_ref
  36.3 19.0 %small_gather.1 = f32[32,1,384]{2,1,0:T(1,128)} custom-call(f32[1,1,384]{2,1,0:T(1,128)} %reshape.119.x_ref), custom_call_target="tpu_custom_call" | custom-call | tf_op jit(solution)/shard_map/small_gather/pallas_call | solution.py:99
  55.2 0.8 copy.32
  56.1 0.3 collective-permute-start.4
  56.6 0.7 reshape.102.gain
  57.3 0.7 reshape.103.shift
  57.9 0.6 dynamic_slice.14.slopes
  58.5 0.6 pad_add_fusion.scal
  59.2 0.6 fusion.6.bias
  59.8 8.7 %qkv.1 = (bf16[1536,1024]{1,0:T(8,128)(2,1)}, bf16[1536,768]{1,0:T(8,128)(2,1)}) custom-call(s32[2]{0:T(128)} %pad_add_fusion.scal, bf16[384,1024]{1,0:T(8,128)(2,1)} %x.3, bf16[384,1024]{1,0:T(8,128)(2,1)} %collective-permute-done.x1, bf16[384,1024]{1,0:T(8,128)(2,1)} %copy-done.10, bf16[384,1024]{1,0:T(8,128)(2,1)} %copy-done.11, ...), custom_call_target="tpu_custom_call" | custom-call | tf_op jit(solution)/shard_map/qkv/pallas_call | solution.py:196
  68.5 15.1 %attend.1 = (bf16[1536,256]{1,0:T(8,128)(2,1)}, f32[2,8,1536]{2,1,0:T(8,128)}) custom-call(s32[2]{0:T(128)} %pad_add_fusion.scal, bf16[1536,768]{1,0:T(8,128)(2,1)} %get-tuple-element.61.q.k.v, bf16[1536,768]{1,0:T(8,128)(2,1)} %get-tuple-element.61.q.k.v, bf16[1536,768]{1,0:T(8,128)(2,1)} %get-tuple-element.61.q.k.v, f32[4]{0:T(128)} %dynamic_slice.14.slopes), custom_call_target="tpu_custom_call" | custom-call | tf_op jit(solution)/shard_map/attend/pallas_call | solution.py:273
  83.6 30.2 %all-gather.9.cloned.1.call-done = bf16[10240,128]{1,0:T(8,128)(2,1)} async-done(((bf16[1280,128]{1,0:T(8,128)(2,1)}), bf16[10240,128]{1,0:T(8,128)(2,1)}) %all-gather.9.cloned.1.call-update) | async-done | bytes 2621456 | tf_op jit(solution)/shard_map/all_gather | solution.py:1089
  113.8 6.6 %out_proj.1 = (bf16[2,384,1024]{2,1,0:T(8,128)(2,1)}, bf16[2,384,1024]{2,1,0:T(8,128)(2,1)}) custom-call(s32[2]{0:T(128)} %pad_add_fusion.scal, bf16[1536,256]{1,0:T(8,128)(2,1)} %get-tuple-element.64.o, bf16[8,1280,128]{2,1,0:T(8,128)(2,1)} %bitcast.40), custom_call_target="tpu_custom_call" | custom-call | tf_op jit(solution)/shard_map/out_proj/pallas_call | solution.py:411
  120.5 0.2 reduce-scatter.3.cloned.1.call-start
  120.7 3.4 collective-permute-done.5.b
  124.1 1.8 fusion.5
  125.8 1.5 collective-permute-start.6
  127.4 0.7 reshape.106.gain
  128.1 0.7 reshape.107.shift
  128.7 0.7 reshape.105.bias
  129.4 16.2 %collective-permute-done.6.c = bf16[384,1024]{1,0:T(8,128)(2,1)} collective-permute-done((bf16[384,1024]{1,0:T(8,128)(2,1)S(1)}, bf16[384,1024]{1,0:T(8,128)(2,1)}, u32[]{:S(2)}, u32[]{:S(2)}) %collective-permute-start.6) | collective-permute-done | bytes 786464 | tf_op jit(solution)/shard_map/ppermute | solution.py:155
  145.6 3.2 mid_norm.1
  148.8 1.6 collective-permute-start.8
  150.5 0.5 collective-permute-start.7
  151.0 16.9 %collective-permute-done.8.h2 = bf16[384,1024]{1,0:T(8,128)(2,1)S(1)} collective-permute-done((bf16[384,1024]{1,0:T(8,128)(2,1)}, bf16[384,1024]{1,0:T(8,128)(2,1)S(1)}, u32[]{:S(2)}, u32[]{:S(2)}) %collective-permute-start.8) | collective-permute-done | bytes 786464 | tf_op jit(solution)/shard_map/ppermute | solution.py:155
  167.9 0.7 constant_dynamic-slice_fusion.b1
  168.6 1.6 collective-permute-done.9.h3
  170.3 26.1 %mlp.1 = (bf16[2,384,1024]{2,1,0:T(8,128)(2,1)}, bf16[2,384,1024]{2,1,0:T(8,128)(2,1)}, bf16[2,384,1024]{2,1,0:T(8,128)(2,1)}, bf16[2,384,1024]{2,1,0:T(8,128)(2...) custom-call(bf16[384,1024]{1,0:T(8,128)(2,1)} %get-tuple-element.68., ...), custom_call_target="tpu_custom_call" | custom-call | tf_op jit(solution)/shard_map/mlp/pallas_call | solution.py:517
  196.4 8.2 %grad_fc1.1 = bf16[1024,1024]{1,0:T(8,128)(2,1)} custom-call(bf16[1536,1024]{1,0:T(8,128)(2,1)} %get-tuple-element.102.left, bf16[1536,1024]{1,0:T(8,128)(2,1)} %get-tuple-element.103.right), custom_call_target="tpu_custom_call" | custom-call | tf_op jit(solution)/shard_map/grad_fc1/pallas_call | solution.py:571
  204.7 0.2 collective-permute-start.11
  204.9 3.5 collective-permute-done.11.b
  208.4 1.1 fusion.4
  209.5 1.3 collective-permute-start.12
  210.8 8.2 %grad_fc2.1 = bf16[8,1024,128]{2,1,0:T(8,128)(2,1)} custom-call(bf16[1536,1024]{1,0:T(8,128)(2,1)} %get-tuple-element.105.left, bf16[1536,1024]{1,0:T(8,128)(2,1)} %get-tuple-element.106.right), custom_call_target="tpu_custom_call" | custom-call | tf_op jit(solution)/shard_map/grad_fc2/pallas_call | solution.py:571
  219.0 10.3 %collective-permute-done.12.c = bf16[384,1024]{1,0:T(8,128)(2,1)S(1)} collective-permute-done((bf16[384,1024]{1,0:T(8,128)(2,1)}, bf16[384,1024]{1,0:T(8,128)(2,1)S(1)}, u32[]{:S(2)}, u32[]{:S(2)}) %collective-permute-start.12) | collective-permute-done | bytes 786464 | tf_op jit(solution)/shard_map/ppermute | solution.py:155
  229.3 0.9 copy-done.17
  230.2 4.6 %mid_back.1 = (f32[384,1024]{1,0:T(8,128)}, bf16[384,1024]{1,0:T(8,128)(2,1)}, f32[8,1024]{1,0:T(8,128)}) custom-call(f32[384,1024]{1,0:T(8,128)} %get-tuple-element.67.mid, bf16[2,384,1024]{2,1,0:T(8,128)(2,1)} %get-tuple-element.71.a, bf16[2,384,1024]{2,1,0:T(8,128)(2,1)} %copy-done.5, bf16[384,1024]{1,0:T(8,128)(2,1)} %copy-done.17, ...), custom_call_target="tpu_custom_call" | custom-call | tf_op jit(solution)/shard_map/mid_back/pallas_call | solution.py:607
  234.8 1.3 collective-permute-start.13
  236.1 17.8 %collective-permute-done.13.b2 = bf16[384,1024]{1,0:T(8,128)(2,1)S(1)} collective-permute-done((bf16[384,1024]{1,0:T(8,128)(2,1)}, bf16[384,1024]{1,0:T(8,128)(2,1)S(1)}, u32[]{:S(2)}, u32[]{:S(2)}) %collective-permute-start.13) | collective-permute-done | bytes 786464 | tf_op jit(solution)/shard_map/ppermute | solution.py:155
  253.8 2.3 collective-permute-done.14.b3
  256.1 0.1 collective-permute-start.15
  256.3 0.4 collective-permute-start.17
  256.6 3.1 collective-permute-done.15
  259.8 1.1 copy-done.7
  260.9 1.0 fusion.3
  261.9 1.3 collective-permute-start.16
  263.2 8.0 %out_back.1 = (bf16[1536,256]{1,0:T(8,128)(2,1)}, bf16[8,256,128]{2,1,0:T(8,128)(2,1)}) custom-call(s32[2]{0:T(128)} %pad_add_fusion.scal, bf16[384,1024]{1,0:T(8,128)(2,1)} %get-tuple-element.73.b0, bf16[384,1024]{1,0:T(8,128)(2,1)} %collective-permute-done.17.b1, bf16[384,1024]{1,0:T(8,128)(2,1)} %copy-done.15, bf16[384,1024]{1,0:T(8,128)(2,1)} %copy-done.16, ...), custom_call_target="tpu_custom_call" | custom-call | tf_op jit(solution)/shard_map/out_back/pallas_call | solution.py:646
  271.2 21.4 %attend_back.1 = (bf16[1536,256]{1,0:T(8,128)(2,1)}, bf16[1536,256]{1,0:T(8,128)(2,1)}, bf16[1536,256]{1,0:T(8,128)(2,1)}) custom-call(s32[2]{0:T(128)} %pad_add_fusion.scal, bf16[1536,768]{1,0:T(8,128)(2,1)} %get-tuple-element.61.q.k.v, bf16[1536,768]{1,0:T(8,128)(2,1)} %get-tuple-element.61.q.k.v, bf16[1536,768]{1,0:T(8,128)(2,1)} %get-tuple-element.61.q.k.v, ...), custom_call_target="tpu_custom_call" | custom-call | tf_op jit(solution)/shard_map/attend_back/pallas_call | solution.py:347
  292.6 8.3 %qkv_back.1 = (bf16[2,384,1024]{2,1,0:T(8,128)(2,1)}, bf16[2,384,1024]{2,1,0:T(8,128)(2,1)}, bf16[1536,768]{1,0:T(8,128)(2,1)}, f32[1,768]{1,0:T(1,128)}) custom-call(s32[2]{0:T(128)} %pad_add_fusion.scal, bf16[1536,256]{1,0:T(8,128)(2,1)} %get-tuple-element.77.dq, bf16[1536,256]{1,0:T(8,128)(2,1)} %get-tuple-element.78.dk, ...), custom_call_target="tpu_custom_call" | custom-call | tf_op jit(solution)/shard_map/qkv_back/pallas_call | solution.py:692
  300.9 7.3 %grad_qkv.1 = bf16[1024,768]{1,0:T(8,128)(2,1)} custom-call(bf16[1536,1024]{1,0:T(8,128)(2,1)} %get-tuple-element.83.left, bf16[1536,768]{1,0:T(8,128)(2,1)} %get-tuple-element.84.right), custom_call_target="tpu_custom_call" | custom-call | tf_op jit(solution)/shard_map/grad_qkv/pallas_call | solution.py:571
  308.2 55.6 %tail.1 = (bf16[384,1024]{1,0:T(8,128)(2,1)}, f32[128,768]{1,0:T(8,128)}, f32[256,128]{1,0:T(8,128)}, f32[16,128]{1,0:T(8,128)}) custom-call(bf16[2,384,1024]{2,1,0:T(8,128)(2,1)} %get-tuple-element.80.near, bf16[2,384,1024]{2,1,0:T(8,128)(2,1)} %get-tuple-element.81.far, bf16[384,1024]{1,0:T(8,128)(2,1)} %x.3, f32[384,1024]{1,0:T(8,128)} %get-tuple-element.82.dmid, ...), custom_call_target="tpu_custom_call" | custom-call | tf_op jit(solution)/shard_map/tail/pallas_call | solution.py:981
  363.7 2.7 finish.1
  366.5 2.0 copy.29
  368.4 1.8 convert_element_type.39
  370.2 1.8 bitcast_convert_fusion
  372.0 2.8 fusion.2
  (88 shorter events, 0.9 us)
Async XLA Ops:
  7.2 3.7 copy-start
  7.2 52.6 %all-gather.5.cloned.1.call-start = ((), (), s32[]{:S(2)}) async-start(), calls=%async_computation.2 | async-start | bytes 1769472 | tf_op jit(solution)/shard_map/all_gather | solution.py:1082
  8.2 27.3 %copy-start.18 = (bf16[32]{0:T(256)(128)(2,1)S(1)}, bf16[32]{0:T(256)(128)(2,1)}, u32[]{:S(2)}) copy-start(bf16[32]{0:T(256)(128)(2,1)} %param.18) | copy-start | bytes 196
  8.2 27.3 %copy-start.19 = (bf16[32]{0:T(256)(128)(2,1)S(1)}, bf16[32]{0:T(256)(128)(2,1)}, u32[]{:S(2)}) copy-start(bf16[32]{0:T(256)(128)(2,1)} %param.19) | copy-start | bytes 196
  8.2 27.3 %copy-start.20 = (bf16[64]{0:T(256)(128)(2,1)S(1)}, bf16[64]{0:T(256)(128)(2,1)}, u32[]{:S(2)}) copy-start(bf16[64]{0:T(256)(128)(2,1)} %param.21) | copy-start | bytes 388
  8.3 27.3 %copy-start.21 = (bf16[32]{0:T(256)(128)(2,1)S(1)}, bf16[32]{0:T(256)(128)(2,1)}, u32[]{:S(2)}) copy-start(bf16[32]{0:T(256)(128)(2,1)} %param.23) | copy-start | bytes 196
  8.3 27.3 %copy-start.22 = (bf16[32]{0:T(256)(128)(2,1)S(1)}, bf16[32]{0:T(256)(128)(2,1)}, u32[]{:S(2)}) copy-start(bf16[32]{0:T(256)(128)(2,1)} %param.24) | copy-start | bytes 196
  8.3 27.3 %copy-start.23 = (bf16[32]{0:T(256)(128)(2,1)S(1)}, bf16[32]{0:T(256)(128)(2,1)}, u32[]{:S(2)}) copy-start(bf16[32]{0:T(256)(128)(2,1)} %param.25) | copy-start | bytes 196
  8.3 27.3 %copy-start.24 = (bf16[128]{0:T(256)(128)(2,1)S(1)}, bf16[128]{0:T(256)(128)(2,1)}, u32[]{:S(2)}) copy-start(bf16[128]{0:T(256)(128)(2,1)} %param.27) | copy-start | bytes 772
  8.3 27.3 %copy-start.25 = (bf16[32]{0:T(256)(128)(2,1)S(1)}, bf16[32]{0:T(256)(128)(2,1)}, u32[]{:S(2)}) copy-start(bf16[32]{0:T(256)(128)(2,1)} %param.29) | copy-start | bytes 196
  9.0 104.8 %all-gather.9.cloned.1.call-start = ((), (), s32[]{:S(2)}) async-start(), calls=%async_computation.6 | async-start | bytes 2949120 | tf_op jit(solution)/shard_map/all_gather | solution.py:1089
  10.8 157.8 %all-gather.7.cloned.1.call-start = ((), (), s32[]{:S(2)}) async-start(), calls=%async_computation.3 | async-start | bytes 2359296 | tf_op jit(solution)/shard_map/all_gather | solution.py:1093
  10.9 20.6 %collective-permute-start.1 = (bf16[384,1024]{1,0:T(8,128)(2,1)S(1)}, bf16[384,1024]{1,0:T(8,128)(2,1)S(1)}, u32[]{:S(2)}, u32[]{:S(2)}) collective-permute-start(bf16[384,1024]{1,0:T(8,128)(2,1)S(1)} %copy-done), channel_id=1, source_target_pairs={{0,2},{1,3},{2,0},{3,1},{4,6},{5,7},{6,4},{7,5},{8,10},{9,11},{10,... | collective-permute-start | bytes 2359304 | tf_op jit(solution)/shard_map/ppermute | solution.py:155
  31.5 1.9 copy-start.10
  31.5 2.3 collective-permute-start.2
  33.5 117.0 %copy-start.1 = (bf16[384,1024]{1,0:T(8,128)(2,1)}, bf16[384,1024]{1,0:T(8,128)(2,1)S(1)}, u32[]{:S(2)}) copy-start(bf16[384,1024]{1,0:T(8,128)(2,1)S(1)} %broadcast_select_fusion.g0.g) | copy-start | bytes 2359300
  33.8 22.3 %copy-start.11 = (bf16[384,1024]{1,0:T(8,128)(2,1)}, bf16[384,1024]{1,0:T(8,128)(2,1)S(1)}, u32[]{:S(2)}) copy-start(bf16[384,1024]{1,0:T(8,128)(2,1)S(1)} %collective-permute-done.2.x3) | copy-start | bytes 2359300
  33.8 22.3 %collective-permute-start.3 = (bf16[384,1024]{1,0:T(8,128)(2,1)S(1)}, bf16[384,1024]{1,0:T(8,128)(2,1)S(1)}, u32[]{:S(2)}, u32[]{:S(2)}) collective-permute-start(bf16[384,1024]{1,0:T(8,128)(2,1)S(1)} %broadcast_select_fusion.g0.g), channel_id=1, source_target_pairs={{0,2},{1,3},{2,0},{3,1},{4,6},{5,7},{6,4},{7,5},{8,10},{9,11},{10,... | collective-permute-start | bytes 2359304 | tf_op jit(solution)/shard_map/ppermute | solution.py:155
  35.5 24.2 %collective-permute-start = (bf16[384,1024]{1,0:T(8,128)(2,1)S(1)}, bf16[384,1024]{1,0:T(8,128)(2,1)}, u32[]{:S(2)}, u32[]{:S(2)}) collective-permute-start(bf16[384,1024]{1,0:T(8,128)(2,1)S(1)} %copy-done), channel_id=1, source_target_pairs={{0,1},{1,0},{2,3},{3,2},{4,5},{5,4},{6,7},{7,6},{8,9},{9,8},{10,11... | collective-permute-start | bytes 2359304 | tf_op jit(solution)/shard_map/ppermute | solution.py:155
  56.1 12.5 %copy-start.8 = (bf16[384,1024]{1,0:T(8,128)(2,1)}, bf16[384,1024]{1,0:T(8,128)(2,1)S(1)}, u32[]{:S(2)}) copy-start(bf16[384,1024]{1,0:T(8,128)(2,1)S(1)} %collective-permute-done.3.g2) | copy-start | bytes 2359300
  56.1 27.5 %collective-permute-start.4 = (bf16[384,1024]{1,0:T(8,128)(2,1)S(1)}, bf16[384,1024]{1,0:T(8,128)(2,1)S(1)}, u32[]{:S(2)}, u32[]{:S(2)}) collective-permute-start(bf16[384,1024]{1,0:T(8,128)(2,1)S(1)} %collective-permute-done.3.g2), channel_id=1, source_target_pairs={{0,1},{1,0},{2,3},{3,2},{4,5},{5,4},{6,7},{7,6},{8,9},{9,8},{10,11... | collective-permute-start | bytes 2359304 | tf_op jit(solution)/shard_map/ppermute | solution.py:155
  83.6 36.9 %copy-start.9 = (bf16[384,1024]{1,0:T(8,128)(2,1)}, bf16[384,1024]{1,0:T(8,128)(2,1)S(1)}, u32[]{:S(2)}) copy-start(bf16[384,1024]{1,0:T(8,128)(2,1)S(1)} %collective-permute-done.4.g3) | copy-start | bytes 2359300
  120.5 3.6 collective-permute-start.5
  120.5 247.9 %reduce-scatter.3.cloned.1.call-start = ((), (), s32[]{:S(2)}) async-start(), calls=%async_computation.4 | async-start | bytes 2359296 | tf_op jit(solution)/shard_map/reduce_scatter | solution.py:1156
  124.1 21.5 %copy-start.4 = (bf16[2,384,1024]{2,1,0:T(8,128)(2,1)}, bf16[2,384,1024]{2,1,0:T(8,128)(2,1)S(1)}, u32[]{:S(2)}) copy-start(bf16[2,384,1024]{2,1,0:T(8,128)(2,1)S(1)} %collective-permute-done.5.b) | copy-start | bytes 4718596
  125.8 19.8 %collective-permute-start.6 = (bf16[384,1024]{1,0:T(8,128)(2,1)S(1)}, bf16[384,1024]{1,0:T(8,128)(2,1)}, u32[]{:S(2)}, u32[]{:S(2)}) collective-permute-start(bf16[384,1024]{1,0:T(8,128)(2,1)S(1)} %fusion.5), channel_id=1, source_target_pairs={{0,2},{1,3},{2,0},{3,1},{4,6},{5,7},{6,4},{7,5},{8,10},{9,11},{10,... | collective-permute-start | bytes 2359304 | tf_op jit(solution)/shard_map/ppermute | solution.py:155
  148.8 19.0 %collective-permute-start.8 = (bf16[384,1024]{1,0:T(8,128)(2,1)}, bf16[384,1024]{1,0:T(8,128)(2,1)S(1)}, u32[]{:S(2)}, u32[]{:S(2)}) collective-permute-start(bf16[384,1024]{1,0:T(8,128)(2,1)} %get-tuple-element.68.h0), channel_id=1, source_target_pairs={{0,2},{1,3},{2,0},{3,1},{4,6},{5,7},{6,4},{7,5},{8,10},{9,11},{10,... | collective-permute-start | bytes 2359304 | tf_op jit(solution)/shard_map/ppermute | solution.py:155
  150.5 18.2 %collective-permute-start.10 = (bf16[384,1024]{1,0:T(8,128)(2,1)S(1)}, bf16[384,1024]{1,0:T(8,128)(2,1)S(1)}, u32[]{:S(2)}, u32[]{:S(2)}) collective-permute-start(bf16[384,1024]{1,0:T(8,128)(2,1)S(1)} %broadcast_select_fusion.g0.g), channel_id=1, source_target_pairs={{0,1},{1,0},{2,3},{3,2},{4,5},{5,4},{6,7},{7,6},{8,9},{9,8},{10,11... | collective-permute-start | bytes 2359304 | tf_op jit(solution)/shard_map/ppermute | solution.py:155
  150.5 18.2 %collective-permute-start.7 = (bf16[384,1024]{1,0:T(8,128)(2,1)}, bf16[384,1024]{1,0:T(8,128)(2,1)S(1)}, u32[]{:S(2)}, u32[]{:S(2)}) collective-permute-start(bf16[384,1024]{1,0:T(8,128)(2,1)} %get-tuple-element.68.h0), channel_id=1, source_target_pairs={{0,1},{1,0},{2,3},{3,2},{4,5},{5,4},{6,7},{7,6},{8,9},{9,8},{10,11... | collective-permute-start | bytes 2359304 | tf_op jit(solution)/shard_map/ppermute | solution.py:155
  167.8 2.4 copy-start.12
  167.8 2.4 collective-permute-start.9
  168.6 1.6 copy-start.13
  168.6 1.6 copy-start.14
  204.7 3.8 copy-start.3
  204.7 165.5 %reduce-scatter.5.cloned.1.call-start = ((), (), s32[]{:S(2)}) async-start(), calls=%async_computation.5 | async-start | bytes 2359296 | tf_op jit(solution)/shard_map/reduce_scatter | solution.py:1152
  204.7 3.7 collective-permute-start.11
  208.4 10.5 %copy-start.5 = (bf16[2,384,1024]{2,1,0:T(8,128)(2,1)}, bf16[2,384,1024]{2,1,0:T(8,128)(2,1)S(1)}, u32[]{:S(2)}) copy-start(bf16[2,384,1024]{2,1,0:T(8,128)(2,1)S(1)} %collective-permute-done.11.b) | copy-start | bytes 4718596
  209.5 19.8 %collective-permute-start.12 = (bf16[384,1024]{1,0:T(8,128)(2,1)}, bf16[384,1024]{1,0:T(8,128)(2,1)S(1)}, u32[]{:S(2)}, u32[]{:S(2)}) collective-permute-start(bf16[384,1024]{1,0:T(8,128)(2,1)} %fusion.4), channel_id=1, source_target_pairs={{0,2},{1,3},{2,0},{3,1},{4,6},{5,7},{6,4},{7,5},{8,10},{9,11},{10,... | collective-permute-start | bytes 2359304 | tf_op jit(solution)/shard_map/ppermute | solution.py:155
  229.3 0.9 copy-start.17
  230.2 30.8 %copy-start.6 = (bf16[2,384,1024]{2,1,0:T(8,128)(2,1)S(1)}, bf16[2,384,1024]{2,1,0:T(8,128)(2,1)}, u32[]{:S(2)}) copy-start(bf16[2,384,1024]{2,1,0:T(8,128)(2,1)} %get-tuple-element.69) | copy-start | bytes 4718596
  234.8 19.1 %collective-permute-start.13 = (bf16[384,1024]{1,0:T(8,128)(2,1)}, bf16[384,1024]{1,0:T(8,128)(2,1)S(1)}, u32[]{:S(2)}, u32[]{:S(2)}) collective-permute-start(bf16[384,1024]{1,0:T(8,128)(2,1)} %get-tuple-element.73.b0), channel_id=1, source_target_pairs={{0,2},{1,3},{2,0},{3,1},{4,6},{5,7},{6,4},{7,5},{8,10},{9,11},{10,... | collective-permute-start | bytes 2359304 | tf_op jit(solution)/shard_map/ppermute | solution.py:155
  253.8 9.4 %copy-start.15 = (bf16[384,1024]{1,0:T(8,128)(2,1)}, bf16[384,1024]{1,0:T(8,128)(2,1)S(1)}, u32[]{:S(2)}) copy-start(bf16[384,1024]{1,0:T(8,128)(2,1)S(1)} %collective-permute-done.13.b2) | copy-start | bytes 2359300
  253.8 2.3 collective-permute-start.14
  256.1 7.1 %copy-start.16 = (bf16[384,1024]{1,0:T(8,128)(2,1)}, bf16[384,1024]{1,0:T(8,128)(2,1)S(1)}, u32[]{:S(2)}) copy-start(bf16[384,1024]{1,0:T(8,128)(2,1)S(1)} %collective-permute-done.14.b3) | copy-start | bytes 2359300
  256.1 3.6 collective-permute-start.15
  256.3 7.0 %collective-permute-start.17 = (bf16[384,1024]{1,0:T(8,128)(2,1)}, bf16[384,1024]{1,0:T(8,128)(2,1)}, u32[]{:S(2)}, u32[]{:S(2)}) collective-permute-start(bf16[384,1024]{1,0:T(8,128)(2,1)} %get-tuple-element.73.b0), channel_id=1, source_target_pairs={{0,1},{1,0},{2,3},{3,2},{4,5},{5,4},{6,7},{7,6},{8,9},{9,8},{10,11... | collective-permute-start | bytes 2359304 | tf_op jit(solution)/shard_map/ppermute | solution.py:155
  259.8 1.1 copy-start.7
  261.9 110.1 %collective-permute-start.16 = (bf16[384,1024]{1,0:T(8,128)(2,1)}, bf16[384,1024]{1,0:T(8,128)(2,1)}, u32[]{:S(2)}, u32[]{:S(2)}) collective-permute-start(bf16[384,1024]{1,0:T(8,128)(2,1)} %fusion.3), channel_id=1, source_target_pairs={{0,2},{1,3},{2,0},{3,1},{4,6},{5,7},{6,4},{7,5},{8,10},{9,11},{10,... | collective-permute-start | bytes 2359304 | tf_op jit(solution)/shard_map/ppermute | solution.py:155
  366.4 5.6 %copy-start.2 = (f32[384,1024]{1,0:T(8,128)S(1)}, f32[384,1024]{1,0:T(8,128)}, u32[]{:S(2)}) copy-start(f32[384,1024]{1,0:T(8,128)} %get-tuple-element.67.mid) | copy-start | bytes 4718596
Sparse Core Ops, SparseCore 0:
  10.8 47.1 all-gather.4
  60.7 53.0 all-gather.8
  120.6 47.7 all-gather.6
  204.8 66.6 reduce-scatter.2
  274.9 72.0 reduce-scatter.4

commit v3 on v2

--- a/solution.py
+++ b/solution.py
@@ -468,7 +468,7 @@
 
 
 def mlp_body(
-    h0, h1, h2, h3, g0, g1, g2, g3, w1, w2, b1,
+    h0, h1, h2, h3, g_rows, w1, w2, b1,
     y_near, y_far, d_near, d_far, a_all, du_all, h_all, g_all, bias_sum,
     flat, hb, gb,
 ):
@@ -480,7 +480,7 @@
         bias_sum[...] = jnp.zeros_like(bias_sum)
 
     pick(rel_of(t), (h0, h1, h2, h3), hb)
-    pick(rel_of(t), (g0, g1, g2, g3), gb)
+    gb[...] = g_rows[rel_of(t)]
     h_all[...] = hb[...]
     g_all[...] = gb[...]
     inner = w1.shape[1]
@@ -507,7 +507,7 @@
         d_far[0] = d
 
 
-def mlp_call(h_pieces, g_pieces, w1, w2, b1):
+def mlp_call(h_pieces, g_rows, w1, w2, b1):
     rows, width = h_pieces[0].shape
     inner = w1.shape[1]
     pair = jax.ShapeDtypeStruct((2, rows, width), bf16)
@@ -528,7 +528,7 @@
             jax.ShapeDtypeStruct((1, inner), f32),
         ),
         grid=(4,),
-        in_specs=[WHOLE] * 11,
+        in_specs=[WHOLE] * 8,
         out_specs=(
             near, far, near, far, block(inner), block(inner), block(width), block(width),
             pl.BlockSpec((1, inner), lambda t: (0, 0)),
@@ -540,7 +540,7 @@
         ],
         compiler_params=params(),
         name="mlp",
-    )(*h_pieces, *g_pieces, w1, w2, b1)
+    )(*h_pieces, g_rows, w1, w2, b1)
 
 
 def outer_body(left, right, out, turned, *, blocks):
@@ -1005,6 +1005,397 @@
         compiler_params=params(collective_id=3, has_side_effects=True),
         name="tail",
     )(near, far, x, dmid, gain, gq, go, mid_sums, up_sum, qkv_sums)
+
+
+class Gather:
+    def __init__(self, own, out, sems, dp, seq):
+        self.own, self.out, self.sems = own, out, sems
+        self.seq, self.z, self.x = seq, dp // 2, dp % 2
+
+    def along(self, k, step, src=None):
+        slot = self.out.at[2 * k + self.x]
+        return remote(
+            slot if src is None else src,
+            slot,
+            self.sems.at[0 if step > 0 else 1, k],
+            self.sems.at[3, k],
+            2 * ((self.z + step + 4) % 4) + self.x,
+            self.seq,
+        )
+
+    def over(self, k, src=None):
+        slot = self.out.at[2 * k + self.x]
+        return remote(
+            slot if src is None else src,
+            slot,
+            self.sems.at[2, k],
+            self.sems.at[4, k],
+            2 * self.z + (1 - self.x),
+            self.seq,
+        )
+
+    def keep(self):
+        return pltpu.make_async_copy(
+            self.own, self.out.at[2 * self.z + self.x], self.sems.at[5, 0]
+        )
+
+    def start(self):
+        z = self.z
+
+        @pl.when(z < 3)
+        def _():
+            self.along(z, 1, self.own).start()
+
+        @pl.when(z > 0)
+        def _():
+            self.along(z, -1, self.own).start()
+
+        self.over(z, self.own).start()
+        self.keep().start()
+
+    def hop(self, dist):
+        z = self.z
+
+        @pl.when(z - dist >= 0)
+        def _():
+            k = z - dist
+            self.along(k, 1).wait_recv()
+
+            @pl.when(z < 3)
+            def _():
+                self.along(k, 1).start()
+
+            self.over(k).start()
+
+        @pl.when(z + dist <= 3)
+        def _():
+            k = z + dist
+            self.along(k, -1).wait_recv()
+
+            @pl.when(z > 0)
+            def _():
+                self.along(k, -1).start()
+
+            self.over(k).start()
+
+    def finish(self):
+        z = self.z
+        self.keep().wait()
+        for k in range(4):
+            self.over(k).wait_recv()
+            self.over(k).wait_send()
+
+            @pl.when((z < 3) & (z >= k))
+            def _(k=k):
+                self.along(k, 1).wait_send()
+
+            @pl.when((z > 0) & (z <= k))
+            def _(k=k):
+                self.along(k, -1).wait_send()
+
+    @staticmethod
+    def scratch():
+        return pltpu.SemaphoreType.DMA((6, 4))
+
+
+class Spread:
+    def __init__(self, own, rows, sems, dp, seq):
+        mate, across = seq + 1 - 2 * (seq % 2), (seq + 2) % 4
+        to = lambda src, r, peer: remote(src, rows.at[r], sems.at[0, r], sems.at[1, r], dp, peer)
+        self.near, self.far = to(own, 1, mate), to(own, 2, across)
+        self.last = to(rows.at[2], 3, mate)
+
+    def start(self):
+        self.far.start()
+        self.near.start()
+
+    def forward(self):
+        self.far.wait_recv()
+        self.last.start()
+
+    def drain(self):
+        for copy in (self.near, self.far, self.last):
+            copy.wait_send()
+
+
+def neighbours(seq):
+    mate = seq + 1 - 2 * (seq % 2)
+    return mate, (seq + 2) % 4, (mate + 2) % 4
+
+
+def block_at(seq, rel):
+    return 2 * ((seq // 2 + rel // 2) % 2) + (seq + rel) % 2
+
+
+def front_body(
+    wq, wo, x, small,
+    wq_all, wo_all, x_rows, gain1, shift1, bias_qkv, bias_out, gain2, shift2, bias_up, bias_down,
+    vectors, q_sem, o_sem, x_sem, seq_sem, dp_sem, keep_sem,
+):
+    dp, seq = lax.axis_index("dp"), lax.axis_index("seq")
+    greet([((dp + i) % 8, seq) for i in range(1, 8)] + [(dp, p) for p in neighbours(seq)])
+    gather_q = Gather(wq, wq_all, q_sem, dp, seq)
+    gather_o = Gather(wo, wo_all, o_sem, dp, seq)
+    rows = Spread(x, x_rows, x_sem, dp, seq)
+    rows.start()
+    gather_q.start()
+    keep_x = pltpu.make_async_copy(x, x_rows.at[0], keep_sem.at[0])
+    keep_x.start()
+    keep_v = pltpu.make_async_copy(small, vectors.at[dp, seq], keep_sem.at[1])
+    keep_v.start()
+    group = [
+        remote(small, vectors.at[dp, seq], seq_sem.at[0, i], seq_sem.at[1, i], dp, peer)
+        for i, peer in enumerate(neighbours(seq))
+    ]
+    for copy in group:
+        copy.start()
+    gather_o.start()
+    keep_v.wait()
+    for copy in group:
+        copy.wait_recv()
+
+    def to_dp(i):
+        return remote(
+            vectors.at[dp], vectors.at[dp], dp_sem.at[0, i], dp_sem.at[1, i], (dp + i) % 8, seq
+        )
+
+    for i in range(1, 8):
+        to_dp(i).start()
+    gather_q.hop(1)
+    gather_o.hop(1)
+    for i in range(1, 8):
+        to_dp(i).wait_recv()
+    for ref, at in (
+        (gain1, 192), (shift1, 224), (bias_out, 256), (gain2, 288), (shift2, 320), (bias_down, 352),
+    ):
+        for d in range(8):
+            ref[:, d * LANES : (d + 1) * LANES] = jnp.concatenate(
+                [vectors[d, i, :, at : at + 32] for i in range(4)], axis=1
+            )
+    for part in range(2):
+        for half in range(2):
+            lane = part * 512 + half * LANES
+            bias_qkv[:, lane : lane + LANES] = jnp.concatenate(
+                [vectors[4 * part + seq, 2 * half + i, :, 128:192] for i in range(2)], axis=1
+            )
+    bias_qkv[:, 256:512] = jnp.zeros((1, 256), f32)
+    for i in range(8):
+        bias_up[:, i * LANES : (i + 1) * LANES] = vectors[2 * seq + i // 4, i % 4, :, 0:LANES]
+    gather_q.hop(2)
+    gather_o.hop(2)
+    rows.forward()
+    gather_q.hop(3)
+    gather_o.hop(3)
+    gather_q.finish()
+    gather_o.finish()
+    rows.near.wait_recv()
+    rows.last.wait_recv()
+    rows.drain()
+    keep_x.wait()
+    for copy in group:
+        copy.wait_send()
+    for i in range(1, 8):
+        to_dp(i).wait_send()
+
+
+def front_call(wq, wo, x, small):
+    rows, width = x.shape
+    one = lambda n: jax.ShapeDtypeStruct((1, n), f32)
+    sem = pltpu.SemaphoreType.DMA
+    return pl.pallas_call(
+        front_body,
+        out_shape=(
+            jax.ShapeDtypeStruct((8, *wq.shape), bf16),
+            jax.ShapeDtypeStruct((8, *wo.shape), bf16),
+            jax.ShapeDtypeStruct((4, rows, width), bf16),
+            one(width), one(width), one(wq.shape[1]), one(width), one(width), one(width),
+            one(width), one(width),
+        ),
+        in_specs=[WHOLE] * 4,
+        out_specs=(WHOLE,) * 11,
+        scratch_shapes=[
+            pltpu.VMEM((8, 4, 1, small.shape[-1]), f32),
+            Gather.scratch(),
+            Gather.scratch(),
+            sem((2, 4)),
+            sem((2, 3)),
+            sem((2, 8)),
+            sem((2,)),
+        ],
+        compiler_params=params(collective_id=4, has_side_effects=True),
+        name="front",
+    )(wq, wo, x, small.reshape(1, -1))
+
+
+def attention_body(
+    scal, slopes, x_rows, g, wq, wo, gain1, shift1, bias_qkv, bias_out, gain2, shift2,
+    h1, qkv, o, lse, mid, h2, g_rows,
+    bias, vt, flat, part, land_c, sum_y, land_y, g_sem, row_sems, keep_sem,
+):
+    dp, seq = lax.axis_index("dp"), lax.axis_index("seq")
+    mate, across, _ = neighbours(seq)
+    greet([(dp, mate), (dp, across)])
+    rows, width = g.shape
+    keys = qkv.shape[0]
+    inner = o.shape[1]
+    pairs = inner // LANES
+    spread_g = Spread(g, g_rows, g_sem, dp, seq)
+    spread_g.start()
+    keep = pltpu.make_async_copy(g, g_rows.at[0], keep_sem.at[0])
+    keep.start()
+    lay_columns(wo, 0, flat)
+
+    def project(r, carry):
+        at = pl.ds(pl.multiple_of(block_at(seq, r) * rows, rows), rows)
+        unit, _ = normalize(x_rows[r].astype(f32))
+        low = (unit * gain1[...] + shift1[...]).astype(bf16)
+        h1[at, :] = low
+        qkv[at, :] = (mm(low, wq[...]) + bias_qkv[...]).astype(bf16)
+        return carry
+
+    lax.fori_loop(0, 4, project, 0)
+
+    def prepare(p, carry):
+        pos = lax.broadcasted_iota(jnp.int32, (keys, LANES), 0)
+        ramp = pos.astype(f32)
+        inside = pos < scal[1]
+        for h in range(2):
+            bias[2 * p + h] = jnp.where(inside, ramp * slopes[2 * p + h], NEG)
+        lane = pl.ds(pl.multiple_of(2 * inner + p * LANES, LANES), LANES)
+        vt[p] = qkv[:, lane].T
+        return carry
+
+    lax.fori_loop(0, pairs, prepare, 0)
+    spread_g.forward()
+
+    cores = [
+        remote(part.at[r], land_c.at[k], row_sems.at[0, k], row_sems.at[1, k], dp, mate)
+        for k, r in ((0, 1), (1, 3))
+    ]
+    over = remote(sum_y, land_y, row_sems.at[0, 2], row_sems.at[1, 2], dp, across)
+    chunk = 128
+
+    def attend(t, carry):
+        rel = 3 - t
+        c_now = block_at(seq, rel)
+        at = pl.ds(pl.multiple_of(c_now * rows, rows), rows)
+        for c in range(keys // rows):
+
+            @pl.when(c_now == c)
+            def _(c=c):
+                length = (c + 1) * rows
+
+                def one_pair(p, carry):
+                    lane = pl.ds(pl.multiple_of(p * LANES, LANES), LANES)
+                    k_lane = pl.ds(pl.multiple_of(inner + p * LANES, LANES), LANES)
+                    scaled = qkv[c * rows : length, lane] * bf16(HEAD_DIM**-0.5)
+                    k = qkv[0:length, k_lane]
+                    outs, logs = [], []
+                    for h in range(2):
+                        s = scores(k, head_only(scaled, h), bias[2 * p + h, 0:length, :])
+                        top = jnp.max(s, axis=0, keepdims=True)
+                        e = jnp.exp(s - top)
+                        total = jnp.sum(e, axis=0, keepdims=True)
+                        half = vt[p, h * HEAD_DIM : (h + 1) * HEAD_DIM, 0:length]
+                        outs.append(mm(half, e.astype(bf16)) / total)
+                        logs.append(top + jnp.log(total))
+                    o[c * rows : length, lane] = jnp.concatenate(outs, axis=0).T.astype(bf16)
+                    lse[p, 0:2, c * rows : length] = jnp.concatenate(logs, axis=0)
+                    return carry
+
+                lax.fori_loop(0, pairs, one_pair, 0)
+
+        part[rel] = mm(o[at, :], flat[...]).astype(bf16)
+
+        @pl.when(t == 0)
+        def _():
+            cores[1].start()
+
+        @pl.when(t == 1)
+        def _():
+            cores[1].wait_recv()
+            for i in range(rows // chunk):
+                at = slice(i * chunk, (i + 1) * chunk)
+                total = part[2, at, :].astype(f32) + land_c[1, at, :].astype(f32)
+                sum_y[at, :] = total.astype(bf16)
+            over.start()
+
+        @pl.when(t == 2)
+        def _():
+            cores[0].start()
+
+        return carry
+
+    lax.fori_loop(0, 4, attend, 0)
+    cores[0].wait_recv()
+    over.wait_recv()
+
+    def second_norm(i, carry):
+        at = pl.ds(pl.multiple_of(i * chunk, chunk), chunk)
+        total = (part[0, at, :].astype(f32) + land_c[0, at, :].astype(f32)) + land_y[
+            at, :
+        ].astype(f32)
+        value = x_rows[0, at, :].astype(f32) + (total + bias_out[...])
+        mid[at, :] = value
+        unit, _ = normalize(value)
+        h2[at, :] = (unit * gain2[...] + shift2[...]).astype(bf16)
+        return carry
+
+    lax.fori_loop(0, rows // chunk, second_norm, 0)
+    spread_g.near.wait_recv()
+    spread_g.last.wait_recv()
+    spread_g.drain()
+    keep.wait()
+    for copy in cores + [over]:
+        copy.wait_send()
+
+
+def scores(k, qm, ramp):
+    block = qm.shape[0]
+    length = k.shape[0]
+    s = mm_t(k, qm) + jnp.concatenate([ramp] * (block // LANES), axis=1)
+    key = lax.broadcasted_iota(jnp.int32, (block, block), 0)
+    query = lax.broadcasted_iota(jnp.int32, (block, block), 1)
+    last = jnp.where(key <= query, s[length - block :], NEG)
+    if length == block:
+        return last
+    return jnp.concatenate([s[: length - block], last], axis=0)
+
+
+def attention_call(scal, slopes, x_rows, g, wq, wo, *vectors):
+    rows, width = g.shape
+    keys = 4 * rows
+    inner = wo.shape[1]
+    pairs = inner // LANES
+    sem = pltpu.SemaphoreType.DMA
+    return pl.pallas_call(
+        attention_body,
+        out_shape=(
+            jax.ShapeDtypeStruct((keys, width), bf16),
+            jax.ShapeDtypeStruct((keys, 3 * inner), bf16),
+            jax.ShapeDtypeStruct((keys, inner), bf16),
+            jax.ShapeDtypeStruct((pairs, 8, keys), f32),
+            jax.ShapeDtypeStruct((rows, width), f32),
+            jax.ShapeDtypeStruct((rows, width), bf16),
+            jax.ShapeDtypeStruct((4, rows, width), bf16),
+        ),
+        in_specs=[SCALAR, SCALAR] + [WHOLE] * (4 + len(vectors)),
+        out_specs=(WHOLE,) * 7,
+        scratch_shapes=[
+            pltpu.VMEM((2 * pairs, keys, LANES), f32),
+            pltpu.VMEM((pairs, LANES, keys), bf16),
+            pltpu.VMEM((inner, width), bf16),
+            pltpu.VMEM((4, rows, width), bf16),
+            pltpu.VMEM((2, rows, width), bf16),
+            pltpu.VMEM((rows, width), bf16),
+            pltpu.VMEM((rows, width), bf16),
+            sem((2, 4)),
+            sem((2, 3)),
+            sem((1,)),
+        ],
+        compiler_params=params(collective_id=5, has_side_effects=True),
+        name="attention",
+    )(scal, slopes, x_rows, g, wq, wo, *vectors)
 
 
 def finish_body(
@@ -1079,56 +1470,72 @@
     s = lax.axis_index("seq")
     length = lengths[0]
 
-    wq = lax.all_gather(
-        jnp.concatenate([w_qkv[:, c, :] for c in range(3)], axis=1), "dp", axis=0, tiled=True
-    )
-    col = w_fc2.shape[1]
-    both = jnp.concatenate([w_fc2, w_out], axis=0)
-    if col % LANES == 0:
-        parts = dp_n
-        w_cols = lax.all_gather(both, "dp", axis=0, tiled=False)
-    else:
-        parts = 1
-        w_cols = lax.all_gather(both, "dp", axis=1, tiled=True)[None]
-    w1 = lax.all_gather(w_fc1, "dp", axis=0, tiled=True)
-
+    scal = jnp.stack([s.astype(jnp.int32), length])
+    slopes = 2.0 ** (-8.0 * (jnp.arange(heads, dtype=jnp.int32) + 1).astype(f32) / heads)
+    slopes = lax.dynamic_slice(slopes, (s * (heads // seq_n),), (heads // seq_n,))
+    valid = s * rows + jnp.arange(rows, dtype=jnp.int32) < length
+    grad_low = jnp.where(valid[:, None], cotangent, jnp.zeros_like(cotangent))
+    wq_own = jnp.concatenate([w_qkv[:, c, :] for c in range(3)], axis=1)
     small = (ln1_gain, ln1_shift, b_qv, b_out, ln2_gain, ln2_shift, b_fc1, b_fc2)
     sizes = [v.shape[0] for v in small]
     ends = [sum(sizes[: i + 1]) for i in range(len(sizes))]
-    packed = small_gather(jnp.concatenate([v.astype(f32) for v in small]), count, seq_n)
-    packed = packed.reshape(count, ends[-1])
-    gain1, shift1, bias_qv, bias_out, gain2, shift2, bias_up, bias_down = (
-        packed[:, e - n : e].reshape(1, count * n) for e, n in zip(ends, sizes)
-    )
-
-    scal = jnp.stack([s.astype(jnp.int32), length])
-    slopes = 2.0 ** (-8.0 * (jnp.arange(heads, dtype=jnp.int32) + 1).astype(f32) / heads)
-    slopes = lax.dynamic_slice(slopes, (s * (heads // seq_n),), (heads // seq_n,))
-    own_bias = lambda v, n: lax.dynamic_slice(v, (0, s * n), (1, n))
-    qkv_bias = jnp.concatenate(
-        [
-            own_bias(bias_qv[:, :width], inner),
-            jnp.zeros((1, inner), f32),
-            own_bias(bias_qv[:, width:], inner),
-        ],
-        axis=1,
-    )
-
-    x_pieces = spread(tokens)
-    valid = s * rows + jnp.arange(rows, dtype=jnp.int32) < length
-    grad_low = jnp.where(valid[:, None], cotangent, jnp.zeros_like(cotangent))
-    g_pieces = spread(after(grad_low, x_pieces[3]))
-
     block = 384
-    h1, qkv = qkv_call(scal, x_pieces, wq, gain1, shift1, qkv_bias)
-    o, lse = attend_call(scal, slopes, qkv, block)
-    o = after(o, g_pieces[2], g_pieces[3])
-    near, far = out_call(scal, o, w_cols, ff)
-    got, across = reduce_rows(near, far)
-    mid, h2 = mid_call(tokens, far, got, across, bias_out, gain2, shift2)
+    fast = dp_n == 8 and seq_n == 4 and width == 8 * LANES and ff == width and inner == 2 * LANES
+    if fast:
+        parts = dp_n
+        w1 = lax.all_gather(w_fc1, "dp", axis=0, tiled=True)
+        w_cols = lax.all_gather(w_fc2, "dp", axis=0, tiled=False)
+        order = (b_fc1, b_qv, ln1_gain, ln1_shift, b_out, ln2_gain, ln2_shift, b_fc2)
+        wq, w_o, x_rows, gain1, shift1, qkv_bias, bias_out, gain2, shift2, own_up, bias_down = (
+            front_call(
+                wq_own, w_out, tokens, jnp.concatenate([v.astype(f32) for v in order])
+            )
+        )
+        wq = wq.reshape(width, 3 * inner)
+        h1, qkv, o, lse, mid, h2, g_rows = attention_call(
+            scal, slopes, x_rows, grad_low, wq, w_o,
+            gain1, shift1, qkv_bias, bias_out, gain2, shift2,
+        )
+        out_first = 0
+    else:
+        wq = lax.all_gather(wq_own, "dp", axis=0, tiled=True)
+        col = w_fc2.shape[1]
+        both = jnp.concatenate([w_fc2, w_out], axis=0)
+        if col % LANES == 0:
+            parts = dp_n
+            w_cols = lax.all_gather(both, "dp", axis=0, tiled=False)
+        else:
+            parts = 1
+            w_cols = lax.all_gather(both, "dp", axis=1, tiled=True)[None]
+        w_o = w_cols
+        out_first = ff
+        w1 = lax.all_gather(w_fc1, "dp", axis=0, tiled=True)
+        packed = small_gather(jnp.concatenate([v.astype(f32) for v in small]), count, seq_n)
+        packed = packed.reshape(count, ends[-1])
+        gain1, shift1, bias_qv, bias_out, gain2, shift2, bias_up, bias_down = (
+            packed[:, e - n : e].reshape(1, count * n) for e, n in zip(ends, sizes)
+        )
+        own_bias = lambda v, n: lax.dynamic_slice(v, (0, s * n), (1, n))
+        own_up = own_bias(bias_up, ff)
+        qkv_bias = jnp.concatenate(
+            [
+                own_bias(bias_qv[:, :width], inner),
+                jnp.zeros((1, inner), f32),
+                own_bias(bias_qv[:, width:], inner),
+            ],
+            axis=1,
+        )
+        x_pieces = spread(tokens)
+        g_rows = jnp.stack(spread(after(grad_low, x_pieces[3])))
+        h1, qkv = qkv_call(scal, x_pieces, wq, gain1, shift1, qkv_bias)
+        o, lse = attend_call(scal, slopes, qkv, block)
+        near, far = out_call(scal, o, w_o, out_first)
+        got, across = reduce_rows(near, far)
+        mid, h2 = mid_call(tokens, far, got, across, bias_out, gain2, shift2)
+
     h_pieces = spread(h2)
     y_near, y_far, d_near, d_far, a_all, du_all, h_all, g_all, up_sum = mlp_call(
-        h_pieces, g_pieces, w1, w_cols, own_bias(bias_up, ff)
+        h_pieces, g_rows, w1, w_cols, own_up
     )
     got, across = reduce_rows(d_near, d_far)
     grad_down = outer_call(a_all, g_all, parts, "grad_fc2")
@@ -1142,7 +1549,7 @@
         mid + ((y_far[1].astype(f32) + got[0].astype(f32)) + across.astype(f32) + bias_down)
     ).astype(bf16)
 
-    do, grad_out = out_back_call(scal, b_pieces, o, w_cols, ff)
+    do, grad_out = out_back_call(scal, b_pieces, o, w_o, out_first)
     dq, dk, dv = attend_back_call(scal, slopes, qkv, o, do, lse, block)
     near, far, merged, qkv_sums = qkv_back_call(scal, dq, dk, dv, wq)
     grad_qkv = outer_call(h1, merged, 1, "grad_qkv")
@@ -1154,7 +1561,7 @@
 
     grad_down = shared(grad_down if parts > 1 else grad_down)
     grad_up = lax.psum_scatter(grad_up, "dp", scatter_dimension=0, tiled=True).astype(f32)
-    if dp_n == 8 and seq_n == 4 and width == 8 * LANES and ff == width and inner == 2 * LANES:
+    if fast:
         tail = tail_call(
             near, far, tokens, dmid, gain1, grad_qkv.reshape(8, -1, 3 * inner), grad_out,
             mid_sums, up_sum, qkv_sums,

time: 382 us -> 365 us (0.955)
  waiting for transfers between devices: 123 us -> 56.1 us
  Pallas kernels: 203 us -> 261 us
  other arithmetic: 15.1 us -> 10.7 us
  starting transfers between devices: 13.7 us -> 9.36 us
    pallas_call x5 -> x2, Pallas kernels: 52.7 us -> 111 us  [the longest x1 59.4 us: front_call(): pl.pallas_call(front_body, out_shape=(jax.ShapeDtypeStruct((8, *wq.shape)...]
    ppermute x18 -> x10, waiting for transfers between devices: 93 us -> 54.7 us  [swap(): return lax.ppermute(x, 'seq', [(i, i ^ bit) for i in range(4)])]
    all_gather x2 -> x1, waiting for transfers between devices: 30.2 us -> 0.01 us  [on_device(): w_cols = lax.all_gather(w_fc2, 'dp', axis=0, tiled=False)]
    concatenate x2 -> x1, local copies, waits for them, and re-layouts: 0.11 us -> 5.43 us  [on_device(): jnp.concatenate([v.astype(f32) for v in order])]
    ppermute x18 -> x10, starting transfers between devices: 13.3 us -> 9.21 us  [swap(): return lax.ppermute(x, 'seq', [(i, i ^ bit) for i in range(4)])]
  transfers between devices with their start and end apart: 23 -> 14, of which waited for: 12 -> 7; matrix products, arithmetic and copies ran while one was open for 5% -> 5% of each run, Pallas kernels for 42% -> 62%
where the time goes in v3:
time: 365 us; the launch traced here: 364 us
  Pallas kernels  261 us (72%)
  waiting for transfers between devices  56.1 us (15%)
  between operations  14.6 us (4%)
  local copies, waits for them, and re-layouts  12.5 us (3%)
  other arithmetic  10.7 us (3%)
  starting transfers between devices  9.36 us (3%)
    pallas_call x1, Pallas kernels, front_call(): pl.pallas_call(front_body, out_shape=(jax.ShapeDtypeStruct((8, *wq.shape)...  59.4 us
    pallas_call x1, Pallas kernels, tail_call(): pl.pallas_call(tail_body, out_shape=(jax.ShapeDtypeStruct((rows, width),...  57.1 us
    ppermute x10, waiting for transfers between devices, swap(): return lax.ppermute(x, 'seq', [(i, i ^ bit) for i in range(4)])  54.7 us
    pallas_call x1, Pallas kernels, attention_call(): pl.pallas_call(attention_body, out_shape=(jax.ShapeDtypeStruct((keys, wid...  51.5 us
    pallas_call x1, Pallas kernels, mlp_call(): pl.pallas_call(mlp_body, out_shape=(pair, pair, pair, pair, jax.ShapeDtyp...  25.4 us
    pallas_call x3, Pallas kernels, outer_call(): pl.pallas_call(functools.partial(outer_body, blocks=parts > 1), out_shape...  23.7 us
    pallas_call x1, Pallas kernels, attend_back_call(): pl.pallas_call(attend_back_body, out_shape=(jax.ShapeDtypeStruct((keys, w...  21.4 us
    ppermute x10, starting transfers between devices, swap(): return lax.ppermute(x, 'seq', [(i, i ^ bit) for i in range(4)])  9.21 us
  transfers between devices with their start and end apart: 14, of which 7 were waited for; matrix products, arithmetic and copies ran while one was open for 5% of the time, Pallas kernels for 62%

profile of v3, /device:TPU:0, one launch (start us, length us, event | category | flops | bytes accessed | tf_op | source)
XLA Modules:
  0.0 364.4 jit_solution(12160493463489271873)
XLA Ops:
  7.2 0.0 copy-start.10
  7.2 0.0 all-gather.4.cloned.1.call-start
  7.2 0.7 all-gather.4.cloned.1.call-update
  7.9 0.0 all-gather.6.cloned.1.call-start
  8.0 0.7 all-gather.6.cloned.1.call-update
  8.7 0.0 reduce-scatter.3.cloned.1.call-start
  9.4 5.4 %concatenate.8 = bf16[384]{0:T(512)(128)(2,1)S(1)} concatenate(bf16[128]{0:T(256)(128)(2,1)} %param.27, bf16[64]{0:T(256)(128)(2,1)} %param.21, bf16[32]{0:T(256)(128)(2,1)} %param.18, bf16[32]{0:T(256)(128)(2,1)} %param.19, bf16[32]{0:T(256)(128)(2,1)} %param.23, bf16[32]{0:T(256)(128)(2,1)} %param.24, bf16[32]{0:T(256)(128)(2,1)} %param.25, bf16[32]{0:T(256)(128)(2,1)} %param.29), dimensions={0} | concatenate | bytes 1536 | tf_op jit(solution)/shard_map/concatenate | solution.py:1491
  14.8 0.6 reshape.88.small
  15.4 0.6 dynamic_slice.3.slopes
  16.0 0.9 slice_bitcast_fusion.2
  16.9 0.7 pad_maximum_fusion.wq
  17.6 59.4 %front.1 = (bf16[8,128,768]{2,1,0:T(8,128)(2,1)}, bf16[8,256,128]{2,1,0:T(8,128)(2,1)}, bf16[4,384,1024]{2,1,0:T(8,128)(2,1)}, f32[1,1024]{1,0:T(1,128)}, f32[1,...) custom-call(bf16[128,768]{1,0:T(8,128)(2,1)} %pad_maximum_fusion.wq,, ...), custom_call_target="tpu_custom_call" | custom-call | tf_op jit(solution)/shard_map/front/pallas_call | solution.py:1205
  77.0 0.7 pad_add_fusion.scal
  77.6 0.0 copy-done.10
  77.6 1.0 broadcast_select_fusion.g
  78.6 51.5 %attention.1 = (bf16[1536,1024]{1,0:T(8,128)(2,1)}, bf16[1536,768]{1,0:T(8,128)(2,1)}, bf16[1536,256]{1,0:T(8,128)(2,1)}, f32[2,8,1536]{2,1,0:T(8,128)}, f32[384...) custom-call(s32[2]{0:T(128)} %pad_add_fusion.scal, f32[4]{0:T(128)} %dynamic_slice.3.slopes, ...), custom_call_target="tpu_custom_call" | custom-call | tf_op jit(solution)/shard_map/attention/pallas_call | solution.py:1371
  130.2 3.2 collective-permute-start.1
  133.4 0.0 collective-permute-start
  133.4 16.4 %collective-permute-done.1.h2 = bf16[384,1024]{1,0:T(8,128)(2,1)S(1)} collective-permute-done((bf16[384,1024]{1,0:T(8,128)(2,1)}, bf16[384,1024]{1,0:T(8,128)(2,1)S(1)}, u32[]{:S(2)}, u32[]{:S(2)}) %collective-permute-start.1) | collective-permute-done | bytes 786464 | tf_op jit(solution)/shard_map/ppermute | solution.py:155
  149.8 0.0 collective-permute-start.2
  149.8 0.0 collective-permute-done.h1
  149.8 0.0 copy-start.6
  149.8 2.3 collective-permute-done.2.h3
  152.1 0.0 copy-done.5
  152.1 0.8 copy-done.8
  152.9 25.4 %mlp.1 = (bf16[2,384,1024]{2,1,0:T(8,128)(2,1)}, bf16[2,384,1024]{2,1,0:T(8,128)(2,1)}, bf16[2,384,1024]{2,1,0:T(8,128)(2,1)}, bf16[2,384,1024]{2,1,0:T(8,128)(2...) custom-call(bf16[384,1024]{1,0:T(8,128)(2,1)} %get-tuple-element.79., ...), custom_call_target="tpu_custom_call" | custom-call | tf_op jit(solution)/shard_map/mlp/pallas_call | solution.py:517
  178.4 8.2 %grad_fc1.1 = bf16[1024,1024]{1,0:T(8,128)(2,1)} custom-call(bf16[1536,1024]{1,0:T(8,128)(2,1)} %get-tuple-element.118.left, bf16[1536,1024]{1,0:T(8,128)(2,1)} %get-tuple-element.119.right), custom_call_target="tpu_custom_call" | custom-call | tf_op jit(solution)/shard_map/grad_fc1/pallas_call | solution.py:571
  186.6 0.0 reduce-scatter.3.cloned.1.call-update
  186.6 0.0 reduce-scatter.5.cloned.1.call-start
  186.7 0.2 collective-permute-start.3
  186.9 3.5 collective-permute-done.3.b
  190.4 0.0 copy-done.1
  190.4 1.0 fusion.4
  191.4 1.7 collective-permute-start.4
  193.2 8.2 %grad_fc2.1 = bf16[8,1024,128]{2,1,0:T(8,128)(2,1)} custom-call(bf16[1536,1024]{1,0:T(8,128)(2,1)} %get-tuple-element.121.left, bf16[1536,1024]{1,0:T(8,128)(2,1)} %get-tuple-element.122.right), custom_call_target="tpu_custom_call" | custom-call | tf_op jit(solution)/shard_map/grad_fc2/pallas_call | solution.py:571
  201.4 0.0 reduce-scatter.5.cloned.1.call-update
  201.4 9.8 %collective-permute-done.4.c = bf16[384,1024]{1,0:T(8,128)(2,1)S(1)} collective-permute-done((bf16[384,1024]{1,0:T(8,128)(2,1)}, bf16[384,1024]{1,0:T(8,128)(2,1)S(1)}, u32[]{:S(2)}, u32[]{:S(2)}) %collective-permute-start.4) | collective-permute-done | bytes 786464 | tf_op jit(solution)/shard_map/ppermute | solution.py:155
  211.2 0.9 copy-done.11
  212.1 4.6 %mid_back.1 = (f32[384,1024]{1,0:T(8,128)}, bf16[384,1024]{1,0:T(8,128)(2,1)}, f32[8,1024]{1,0:T(8,128)}) custom-call(f32[384,1024]{1,0:T(8,128)} %get-tuple-element.78.mid, bf16[2,384,1024]{2,1,0:T(8,128)(2,1)} %get-tuple-element.84.a, bf16[2,384,1024]{2,1,0:T(8,128)(2,1)} %copy-done.2, bf16[384,1024]{1,0:T(8,128)(2,1)} %copy-done.11, ...), custom_call_target="tpu_custom_call" | custom-call | tf_op jit(solution)/shard_map/mid_back/pallas_call | solution.py:607
  216.7 1.8 collective-permute-start.5
  218.4 17.3 %collective-permute-done.5.b2 = bf16[384,1024]{1,0:T(8,128)(2,1)S(1)} collective-permute-done((bf16[384,1024]{1,0:T(8,128)(2,1)}, bf16[384,1024]{1,0:T(8,128)(2,1)S(1)}, u32[]{:S(2)}, u32[]{:S(2)}) %collective-permute-start.5) | collective-permute-done | bytes 786464 | tf_op jit(solution)/shard_map/ppermute | solution.py:155
  235.8 0.0 collective-permute-start.6
  235.8 2.3 collective-permute-done.6.b3
  238.1 0.1 collective-permute-start.7
  238.2 0.4 collective-permute-start.9
  238.6 3.1 collective-permute-done.7
  241.7 1.2 copy-done.4
  242.9 1.0 fusion.3
  243.9 1.7 collective-permute-start.8
  245.6 0.0 collective-permute-done.9.b1
  245.6 0.0 copy-done.9
  245.6 7.2 %out_back.1 = (bf16[1536,256]{1,0:T(8,128)(2,1)}, bf16[8,256,128]{2,1,0:T(8,128)(2,1)}) custom-call(s32[2]{0:T(128)} %pad_add_fusion.scal, bf16[384,1024]{1,0:T(8,128)(2,1)} %get-tuple-element.86.b0, bf16[384,1024]{1,0:T(8,128)(2,1)} %collective-permute-done.9.b1, bf16[384,1024]{1,0:T(8,128)(2,1)} %copy-done.7, bf16[384,1024]{1,0:T(8,128)(2,1)} %copy-done.9, ...), custom_call_target="tpu_custom_call" | custom-call | tf_op jit(solution)/shard_map/out_back/pallas_call | solution.py:646
  252.9 21.4 %attend_back.1 = (bf16[1536,256]{1,0:T(8,128)(2,1)}, bf16[1536,256]{1,0:T(8,128)(2,1)}, bf16[1536,256]{1,0:T(8,128)(2,1)}) custom-call(s32[2]{0:T(128)} %pad_add_fusion.scal, bf16[1536,768]{1,0:T(8,128)(2,1)} %get-tuple-element.89.q.k.v, bf16[1536,768]{1,0:T(8,128)(2,1)} %get-tuple-element.89.q.k.v, bf16[1536,768]{1,0:T(8,128)(2,1)} %get-tuple-element.89.q.k.v, ...), custom_call_target="tpu_custom_call" | custom-call | tf_op jit(solution)/shard_map/attend_back/pallas_call | solution.py:347
  274.2 8.2 %qkv_back.1 = (bf16[2,384,1024]{2,1,0:T(8,128)(2,1)}, bf16[2,384,1024]{2,1,0:T(8,128)(2,1)}, bf16[1536,768]{1,0:T(8,128)(2,1)}, f32[1,768]{1,0:T(1,128)}) custom-call(s32[2]{0:T(128)} %pad_add_fusion.scal, bf16[1536,256]{1,0:T(8,128)(2,1)} %get-tuple-element.93.dq, bf16[1536,256]{1,0:T(8,128)(2,1)} %get-tuple-element.94.dk, ...), custom_call_target="tpu_custom_call" | custom-call | tf_op jit(solution)/shard_map/qkv_back/pallas_call | solution.py:692
  282.5 7.3 %grad_qkv.1 = bf16[1024,768]{1,0:T(8,128)(2,1)} custom-call(bf16[1536,1024]{1,0:T(8,128)(2,1)} %get-tuple-element.99.left, bf16[1536,768]{1,0:T(8,128)(2,1)} %get-tuple-element.100.right), custom_call_target="tpu_custom_call" | custom-call | tf_op jit(solution)/shard_map/grad_qkv/pallas_call | solution.py:571
  289.7 57.1 %tail.1 = (bf16[384,1024]{1,0:T(8,128)(2,1)}, f32[128,768]{1,0:T(8,128)}, f32[256,128]{1,0:T(8,128)}, f32[16,128]{1,0:T(8,128)}) custom-call(bf16[2,384,1024]{2,1,0:T(8,128)(2,1)} %get-tuple-element.96.near, bf16[2,384,1024]{2,1,0:T(8,128)(2,1)} %get-tuple-element.97.far, bf16[384,1024]{1,0:T(8,128)(2,1)} %x.3, f32[384,1024]{1,0:T(8,128)} %get-tuple-element.98.dmid, ...), custom_call_target="tpu_custom_call" | custom-call | tf_op jit(solution)/shard_map/tail/pallas_call | solution.py:981
  346.8 2.7 finish.1
  349.5 0.0 copy-start
  349.5 0.0 copy-start.12
  349.6 2.0 copy.29
  351.5 1.8 convert_element_type.39
  353.3 1.8 bitcast_convert_fusion
  355.1 0.0 collective-permute-done.8
  355.1 2.8 fusion.2
  (21 shorter events, 0.0 us)
Async XLA Ops:
  7.2 70.5 %copy-start.10 = (bf16[384,1024]{1,0:T(8,128)(2,1)S(1)}, bf16[384,1024]{1,0:T(8,128)(2,1)}, u32[]{:S(2)}) copy-start(bf16[384,1024]{1,0:T(8,128)(2,1)} %param.17) | copy-start | bytes 2359300
  7.2 144.9 %all-gather.4.cloned.1.call-start = ((), (), s32[]{:S(2)}) async-start(), calls=%async_computation.2 | async-start | bytes 2359296 | tf_op jit(solution)/shard_map/all_gather | solution.py:1486
  7.9 144.1 %all-gather.6.cloned.1.call-start = ((), (), s32[]{:S(2)}) async-start(), calls=%async_computation.5 | async-start | bytes 2359296 | tf_op jit(solution)/shard_map/all_gather | solution.py:1487
  8.7 342.9 %reduce-scatter.3.cloned.1.call-start = ((), (), s32[]{:S(2)}) async-start(), calls=%async_computation.3 | async-start | bytes 2359296 | tf_op jit(solution)/shard_map/reduce_scatter | solution.py:1563
  130.2 19.6 %collective-permute-start.1 = (bf16[384,1024]{1,0:T(8,128)(2,1)}, bf16[384,1024]{1,0:T(8,128)(2,1)S(1)}, u32[]{:S(2)}, u32[]{:S(2)}) collective-permute-start(bf16[384,1024]{1,0:T(8,128)(2,1)} %get-tuple-element.79.h0), channel_id=1, source_target_pairs={{0,2},{1,3},{2,0},{3,1},{4,6},{5,7},{6,4},{7,5},{8,10},{9,11},{10,... | collective-permute-start | bytes 2359304 | tf_op jit(solution)/shard_map/ppermute | solution.py:155
  133.4 16.4 %collective-permute-start = (bf16[384,1024]{1,0:T(8,128)(2,1)}, bf16[384,1024]{1,0:T(8,128)(2,1)S(1)}, u32[]{:S(2)}, u32[]{:S(2)}) collective-permute-start(bf16[384,1024]{1,0:T(8,128)(2,1)} %get-tuple-element.79.h0), channel_id=1, source_target_pairs={{0,1},{1,0},{2,3},{3,2},{4,5},{5,4},{6,7},{7,6},{8,9},{9,8},{10,11... | collective-permute-start | bytes 2359304 | tf_op jit(solution)/shard_map/ppermute | solution.py:155
  149.8 2.3 copy-start.5
  149.8 2.3 collective-permute-start.2
  149.8 2.3 copy-start.6
  152.1 0.9 copy-start.8
  186.6 3.8 %copy-start.1 = (bf16[2,384,1024]{2,1,0:T(8,128)(2,1)S(1)}, bf16[2,384,1024]{2,1,0:T(8,128)(2,1)}, u32[]{:S(2)}) copy-start(bf16[2,384,1024]{2,1,0:T(8,128)(2,1)} %get-tuple-element.84.a) | copy-start | bytes 4718596
  186.6 166.7 %reduce-scatter.5.cloned.1.call-start = ((), (), s32[]{:S(2)}) async-start(), calls=%async_computation.4 | async-start | bytes 2359296 | tf_op jit(solution)/shard_map/reduce_scatter | solution.py:1559
  186.7 3.7 %collective-permute-start.3 = (bf16[2,384,1024]{2,1,0:T(8,128)(2,1)}, bf16[2,384,1024]{2,1,0:T(8,128)(2,1)S(1)}, u32[]{:S(2)}, u32[]{:S(2)}) collective-permute-start(bf16[2,384,1024]{2,1,0:T(8,128)(2,1)} %get-tuple-element.85), channel_id=1, source_target_pairs={{0,1},{1,0},{2,3},{3,2},{4,5},{5,4},{6,7},{7,6},{8,9},{9,8},{10,11... | collective-permute-start | bytes 4718600 | tf_op jit(solution)/shard_map/ppermute | solution.py:155
  190.4 11.0 %copy-start.2 = (bf16[2,384,1024]{2,1,0:T(8,128)(2,1)}, bf16[2,384,1024]{2,1,0:T(8,128)(2,1)S(1)}, u32[]{:S(2)}) copy-start(bf16[2,384,1024]{2,1,0:T(8,128)(2,1)S(1)} %collective-permute-done.3.b) | copy-start | bytes 4718596
  191.4 19.8 %collective-permute-start.4 = (bf16[384,1024]{1,0:T(8,128)(2,1)}, bf16[384,1024]{1,0:T(8,128)(2,1)S(1)}, u32[]{:S(2)}, u32[]{:S(2)}) collective-permute-start(bf16[384,1024]{1,0:T(8,128)(2,1)} %fusion.4), channel_id=1, source_target_pairs={{0,2},{1,3},{2,0},{3,1},{4,6},{5,7},{6,4},{7,5},{8,10},{9,11},{10,... | collective-permute-start | bytes 2359304 | tf_op jit(solution)/shard_map/ppermute | solution.py:155
  211.2 0.9 copy-start.11
  212.1 30.8 %copy-start.3 = (bf16[2,384,1024]{2,1,0:T(8,128)(2,1)S(1)}, bf16[2,384,1024]{2,1,0:T(8,128)(2,1)}, u32[]{:S(2)}) copy-start(bf16[2,384,1024]{2,1,0:T(8,128)(2,1)} %get-tuple-element.82) | copy-start | bytes 4718596
  216.7 19.1 %collective-permute-start.5 = (bf16[384,1024]{1,0:T(8,128)(2,1)}, bf16[384,1024]{1,0:T(8,128)(2,1)S(1)}, u32[]{:S(2)}, u32[]{:S(2)}) collective-permute-start(bf16[384,1024]{1,0:T(8,128)(2,1)} %get-tuple-element.86.b0), channel_id=1, source_target_pairs={{0,2},{1,3},{2,0},{3,1},{4,6},{5,7},{6,4},{7,5},{8,10},{9,11},{10,... | collective-permute-start | bytes 2359304 | tf_op jit(solution)/shard_map/ppermute | solution.py:155
  235.8 9.8 %copy-start.7 = (bf16[384,1024]{1,0:T(8,128)(2,1)}, bf16[384,1024]{1,0:T(8,128)(2,1)S(1)}, u32[]{:S(2)}) copy-start(bf16[384,1024]{1,0:T(8,128)(2,1)S(1)} %collective-permute-done.5.b2) | copy-start | bytes 2359300
  235.8 2.3 collective-permute-start.6
  238.1 7.6 %copy-start.9 = (bf16[384,1024]{1,0:T(8,128)(2,1)}, bf16[384,1024]{1,0:T(8,128)(2,1)S(1)}, u32[]{:S(2)}) copy-start(bf16[384,1024]{1,0:T(8,128)(2,1)S(1)} %collective-permute-done.6.b3) | copy-start | bytes 2359300
  238.1 3.6 collective-permute-start.7
  238.2 7.4 %collective-permute-start.9 = (bf16[384,1024]{1,0:T(8,128)(2,1)}, bf16[384,1024]{1,0:T(8,128)(2,1)}, u32[]{:S(2)}, u32[]{:S(2)}) collective-permute-start(bf16[384,1024]{1,0:T(8,128)(2,1)} %get-tuple-element.86.b0), channel_id=1, source_target_pairs={{0,1},{1,0},{2,3},{3,2},{4,5},{5,4},{6,7},{7,6},{8,9},{9,8},{10,11... | collective-permute-start | bytes 2359304 | tf_op jit(solution)/shard_map/ppermute | solution.py:155
  241.7 1.2 copy-start.4
  243.9 111.2 %collective-permute-start.8 = (bf16[384,1024]{1,0:T(8,128)(2,1)}, bf16[384,1024]{1,0:T(8,128)(2,1)}, u32[]{:S(2)}, u32[]{:S(2)}) collective-permute-start(bf16[384,1024]{1,0:T(8,128)(2,1)} %fusion.3), channel_id=1, source_target_pairs={{0,2},{1,3},{2,0},{3,1},{4,6},{5,7},{6,4},{7,5},{8,10},{9,11},{10,... | collective-permute-start | bytes 2359304 | tf_op jit(solution)/shard_map/ppermute | solution.py:155
  349.5 5.6 %copy-start = (f32[384,1024]{1,0:T(8,128)S(1)}, f32[384,1024]{1,0:T(8,128)}, u32[]{:S(2)}) copy-start(f32[384,1024]{1,0:T(8,128)} %get-tuple-element.78.mid) | copy-start | bytes 4718596
  349.5 5.6 %copy-start.12 = (f32[1,1024]{1,0:T(1,128)S(1)}, f32[1,1024]{1,0:T(1,128)}, u32[]{:S(2)}) copy-start(f32[1,1024]{1,0:T(1,128)} %get-tuple-element.88) | copy-start | bytes 12292
Sparse Core Ops, SparseCore 0:
  10.1 67.6 all-gather.3
  80.0 48.1 all-gather.5
  186.8 67.9 reduce-scatter.2
  258.2 72.1 reduce-scatter.4

commit v4 on v3

--- a/solution.py
+++ b/solution.py
@@ -1128,9 +1128,9 @@
 
 
 def front_body(
-    wq, wo, x, small,
+    wq, wo, x, v_up, v_qv, v_g1, v_s1, v_out, v_g2, v_s2, v_down,
     wq_all, wo_all, x_rows, gain1, shift1, bias_qkv, bias_out, gain2, shift2, bias_up, bias_down,
-    vectors, q_sem, o_sem, x_sem, seq_sem, dp_sem, keep_sem,
+    small, vectors, q_sem, o_sem, x_sem, seq_sem, dp_sem, keep_sem,
 ):
     dp, seq = lax.axis_index("dp"), lax.axis_index("seq")
     greet([((dp + i) % 8, seq) for i in range(1, 8)] + [(dp, p) for p in neighbours(seq)])
@@ -1141,6 +1141,10 @@
     gather_q.start()
     keep_x = pltpu.make_async_copy(x, x_rows.at[0], keep_sem.at[0])
     keep_x.start()
+    at = 0
+    for ref in (v_up, v_qv, v_g1, v_s1, v_out, v_g2, v_s2, v_down):
+        small[:, at : at + ref.shape[1]] = ref[...].astype(f32)
+        at += ref.shape[1]
     keep_v = pltpu.make_async_copy(small, vectors.at[dp, seq], keep_sem.at[1])
     keep_v.start()
     group = [
@@ -1199,6 +1203,7 @@
 
 
 def front_call(wq, wo, x, small):
+    count = sum(v.shape[0] for v in small)
     rows, width = x.shape
     one = lambda n: jax.ShapeDtypeStruct((1, n), f32)
     sem = pltpu.SemaphoreType.DMA
@@ -1211,10 +1216,11 @@
             one(width), one(width), one(wq.shape[1]), one(width), one(width), one(width),
             one(width), one(width),
         ),
-        in_specs=[WHOLE] * 4,
+        in_specs=[WHOLE] * 11,
         out_specs=(WHOLE,) * 11,
         scratch_shapes=[
-            pltpu.VMEM((8, 4, 1, small.shape[-1]), f32),
+            pltpu.VMEM((1, count), f32),
+            pltpu.VMEM((8, 4, 1, count), f32),
             Gather.scratch(),
             Gather.scratch(),
             sem((2, 4)),
@@ -1224,21 +1230,24 @@
         ],
         compiler_params=params(collective_id=4, has_side_effects=True),
         name="front",
-    )(wq, wo, x, small.reshape(1, -1))
+    )(wq, wo, x, *(v.reshape(1, -1) for v in small))
 
 
 def attention_body(
-    scal, slopes, x_rows, g, wq, wo, gain1, shift1, bias_qkv, bias_out, gain2, shift2,
-    h1, qkv, o, lse, mid, h2, g_rows,
-    bias, vt, flat, part, land_c, sum_y, land_y, g_sem, row_sems, keep_sem,
+    scal, slopes, x_rows, g, wq, wo, w1, w2, gain1, shift1, bias_qkv, bias_out, gain2, shift2,
+    h1, qkv, o, lse, mid, h2, g_rows, w1_all, w2_all,
+    bias, vt, flat, part, land_c, sum_y, land_y, g_sem, row_sems, keep_sem, w1_sem, w2_sem,
 ):
     dp, seq = lax.axis_index("dp"), lax.axis_index("seq")
     mate, across, _ = neighbours(seq)
-    greet([(dp, mate), (dp, across)])
+    greet([((dp + i) % 8, seq) for i in range(1, 8)] + [(dp, mate), (dp, across)])
     rows, width = g.shape
     keys = qkv.shape[0]
     inner = o.shape[1]
     pairs = inner // LANES
+    gathers = [Gather(w1, w1_all, w1_sem, dp, seq), Gather(w2, w2_all, w2_sem, dp, seq)]
+    for gather in gathers:
+        gather.start()
     spread_g = Spread(g, g_rows, g_sem, dp, seq)
     spread_g.start()
     keep = pltpu.make_async_copy(g, g_rows.at[0], keep_sem.at[0])
@@ -1266,6 +1275,8 @@
         return carry
 
     lax.fori_loop(0, pairs, prepare, 0)
+    for gather in gathers:
+        gather.hop(1)
     spread_g.forward()
 
     cores = [
@@ -1319,10 +1330,14 @@
                 total = part[2, at, :].astype(f32) + land_c[1, at, :].astype(f32)
                 sum_y[at, :] = total.astype(bf16)
             over.start()
+            for gather in gathers:
+                gather.hop(2)
 
         @pl.when(t == 2)
         def _():
             cores[0].start()
+            for gather in gathers:
+                gather.hop(3)
 
         return carry
 
@@ -1342,6 +1357,8 @@
         return carry
 
     lax.fori_loop(0, rows // chunk, second_norm, 0)
+    for gather in gathers:
+        gather.finish()
     spread_g.near.wait_recv()
     spread_g.last.wait_recv()
     spread_g.drain()
@@ -1362,7 +1379,7 @@
     return jnp.concatenate([s[: length - block], last], axis=0)
 
 
-def attention_call(scal, slopes, x_rows, g, wq, wo, *vectors):
+def attention_call(scal, slopes, x_rows, g, wq, wo, w1, w2, *vectors):
     rows, width = g.shape
     keys = 4 * rows
     inner = wo.shape[1]
@@ -1378,9 +1395,11 @@
             jax.ShapeDtypeStruct((rows, width), f32),
             jax.ShapeDtypeStruct((rows, width), bf16),
             jax.ShapeDtypeStruct((4, rows, width), bf16),
-        ),
-        in_specs=[SCALAR, SCALAR] + [WHOLE] * (4 + len(vectors)),
-        out_specs=(WHOLE,) * 7,
+            jax.ShapeDtypeStruct((8, *w1.shape), bf16),
+            jax.ShapeDtypeStruct((8, *w2.shape), bf16),
+        ),
+        in_specs=[SCALAR, SCALAR] + [WHOLE] * (6 + len(vectors)),
+        out_specs=(WHOLE,) * 9,
         scratch_shapes=[
             pltpu.VMEM((2 * pairs, keys, LANES), f32),
             pltpu.VMEM((pairs, LANES, keys), bf16),
@@ -1392,10 +1411,175 @@
             sem((2, 4)),
             sem((2, 3)),
             sem((1,)),
+            Gather.scratch(),
+            Gather.scratch(),
         ],
         compiler_params=params(collective_id=5, has_side_effects=True),
         name="attention",
-    )(scal, slopes, x_rows, g, wq, wo, *vectors)
+    )(scal, slopes, x_rows, g, wq, wo, w1, w2, *vectors)
+
+
+def feed_body(
+    h2, g_rows, w1, w2, b1, mid, gain2,
+    y_near, y_far, gw1, gw2, dmid, dbr, sums, up_sum,
+    h_rows, a_all, du_all, flat, part, land_c, sum_y, land_y, turned, h_sem, row_sems, keep_sem,
+):
+    dp, seq = lax.axis_index("dp"), lax.axis_index("seq")
+    mate, across, _ = neighbours(seq)
+    greet([(dp, mate), (dp, across)])
+    rows, width = h2.shape
+    inner = w1.shape[1]
+    spread_h = Spread(h2, h_rows, h_sem, dp, seq)
+    spread_h.start()
+    keep = pltpu.make_async_copy(h2, h_rows.at[0], keep_sem.at[0])
+    keep.start()
+    lay_columns(w2, 0, flat)
+    up_sum[...] = jnp.zeros_like(up_sum)
+    sums[...] = jnp.zeros_like(sums)
+    keep.wait()
+    cores = [
+        remote(part.at[r], land_c.at[k], row_sems.at[0, k], row_sems.at[1, k], dp, mate)
+        for k, r in ((0, 1), (1, 3))
+    ]
+    over = remote(sum_y, land_y, row_sems.at[0, 2], row_sems.at[1, 2], dp, across)
+    chunk = 256
+
+    def block(t, carry):
+        @pl.when(t == 1)
+        def _():
+            spread_h.near.wait_recv()
+
+        @pl.when(t == 2)
+        def _():
+            spread_h.forward()
+
+        @pl.when(t == 3)
+        def _():
+            spread_h.last.wait_recv()
+
+        at = pl.ds(pl.multiple_of(t * rows, rows), rows)
+        for c in range(inner // chunk):
+            cols = slice(c * chunk, (c + 1) * chunk)
+            u = mm(h_rows[t], w1[:, cols]) + b1[:, cols]
+            value, slope = gelu_parts(u)
+            a_all[at, cols] = value.astype(bf16)
+            du = (mm_t(g_rows[t], flat[cols, :]) * slope).astype(bf16)
+            du_all[at, cols] = du
+            up_sum[:, cols] += jnp.sum(du.astype(f32), axis=0, keepdims=True)
+        y = mm(a_all[at, :], flat[...]).astype(bf16)
+        part[t] = mm_t(du_all[at, :], w1[...]).astype(bf16)
+        for r, (ref, k) in enumerate(((y_far, 1), (y_near, 0), (y_far, 0), (y_near, 1))):
+
+            @pl.when(t == r)
+            def _(ref=ref, k=k):
+                ref[k] = y
+
+        @pl.when(t == 1)
+        def _():
+            cores[0].start()
+
+        @pl.when(t == 3)
+        def _():
+            cores[1].start()
+
+        return carry
+
+    lax.fori_loop(0, 4, block, 0)
+
+    def turn(load):
+        def step(i, carry):
+            turned[:, pl.ds(pl.multiple_of(i * rows, rows), rows)] = load(i).T
+            return carry
+
+        lax.fori_loop(0, 4, step, 0)
+
+    turn(lambda i: h_rows[i])
+
+    def outer_up(j, carry):
+        cols = pl.ds(pl.multiple_of(j * chunk, chunk), chunk)
+        gw1[:, cols] = mm(turned[...], du_all[:, cols]).astype(bf16)
+        return carry
+
+    lax.fori_loop(0, 1, outer_up, 0)
+    cores[1].wait_recv()
+    small = 128
+    for i in range(rows // small):
+        at = slice(i * small, (i + 1) * small)
+        total = part[2, at, :].astype(f32) + land_c[1, at, :].astype(f32)
+        sum_y[at, :] = total.astype(bf16)
+    over.start()
+    lax.fori_loop(1, inner // chunk, outer_up, 0)
+    turn(lambda i: a_all[pl.ds(pl.multiple_of(i * rows, rows), rows), :])
+
+    def outer_down(j, carry):
+        cols = pl.ds(pl.multiple_of(j * chunk, chunk), chunk)
+        right = g_rows[:, :, cols].reshape(4 * rows, chunk)
+        grad = mm(turned[...], right).astype(bf16)
+        gw2[2 * j] = grad[:, :LANES]
+        gw2[2 * j + 1] = grad[:, LANES:]
+        return carry
+
+    lax.fori_loop(0, width // chunk, outer_down, 0)
+    cores[0].wait_recv()
+    over.wait_recv()
+
+    def norm_step(i, carry):
+        at = pl.ds(pl.multiple_of(i * small, small), small)
+        unit, inv = normalize(mid[at, :])
+        e = (part[0, at, :].astype(f32) + land_c[0, at, :].astype(f32)) + land_y[at, :].astype(f32)
+        grad = g_rows[0, at, :].astype(f32)
+        value = grad + norm_back(e, gain2[...], unit, inv)
+        dmid[at, :] = value
+        low = value.astype(bf16)
+        dbr[at, :] = low
+        sums[0:1, :] += jnp.sum(e * unit, axis=0, keepdims=True)
+        sums[1:2, :] += jnp.sum(e, axis=0, keepdims=True)
+        sums[2:3, :] += jnp.sum(low.astype(f32), axis=0, keepdims=True)
+        sums[3:4, :] += jnp.sum(grad, axis=0, keepdims=True)
+        return carry
+
+    lax.fori_loop(0, rows // small, norm_step, 0)
+    spread_h.drain()
+    for copy in cores + [over]:
+        copy.wait_send()
+
+
+def feed_call(h2, g_rows, w1, w2, b1, mid, gain2):
+    rows, width = h2.shape
+    inner = w1.shape[1]
+    sem = pltpu.SemaphoreType.DMA
+    pair = jax.ShapeDtypeStruct((2, rows, width), bf16)
+    return pl.pallas_call(
+        feed_body,
+        out_shape=(
+            pair,
+            pair,
+            jax.ShapeDtypeStruct((width, inner), bf16),
+            jax.ShapeDtypeStruct(w2.shape, bf16),
+            jax.ShapeDtypeStruct((rows, width), f32),
+            jax.ShapeDtypeStruct((rows, width), bf16),
+            jax.ShapeDtypeStruct((8, width), f32),
+            jax.ShapeDtypeStruct((1, inner), f32),
+        ),
+        in_specs=[WHOLE] * 7,
+        out_specs=(WHOLE,) * 8,
+        scratch_shapes=[
+            pltpu.VMEM((4, rows, width), bf16),
+            pltpu.VMEM((4 * rows, inner), bf16),
+            pltpu.VMEM((4 * rows, inner), bf16),
+            pltpu.VMEM((inner, width), bf16),
+            pltpu.VMEM((4, rows, width), bf16),
+            pltpu.VMEM((2, rows, width), bf16),
+            pltpu.VMEM((rows, width), bf16),
+            pltpu.VMEM((rows, width), bf16),
+            pltpu.VMEM((width, 4 * rows), bf16),
+            sem((2, 4)),
+            sem((2, 3)),
+            sem((1,)),
+        ],
+        compiler_params=params(collective_id=6, has_side_effects=True),
+        name="feed_forward",
+    )(h2, g_rows, w1, w2, b1, mid, gain2)
 
 
 def finish_body(
@@ -1483,20 +1667,19 @@
     fast = dp_n == 8 and seq_n == 4 and width == 8 * LANES and ff == width and inner == 2 * LANES
     if fast:
         parts = dp_n
-        w1 = lax.all_gather(w_fc1, "dp", axis=0, tiled=True)
-        w_cols = lax.all_gather(w_fc2, "dp", axis=0, tiled=False)
         order = (b_fc1, b_qv, ln1_gain, ln1_shift, b_out, ln2_gain, ln2_shift, b_fc2)
         wq, w_o, x_rows, gain1, shift1, qkv_bias, bias_out, gain2, shift2, own_up, bias_down = (
-            front_call(
-                wq_own, w_out, tokens, jnp.concatenate([v.astype(f32) for v in order])
-            )
+            front_call(wq_own, w_out, tokens, order)
         )
         wq = wq.reshape(width, 3 * inner)
-        h1, qkv, o, lse, mid, h2, g_rows = attention_call(
-            scal, slopes, x_rows, grad_low, wq, w_o,
+        h1, qkv, o, lse, mid, h2, g_rows, w1, w_cols = attention_call(
+            scal, slopes, x_rows, grad_low, wq, w_o, w_fc1, w_fc2,
             gain1, shift1, qkv_bias, bias_out, gain2, shift2,
         )
         out_first = 0
+        y_near, y_far, grad_up, grad_down, dmid, dbr, mid_sums, up_sum = feed_call(
+            h2, g_rows, w1.reshape(width, ff), w_cols, own_up, mid, gain2
+        )
     else:
         wq = lax.all_gather(wq_own, "dp", axis=0, tiled=True)
         col = w_fc2.shape[1]
@@ -1532,15 +1715,15 @@
         near, far = out_call(scal, o, w_o, out_first)
         got, across = reduce_rows(near, far)
         mid, h2 = mid_call(tokens, far, got, across, bias_out, gain2, shift2)
-
-    h_pieces = spread(h2)
-    y_near, y_far, d_near, d_far, a_all, du_all, h_all, g_all, up_sum = mlp_call(
-        h_pieces, g_rows, w1, w_cols, own_up
-    )
-    got, across = reduce_rows(d_near, d_far)
-    grad_down = outer_call(a_all, g_all, parts, "grad_fc2")
-    grad_up = outer_call(h_all, du_all, 1, "grad_fc1")
-    dmid, dbr, mid_sums = mid_back_call(mid, d_far, got, across, grad_low, gain2)
+        h_pieces = spread(h2)
+        y_near, y_far, d_near, d_far, a_all, du_all, h_all, g_all, up_sum = mlp_call(
+            h_pieces, g_rows, w1, w_cols, own_up
+        )
+        got, across = reduce_rows(d_near, d_far)
+        grad_down = outer_call(a_all, g_all, parts, "grad_fc2")
+        grad_up = outer_call(h_all, du_all, 1, "grad_fc1")
+        dmid, dbr, mid_sums = mid_back_call(mid, d_far, got, across, grad_low, gain2)
+
     b_pieces = spread(dbr)
 
     y_near = after(y_near, b_pieces[3])

time: 365 us -> 331 us (0.907)
  waiting for transfers between devices: 56.1 us -> 25.5 us
  Pallas kernels: 261 us -> 272 us
  starting transfers between devices: 9.36 us -> 0.88 us
  local copies, waits for them, and re-layouts: 12.5 us -> 6.47 us
    ppermute x10 -> x5, waiting for transfers between devices: 54.7 us -> 24.5 us  [swap(): return lax.ppermute(x, 'seq', [(i, i ^ bit) for i in range(4)])]
    pallas_call x2 -> x1, Pallas kernels: 30 us -> 58.6 us  [feed_call(): pl.pallas_call(feed_body, out_shape=(pair, pair, jax.ShapeDtypeStruct((wi...]
    pallas_call x3 -> x1, Pallas kernels: 23.7 us -> 7.18 us  [outer_call(): pl.pallas_call(functools.partial(outer_body, blocks=parts > 1), out_shape...]
    pallas_call x1, Pallas kernels: 59.4 us -> 48.2 us  [front_call(): pl.pallas_call(front_body, out_shape=(jax.ShapeDtypeStruct((8, *wq.shape)...]
    pallas_call x1, Pallas kernels: 51.5 us -> 60 us  [attention_call(): pl.pallas_call(attention_body, out_shape=(jax.ShapeDtypeStruct((keys, wid...]
    ppermute x10 -> x5, starting transfers between devices: 9.21 us -> 0.8 us  [swap(): return lax.ppermute(x, 'seq', [(i, i ^ bit) for i in range(4)])]
    concatenate x1 -> x0, local copies, waits for them, and re-layouts: 5.43 us -> none  [on_device(): jnp.concatenate([v.astype(f32) for v in order])]
  transfers between devices with their start and end apart: 14 -> 7, of which waited for: 7 -> 4; matrix products, arithmetic and copies ran while one was open for 5% -> 2% of each run, Pallas kernels for 62% -> 32%
where the time goes in v4:
time: 331 us; the launch traced here: 330 us
  Pallas kernels  272 us (82%)
  waiting for transfers between devices  25.5 us (8%)
  between operations  14.8 us (4%)
  other arithmetic  10.8 us (3%)
  local copies, waits for them, and re-layouts  6.47 us (2%)
    pallas_call x1, Pallas kernels, attention_call(): pl.pallas_call(attention_body, out_shape=(jax.ShapeDtypeStruct((keys, wid...  60 us
    pallas_call x1, Pallas kernels, feed_call(): pl.pallas_call(feed_body, out_shape=(pair, pair, jax.ShapeDtypeStruct((wi...  58.6 us
    pallas_call x1, Pallas kernels, tail_call(): pl.pallas_call(tail_body, out_shape=(jax.ShapeDtypeStruct((rows, width),...  58.1 us
    pallas_call x1, Pallas kernels, front_call(): pl.pallas_call(front_body, out_shape=(jax.ShapeDtypeStruct((8, *wq.shape)...  48.2 us
    ppermute x5, waiting for transfers between devices, swap(): return lax.ppermute(x, 'seq', [(i, i ^ bit) for i in range(4)])  24.5 us
    pallas_call x1, Pallas kernels, attend_back_call(): pl.pallas_call(attend_back_body, out_shape=(jax.ShapeDtypeStruct((keys, w...  21.2 us
    pallas_call x1, Pallas kernels, qkv_back_call(): pl.pallas_call(qkv_back_body, out_shape=(jax.ShapeDtypeStruct((2, rows, w...  8.22 us
    pallas_call x1, Pallas kernels, out_back_call(): pl.pallas_call(functools.partial(out_back_body, first=first), out_shape=(...  7.51 us
  transfers between devices with their start and end apart: 7, of which 4 were waited for; matrix products, arithmetic and copies ran while one was open for 2% of the time, Pallas kernels for 32%

profile of v4, /device:TPU:0, one launch (start us, length us, event | category | flops | bytes accessed | tf_op | source)
XLA Modules:
  0.0 330.3 jit_solution(18387884296173670383)
XLA Ops:
  7.2 0.0 reduce-scatter.5.cloned.1.call-start
  7.9 0.9 slice_bitcast_fusion.2
  8.8 0.6 pad_add_fusion.scal
  9.4 0.6 dynamic_slice.3.slopes
  10.0 2.1 broadcast_select_fusion.g
  12.1 0.7 pad_maximum_fusion.wq
  12.8 48.2 %front.1 = (bf16[8,128,768]{2,1,0:T(8,128)(2,1)}, bf16[8,256,128]{2,1,0:T(8,128)(2,1)}, bf16[4,384,1024]{2,1,0:T(8,128)(2,1)}, f32[1,1024]{1,0:T(1,128)}, f32[1,...) custom-call(bf16[128,768]{1,0:T(8,128)(2,1)} %pad_maximum_fusion.wq,, ...), custom_call_target="tpu_custom_call" | custom-call | tf_op jit(solution)/shard_map/front/pallas_call | solution.py:1210
  61.1 60.0 %attention.1 = (bf16[1536,1024]{1,0:T(8,128)(2,1)}, bf16[1536,768]{1,0:T(8,128)(2,1)}, bf16[1536,256]{1,0:T(8,128)(2,1)}, f32[2,8,1536]{2,1,0:T(8,128)}, f32[384...) custom-call(s32[2]{0:T(128)} %pad_add_fusion.scal, ...), custom_call_target="tpu_custom_call" | custom-call | tf_op jit(solution)/shard_map/attention/pallas_call | solution.py:1388
  121.1 58.6 %feed_forward.1 = (bf16[2,384,1024]{2,1,0:T(8,128)(2,1)}, bf16[2,384,1024]{2,1,0:T(8,128)(2,1)}, bf16[1024,1024]{1,0:T(8,128)(2,1)}, bf16[8,1024,128]{2,1,0:T(8,...) custom-call(bf16[384,1024]{1,0:T(8,128)(2,1)} %get-tuple-element.77.h2, ...), custom_call_target="tpu_custom_call" | custom-call | tf_op jit(solution)/shard_map/feed_forward/pallas_call | solution.py:1552
  179.7 0.0 copy-start.3
  179.7 0.0 reduce-scatter.5.cloned.1.call-update
  179.7 0.0 copy-start.1
  179.8 0.0 reduce-scatter.3.cloned.1.call-start
  179.8 1.0 copy-done.3
  180.8 0.0 collective-permute-start
  180.8 0.0 reduce-scatter.3.cloned.1.call-update
  180.9 19.1 %collective-permute-done.b2 = bf16[384,1024]{1,0:T(8,128)(2,1)S(1)} collective-permute-done((bf16[384,1024]{1,0:T(8,128)(2,1)S(1)}, bf16[384,1024]{1,0:T(8,128)(2,1)S(1)}, u32[]{:S(2)}, u32[]{:S(2)}) %collective-permute-start) | collective-permute-done | bytes 786464 | tf_op jit(solution)/shard_map/ppermute | solution.py:155
  200.0 0.0 copy-start.4
  200.0 0.0 collective-permute-start.1
  200.0 2.3 collective-permute-done.1.b3
  202.3 0.0 copy-start.5
  202.3 0.1 collective-permute-start.2
  202.4 0.4 collective-permute-start.4
  202.8 3.1 collective-permute-done.2
  205.9 0.0 copy-done.5
  205.9 0.0 copy-start.2
  205.9 1.2 copy-done.2
  207.1 0.0 copy-done.1
  207.1 1.0 fusion.3
  208.0 0.3 collective-permute-start.3
  208.3 0.0 collective-permute-done.4.b1
  208.3 0.0 copy-start.6
  208.3 0.9 copy-done.6
  209.2 0.0 copy-done.4
  209.2 7.5 %out_back.1 = (bf16[1536,256]{1,0:T(8,128)(2,1)}, bf16[8,256,128]{2,1,0:T(8,128)(2,1)}) custom-call(s32[2]{0:T(128)} %pad_add_fusion.scal, bf16[384,1024]{1,0:T(8,128)(2,1)} %get-tuple-element.84.b0, bf16[384,1024]{1,0:T(8,128)(2,1)} %copy-done.6, bf16[384,1024]{1,0:T(8,128)(2,1)} %copy-done.4, bf16[384,1024]{1,0:T(8,128)(2,1)} %copy-done.5, ...), custom_call_target="tpu_custom_call" | custom-call | tf_op jit(solution)/shard_map/out_back/pallas_call | solution.py:646
  216.7 21.2 %attend_back.1 = (bf16[1536,256]{1,0:T(8,128)(2,1)}, bf16[1536,256]{1,0:T(8,128)(2,1)}, bf16[1536,256]{1,0:T(8,128)(2,1)}) custom-call(s32[2]{0:T(128)} %pad_add_fusion.scal, bf16[1536,768]{1,0:T(8,128)(2,1)} %get-tuple-element.87.q.k.v, bf16[1536,768]{1,0:T(8,128)(2,1)} %get-tuple-element.87.q.k.v, bf16[1536,768]{1,0:T(8,128)(2,1)} %get-tuple-element.87.q.k.v, ...), custom_call_target="tpu_custom_call" | custom-call | tf_op jit(solution)/shard_map/attend_back/pallas_call | solution.py:347
  237.9 8.2 %qkv_back.1 = (bf16[2,384,1024]{2,1,0:T(8,128)(2,1)}, bf16[2,384,1024]{2,1,0:T(8,128)(2,1)}, bf16[1536,768]{1,0:T(8,128)(2,1)}, f32[1,768]{1,0:T(1,128)}) custom-call(s32[2]{0:T(128)} %pad_add_fusion.scal, bf16[1536,256]{1,0:T(8,128)(2,1)} %get-tuple-element.91.dq, bf16[1536,256]{1,0:T(8,128)(2,1)} %get-tuple-element.92.dk, ...), custom_call_target="tpu_custom_call" | custom-call | tf_op jit(solution)/shard_map/qkv_back/pallas_call | solution.py:692
  246.1 7.2 %grad_qkv.1 = bf16[1024,768]{1,0:T(8,128)(2,1)} custom-call(bf16[1536,1024]{1,0:T(8,128)(2,1)} %get-tuple-element.97.left, bf16[1536,768]{1,0:T(8,128)(2,1)} %get-tuple-element.98.right), custom_call_target="tpu_custom_call" | custom-call | tf_op jit(solution)/shard_map/grad_qkv/pallas_call | solution.py:571
  253.3 58.1 %tail.1 = (bf16[384,1024]{1,0:T(8,128)(2,1)}, f32[128,768]{1,0:T(8,128)}, f32[256,128]{1,0:T(8,128)}, f32[16,128]{1,0:T(8,128)}) custom-call(bf16[2,384,1024]{2,1,0:T(8,128)(2,1)} %get-tuple-element.94.near, bf16[2,384,1024]{2,1,0:T(8,128)(2,1)} %get-tuple-element.95.far, bf16[384,1024]{1,0:T(8,128)(2,1)} %x.3, f32[384,1024]{1,0:T(8,128)} %get-tuple-element.96.dmid, ...), custom_call_target="tpu_custom_call" | custom-call | tf_op jit(solution)/shard_map/tail/pallas_call | solution.py:981
  311.4 0.0 copy-start
  311.4 0.0 copy-start.7
  311.4 2.8 finish.1
  314.3 1.9 copy.29
  316.1 0.0 collective-permute-done.3
  316.1 0.0 copy-done
  316.1 0.0 copy-done.7
  316.1 2.8 fusion.2
  318.9 0.0 reduce-scatter.5.cloned.1.call-done
  318.9 1.8 bitcast_convert_fusion
  320.7 1.0 reduce-scatter.3.cloned.1.call-done
  321.7 1.8 convert_element_type.31
  (2 shorter events, 0.0 us)
Async XLA Ops:
  7.2 311.8 %reduce-scatter.5.cloned.1.call-start = ((), (), s32[]{:S(2)}) async-start(), calls=%async_computation.3 | async-start | bytes 2359296 | tf_op jit(solution)/shard_map/reduce_scatter | solution.py:1742
  179.7 1.1 copy-start.3
  179.7 27.3 %copy-start.1 = (bf16[2,384,1024]{2,1,0:T(8,128)(2,1)S(1)}, bf16[2,384,1024]{2,1,0:T(8,128)(2,1)}, u32[]{:S(2)}) copy-start(bf16[2,384,1024]{2,1,0:T(8,128)(2,1)} %get-tuple-element.82) | copy-start | bytes 4718596
  179.8 142.0 %reduce-scatter.3.cloned.1.call-start = ((), (), s32[]{:S(2)}) async-start(), calls=%async_computation.2 | async-start | bytes 2359296 | tf_op jit(solution)/shard_map/reduce_scatter | solution.py:1746
  180.8 19.2 %collective-permute-start = (bf16[384,1024]{1,0:T(8,128)(2,1)S(1)}, bf16[384,1024]{1,0:T(8,128)(2,1)S(1)}, u32[]{:S(2)}, u32[]{:S(2)}) collective-permute-start(bf16[384,1024]{1,0:T(8,128)(2,1)S(1)} %copy-done.3), channel_id=1, source_target_pairs={{0,2},{1,3},{2,0},{3,1},{4,6},{5,7},{6,4},{7,5},{8,10},{9,11},{10,... | collective-permute-start | bytes 2359304 | tf_op jit(solution)/shard_map/ppermute | solution.py:155
  200.0 9.2 %copy-start.4 = (bf16[384,1024]{1,0:T(8,128)(2,1)}, bf16[384,1024]{1,0:T(8,128)(2,1)S(1)}, u32[]{:S(2)}) copy-start(bf16[384,1024]{1,0:T(8,128)(2,1)S(1)} %collective-permute-done.b2) | copy-start | bytes 2359300
  200.0 2.3 collective-permute-start.1
  202.3 3.6 %copy-start.5 = (bf16[384,1024]{1,0:T(8,128)(2,1)}, bf16[384,1024]{1,0:T(8,128)(2,1)S(1)}, u32[]{:S(2)}) copy-start(bf16[384,1024]{1,0:T(8,128)(2,1)S(1)} %collective-permute-done.1.b3) | copy-start | bytes 2359300
  202.3 3.6 %collective-permute-start.2 = (bf16[2,384,1024]{2,1,0:T(8,128)(2,1)}, bf16[2,384,1024]{2,1,0:T(8,128)(2,1)S(1)}, u32[]{:S(2)}, u32[]{:S(2)}) collective-permute-start(bf16[2,384,1024]{2,1,0:T(8,128)(2,1)} %get-tuple-element.85), channel_id=1, source_target_pairs={{0,1},{1,0},{2,3},{3,2},{4,5},{5,4},{6,7},{7,6},{8,9},{9,8},{10,11... | collective-permute-start | bytes 4718600 | tf_op jit(solution)/shard_map/ppermute | solution.py:155
  202.4 5.9 %collective-permute-start.4 = (bf16[384,1024]{1,0:T(8,128)(2,1)S(1)}, bf16[384,1024]{1,0:T(8,128)(2,1)S(1)}, u32[]{:S(2)}, u32[]{:S(2)}) collective-permute-start(bf16[384,1024]{1,0:T(8,128)(2,1)S(1)} %copy-done.3), channel_id=1, source_target_pairs={{0,1},{1,0},{2,3},{3,2},{4,5},{5,4},{6,7},{7,6},{8,9},{9,8},{10,11... | collective-permute-start | bytes 2359304 | tf_op jit(solution)/shard_map/ppermute | solution.py:155
  205.9 1.2 copy-start.2
  208.0 108.1 %collective-permute-start.3 = (bf16[384,1024]{1,0:T(8,128)(2,1)}, bf16[384,1024]{1,0:T(8,128)(2,1)}, u32[]{:S(2)}, u32[]{:S(2)}) collective-permute-start(bf16[384,1024]{1,0:T(8,128)(2,1)} %fusion.3), channel_id=1, source_target_pairs={{0,2},{1,3},{2,0},{3,1},{4,6},{5,7},{6,4},{7,5},{8,10},{9,11},{10,... | collective-permute-start | bytes 2359304 | tf_op jit(solution)/shard_map/ppermute | solution.py:155
  208.3 0.9 copy-start.6
  311.4 4.7 %copy-start = (f32[384,1024]{1,0:T(8,128)S(1)}, f32[384,1024]{1,0:T(8,128)}, u32[]{:S(2)}) copy-start(f32[384,1024]{1,0:T(8,128)} %get-tuple-element.76.mid) | copy-start | bytes 4718596
  311.4 4.7 %copy-start.7 = (f32[1,1024]{1,0:T(1,128)S(1)}, f32[1,1024]{1,0:T(1,128)}, u32[]{:S(2)}) copy-start(f32[1,1024]{1,0:T(1,128)} %get-tuple-element.86) | copy-start | bytes 12292
Sparse Core Ops, SparseCore 0:
  179.9 66.6 reduce-scatter.4
  250.1 71.5 reduce-scatter.2
